TPU v7x, 512 devices: a whole 4x8x8 slice. The times are simulated.
512 devices in a mesh: lat: 64 (over y_lo, z, core), tgt: 8 (over y_hi, x).
Axes of the slice: x: 4, y: 8 (y_hi: 2, y_lo: 4; y = y_hi * 4 + y_lo), z: 8, core: 2. Of those that a mesh axis runs over, the one named last changes fastest.
Arguments:
- inputs: bfloat16 [512, 2, 2304], P('lat', None, 'tgt'), may hold values from -6 to 6
- w_enc: bfloat16 [2304, 32768], P('tgt', 'lat'), may hold values from -0.125 to 0.125
- b_enc: float32 [32768], P('lat'), may hold values from -4 to 4
- masks: int32 [512, 32768], P(None, 'lat'), may hold values 0 or 1
- w_dec: bfloat16 [8, 32768, 2304], P('tgt', 'lat'), may hold values from -0.046875 to 0.046875
- errors: bfloat16 [8, 512, 2304], P('tgt', 'lat'), may hold values from -6 to 6
- target_of: int32 [8], replicated, may hold values from 0 to 7, each once
Outputs:
- grad_enc: float32 [2304, 32768], P('tgt', 'lat')
- grad_bias: float32 [32768], P('lat')
- grad_in: float32 [512, 2, 2304], P('lat', None, 'tgt')
Inputs may be any that keep to these rules, and one draw needn't show every extreme that they name: `target_of`: each target layer names exactly one slot.
All inputs are finite; a program needn't handle non-finite values. No bound on the sum of `masks` on one device may be relied on, other than what follows from the above.
Results may differ from a plain program's by a relative error of at most 0.0029.
Values may be sent and summed in bfloat16 or wider, within the bound.
No kernel may reach another device: no remote copies, remote signals or barrier semaphores. Data moves between devices by JAX's collectives and lax.ppermute only.
A program may use at most 64 MiB of HBM per device.

v0:
```python
import jax
import jax.numpy as jnp
from jax import lax
from jax.sharding import PartitionSpec as P

F = 16384
S = 2


penalty = 1.0
sharpness = 1.0


def latent_grad(dact, sumsq, act, gates):
    norm = jnp.sqrt(sumsq)[None, :]
    tanh_val = jnp.tanh(sharpness * act * norm)
    return (gates * (dact + penalty * sharpness * norm * (1.0 - tanh_val * tanh_val))).astype(
        jnp.bfloat16
    )


def local(inputs, w_enc, b_enc, masks, w_dec, errors, target_of):
    block = w_enc.shape[1]
    source = lax.axis_index("lat") * block // F
    slot = lax.axis_index("tgt")
    slots = jnp.arange(target_of.shape[0], dtype=jnp.int32)
    layer = jnp.sum(jnp.where(slots == slot, target_of, 0))
    flag = (layer >= source).astype(jnp.float32)
    gathered = lax.all_gather(inputs, "lat", axis=0, tiled=True)
    own = lax.dynamic_index_in_dim(gathered, source, 1, keepdims=False)
    partial_pre = jnp.dot(own, w_enc, preferred_element_type=jnp.float32)
    gates = masks.astype(jnp.float32)
    weights = w_dec[0]
    squares = flag * jnp.einsum("cd,cd->c", weights, weights, preferred_element_type=jnp.float32)
    term = flag * lax.dot_general(
        lax.all_gather(errors, "lat", axis=1, tiled=True)[0],
        weights,
        (((1,), (1,)), ((), ())),
        preferred_element_type=jnp.float32,
    )
    pre = lax.psum(partial_pre, "tgt") + b_enc[None, :]
    act = gates * pre
    dact, sumsq = lax.psum((term, squares), "tgt")
    grad = latent_grad(dact, sumsq, act, gates)
    grad_bias = jnp.sum(grad.astype(jnp.float32), axis=0)
    grad_enc = lax.dot_general(
        own, grad, (((0,), (0,)), ((), ())), preferred_element_type=jnp.float32
    )
    picker = (jnp.arange(S, dtype=jnp.int32) == source).astype(jnp.float32)
    part = lax.dot_general(
        grad, w_enc, (((1,), (1,)), ((), ())), preferred_element_type=jnp.float32
    )
    grad_in = lax.psum_scatter(
        part[:, None, :] * picker[None, :, None], "lat", scatter_dimension=0, tiled=True
    )
    return (grad_enc, grad_bias, grad_in)


def solution(mesh):
    return jax.shard_map(
        local,
        mesh=mesh,
        in_specs=(
            P("lat", None, "tgt"),
            P("tgt", "lat"),
            P("lat"),
            P(None, "lat"),
            P("tgt", "lat", None),
            P("tgt", "lat", None),
            P(),
        ),
        out_specs=(P("tgt", "lat"), P("lat"), P("lat", None, "tgt")),
        check_vma=False,
    )
```

profile of v0, /device:TPU:1, one launch (start us, length us, event | category | flops | bytes accessed | tf_op | source)
XLA Modules:
  0.0 830.5 jit_solution(9047285802787477920)
XLA Ops:
  7.2 0.0 copy-start
  7.2 0.0 all-gather.2.cloned.1.call-start
  7.2 0.7 all-gather.2.cloned.1.call-update
  7.9 0.0 all-reduce.7.cloned.1.call-start
  8.0 1.3 fusion.13
  9.9 89.9 %all_gather.6 = bf16[512,2,288]{2,1,0:T(2,128)(2,1)S(1)} all-gather(bf16[8,2,288]{2,1,0:T(2,128)(2,1)} %param.7), channel_id=1, replica_groups=mesh['lat'=64,'tgt'=8] {'lat'}, dimensions={0}, use_global_device_ids=true | all-gather | bytes 599040 | tf_op jit(solution)/shard_map/all_gather | solution.py:29
  99.9 0.8 constant_dynamic-slice_fusion.1
  100.7 1.1 copy.20
  101.8 0.0 copy-done
  101.8 1.5 fusion.11
  103.2 30.7 %all-gather.2.cloned.1.call-done = bf16[1,512,2304]{2,1,0:T(8,128)(2,1)} async-done(((bf16[1,8,2304]{2,1,0:T(8,128)(2,1)}), bf16[1,512,2304]{2,1,0:T(8,128)(2,1)}) %all-gather.2.cloned.1.call-update) | async-done | bytes 2359312 | tf_op jit(solution)/shard_map/all_gather | solution.py:36
  133.9 0.0 copy-start.1
  133.9 4.9 fusion.4
  138.9 0.0 copy-start.2
  138.9 0.0 all-reduce.7.cloned.1.call-update
  138.9 0.0 all-reduce.5.cloned.1.call-start
  138.9 0.0 copy-done.1
  138.9 0.5 fusion
  139.5 28.6 %psum.22 = f32[512]{0:T(512)S(1)} all-reduce(f32[512]{0:T(512)S(1)} %broadcast_multiply_fusion.1), channel_id=1, replica_groups=mesh['lat'=64,'tgt'=8] {'tgt'}, use_global_device_ids=true, to_apply=%region_2.3 | all-reduce | flops 512 | bytes 4096 | tf_op jit(solution)/shard_map/psum | solution.py:43
  168.1 106.2 %all-reduce.7.cloned.1.call-done = (f32[512,512]{1,0:T(8,128)}, f32[512,512]{1,0:T(8,128)}) async-done(((f32[512,512]{1,0:T(8,128)}, f32[512,512]{1,0:T(8,128)}), (f32[512,512]{1,0:T(8,128)}, f32[512,512]{1,0:T(8,128)})) %all-reduce.7.cloned.1.call-update) | async-done | bytes 2097168 | tf_op jit(solution)/shard_map/psum | solution.py:43
  274.3 0.0 copy-done.2
  274.3 2.9 convert_reduce_fusion
  277.1 0.4 fusion.14
  277.6 1.8 broadcast_multiply_fusion
  279.3 0.0 all-reduce.5.cloned.1.call-update
  279.4 1.3 dynamic-slice
  281.3 1.1 fusion.9
  282.4 540.2 %all-reduce.5.cloned.1.call-done = f32[512,2,288]{2,1,0:T(2,128)} async-done(((f32[512,2,288]{2,1,0:T(2,128)}), f32[512,2,288]{2,1,0:T(2,128)}) %all-reduce.5.cloned.1.call-update) | async-done | bytes 1179664
  822.6 1.4 constant_dynamic-slice_fusion
  (3 shorter events, 0.0 us)
Async XLA Ops:
  7.2 94.6 %copy-start = (bf16[288,512]{1,0:T(8,128)(2,1)S(1)}, bf16[288,512]{1,0:T(8,128)(2,1)}, u32[]{:S(2)}) copy-start(bf16[288,512]{1,0:T(8,128)(2,1)} %param.8) | copy-start | bytes 884740
  7.2 126.8 %all-gather.2.cloned.1.call-start = ((), (), s32[]{:S(2)}) async-start(), calls=%async_computation | async-start | bytes 2396160 | tf_op jit(solution)/shard_map/all_gather | solution.py:36
  7.9 266.3 %all-reduce.7.cloned.1.call-start = ((), (), s32[]{:S(2)}) async-start(), calls=%async_computation.2 | async-start | bytes 4194304 | tf_op jit(solution)/shard_map/psum | solution.py:43
  133.9 5.0 copy-start.1
  138.9 135.4 %copy-start.2 = (f32[512]{0:T(512)S(1)}, f32[512]{0:T(512)}, u32[]{:S(2)}) copy-start(f32[512]{0:T(512)} %param.9) | copy-start | bytes 6148
  138.9 683.7 %all-reduce.5.cloned.1.call-start = ((), (), s32[]{:S(2)}) async-start(), calls=%async_computation.1 | async-start | bytes 3145728
Sparse Core Ops, SparseCore 0:
  10.2 123.7 all-gather.1
  139.0 135.2 all-reduce.6
  279.5 543.0 all-reduce.4
where the time goes:
time: 831 us; the launch traced here: 830 us
  waiting for transfers between devices  678 us (82%)
  blocking collectives  119 us (14%)
  between operations  15.1 us (2%)
    unnamed x4, waiting for transfers between devices  541 us
    psum x1, waiting for transfers between devices, local(): dact, sumsq = lax.psum((term, squares), 'tgt')  106 us
    all_gather x1, blocking collectives, local(): gathered = lax.all_gather(inputs, 'lat', axis=0, tiled=True)  89.9 us
    all_gather x1, waiting for transfers between devices, local(): lax.all_gather(errors, 'lat', axis=1, tiled=True)[0]  30.7 us
    psum x1, blocking collectives, local(): dact, sumsq = lax.psum((term, squares), 'tgt')  28.6 us
  transfers between devices with their start and end apart: 3, of which 3 were waited for; matrix products, arithmetic and copies ran while one was open for 1% of the time, Pallas kernels for 0%

commit v1 on v0

v1 whole, which is shorter than its diff:
```python
import jax
import jax.numpy as jnp
from jax import lax
from jax.sharding import Mesh, PartitionSpec as P

S = 2
penalty = 1.0
sharpness = 1.0

YL, Z, C, YH, X = 4, 8, 2, 2, 4
AXES = ("yl", "z", "c", "yh", "x")
LAT = ("yl", "z", "c")
TGT = ("yh", "x")
PLANE = ("yl", "z")
PRE_BOUND = 1024.0
SWAP = [(0, 1), (1, 0)]
TOP = 14.0


def exponent(bound):
    return jnp.ceil(jnp.log2(jnp.maximum(bound, 1e-30)))


def split_bf16(v):
    hi = v.astype(jnp.bfloat16)
    rest = v - hi.astype(jnp.float32)
    mid = rest.astype(jnp.bfloat16)
    low = (rest - mid.astype(jnp.float32)).astype(jnp.bfloat16)
    return jnp.stack([hi, mid, low])


def local(inputs, w_enc, b_enc, masks, w_dec, errors, target_of):
    f32, bf16, f16 = jnp.float32, jnp.bfloat16, jnp.float16
    yl, core = lax.axis_index("yl"), lax.axis_index("c")
    x = lax.axis_index("x")
    slot = lax.axis_index("yh") * X + x
    source = yl * S // YL
    feats, lats = w_enc.shape
    depth = w_dec.shape[2]
    rows = inputs.shape[0]
    slots = jnp.arange(target_of.shape[0], dtype=jnp.int32)
    layer = jnp.sum(jnp.where(slots == slot, target_of, 0))
    flag = (layer >= source).astype(f32)

    gates5 = masks.reshape(YL, Z, C, rows, lats)
    gates4 = lax.dynamic_index_in_dim(gates5, x, 0, keepdims=False)
    gates_own = lax.dynamic_index_in_dim(gates4, core, 1, keepdims=False).reshape(Z * rows, lats)
    gates_send = lax.dynamic_index_in_dim(gates4, 1 - core, 1, keepdims=False).reshape(Z * rows, lats)
    w_own = w_dec[0]
    w_other = lax.ppermute(w_own, "c", SWAP)
    pack = jnp.concatenate(
        [w_enc, gates_send.astype(bf16), split_bf16(b_enc), jnp.zeros((13, lats), bf16)], axis=0
    )
    pack_other = lax.ppermute(pack, "c", SWAP)

    top_err = jnp.max(jnp.abs(errors[0].astype(f32))) * 1.01
    parts = []
    for dest in range(YL):
        parts.append(
            jnp.concatenate(
                [
                    errors[0],
                    inputs[:, dest * S // YL, :],
                    jnp.broadcast_to(top_err.astype(bf16), (rows, 96)),
                ],
                axis=1,
            )
        )
    send = jnp.stack(parts)[:, None]
    width = send.shape[-1]
    send = jnp.broadcast_to(send, (YL, Z, rows, width)).reshape(YL * Z, rows, width)
    got = lax.all_to_all(send, PLANE, 0, 0, tiled=True).reshape(YL * Z * rows, width)
    errs, own = got[:, :depth], got[:, depth : depth + feats]
    top_err = jnp.max(got[:, depth + feats : depth + feats + 1].astype(f32))
    wide = got.shape[0]
    chunk = wide // X

    sq_own = jnp.einsum("cd,cd->c", w_own, w_own, preferred_element_type=f32)
    sq_other = jnp.einsum("cd,cd->c", w_other, w_other, preferred_element_type=f32)
    w_enc_other = pack_other[:feats]
    gates_other = pack_other[feats : feats + chunk].astype(f32)
    bias_rows = pack_other[feats + chunk : feats + chunk + 3].astype(f32)
    b_other = bias_rows[0] + bias_rows[1] + bias_rows[2]
    squares = flag * jnp.concatenate([sq_own, sq_other])
    dims = (((1,), (1,)), ((), ()))
    term = jnp.concatenate(
        [
            lax.dot_general(errs, w_own, dims, preferred_element_type=f32),
            lax.dot_general(errs, w_other, dims, preferred_element_type=f32),
        ],
        axis=1,
    )
    partial_pre = jnp.concatenate(
        [
            jnp.dot(own, w_enc, preferred_element_type=f32),
            jnp.dot(own, w_enc_other, preferred_element_type=f32),
        ],
        axis=1,
    )

    top_sq = jnp.max(squares)
    e_term = exponent(jnp.sqrt(depth * 1.01 * top_sq) * top_err)
    e_sq = exponent(top_sq)
    pre_scale = 32768.0 / PRE_BOUND

    def extra_rows(sq, e_sq, e_term):
        scaled = sq * jnp.exp2(TOP - e_sq)
        hi = scaled.astype(f16)
        low = (scaled - hi.astype(f32)).astype(f16)
        line = lambda e: jnp.broadcast_to(e.astype(f16), hi.shape)
        return jnp.concatenate(
            [jnp.stack([hi, low, line(e_sq), line(e_term)]), jnp.zeros((12,) + hi.shape, f16)], axis=0
        )

    extra = extra_rows(squares, e_sq, e_term)
    out = jnp.concatenate(
        [
            (term * (flag * jnp.exp2(TOP - e_term))).astype(f16).reshape(X, chunk, C * lats),
            (partial_pre * pre_scale).astype(f16).reshape(X, chunk, C * lats),
            jnp.broadcast_to(extra[None], (X,) + extra.shape),
        ],
        axis=1,
    )
    back = lax.all_to_all(out, "x", 0, 0, tiled=True)

    def decode(block):
        e_sq = block[2 * chunk + 2, 0].astype(f32)
        e_term = block[2 * chunk + 3, 0].astype(f32)
        dact = block[:chunk].astype(f32) * jnp.exp2(e_term - TOP)
        pre = block[chunk : 2 * chunk].astype(f32) * (1.0 / pre_scale)
        sq = (block[2 * chunk].astype(f32) + block[2 * chunk + 1].astype(f32)) * jnp.exp2(e_sq - TOP)
        return dact, pre, sq, e_sq, e_term

    dact, pre, sq, es, et = decode(back[0])
    for i in range(1, X):
        d1, p1, s1, es1, et1 = decode(back[i])
        dact, pre, sq = dact + d1, pre + p1, sq + s1
        es, et = jnp.maximum(es, es1), jnp.maximum(et, et1)
    es, et = es + 2.0, et + 2.0
    half = jnp.concatenate(
        [
            (dact * jnp.exp2(TOP - et)).astype(f16),
            (pre * pre_scale).astype(f16),
            extra_rows(sq, es, et),
        ],
        axis=0,
    )
    d1, p1, s1, _, _ = decode(lax.ppermute(half, "yh", SWAP))
    dact, pre, sumsq = dact + d1, pre + p1, sq + s1

    gates = jnp.concatenate([gates_own.astype(f32), gates_other], axis=1)
    pre = pre + jnp.concatenate([b_enc, b_other])[None, :]
    norm = jnp.sqrt(sumsq)[None, :]
    tanh_val = jnp.tanh(sharpness * (gates * pre) * norm)
    grad = (gates * (dact + penalty * sharpness * norm * (1.0 - tanh_val * tanh_val))).astype(bf16)

    grad = lax.all_to_all(
        jnp.broadcast_to(grad[None], (X,) + grad.shape), "x", 0, 0, tiled=True
    ).reshape(wide, C * lats)
    g_own, g_other = grad[:, :lats], grad[:, lats:]
    rows_dims = (((0,), (0,)), ((), ()))

    def enc(g):
        return lax.dot_general(own, g, rows_dims, preferred_element_type=f32)

    def bias(g):
        return jnp.broadcast_to(jnp.sum(g.astype(f32), axis=0)[None], (8, lats))

    away = lax.ppermute(jnp.concatenate([enc(g_other), bias(g_other)], axis=0), "c", SWAP)

    part = lax.dot_general(g_own, w_enc, dims, preferred_element_type=f32) + lax.dot_general(
        g_other, w_enc_other, dims, preferred_element_type=f32
    )
    e_part = exponent(jnp.max(jnp.abs(part)))
    sent = jnp.concatenate(
        [
            (part * jnp.exp2(TOP - e_part)).astype(f16),
            jnp.broadcast_to(e_part.astype(f16), (wide, 96)),
        ],
        axis=1,
    ).reshape(YL * Z, rows, feats + 96)
    came = lax.all_to_all(sent, PLANE, 0, 0, tiled=True)
    values = came[:, :, :feats].astype(f32) * jnp.exp2(
        came[:, :, feats : feats + 1].astype(f32) - TOP
    )
    sums = jnp.sum(values.reshape(S, YL * Z // S, rows, feats), axis=1)
    grad_in = jnp.transpose(sums, (1, 0, 2))
    grad_enc = enc(g_own) + away[:feats]
    grad_bias = jnp.sum(g_own.astype(f32), axis=0) + away[feats]
    return (grad_enc, grad_bias, grad_in)


def solution(mesh):
    fine = Mesh(mesh.devices.reshape(YL, Z, C, YH, X), AXES)
    return jax.shard_map(
        local,
        mesh=fine,
        in_specs=(
            P(LAT, None, TGT),
            P(TGT, LAT),
            P(LAT),
            P(None, LAT),
            P(TGT, LAT, None),
            P(TGT, LAT, None),
            P(),
        ),
        out_specs=(P(TGT, LAT), P(LAT), P(LAT, None, TGT)),
        check_vma=False,
    )
```

time: 831 us -> 164 us (0.20)
  waiting for transfers between devices: 678 us -> 49.7 us
  blocking collectives: 119 us -> 26.4 us
  starting transfers between devices: 0.12 us -> 33.6 us
  local copies, waits for them, and re-layouts: 4.52 us -> 16.3 us
    unnamed x4 -> x0, waiting for transfers between devices: 541 us -> none
    psum x1 -> x0, waiting for transfers between devices: 106 us -> none  [local(): dact, sumsq = lax.psum((term, squares), 'tgt')]
    all_gather x1 -> x0, blocking collectives: 89.9 us -> none  [local(): gathered = lax.all_gather(inputs, 'lat', axis=0, tiled=True)]
    all_to_all x0 -> x2, waiting for transfers between devices: none -> 36 us  [the longest x1 21.9 us: local(): lax.all_to_all(send, PLANE, 0, 0, tiled=True).reshape(YL * Z * rows, width)]
    all_gather x1 -> x0, waiting for transfers between devices: 30.7 us -> none  [local(): lax.all_gather(errors, 'lat', axis=1, tiled=True)[0]]
    psum x1 -> x0, blocking collectives: 28.6 us -> none  [local(): dact, sumsq = lax.psum((term, squares), 'tgt')]
    all_to_all x0 -> x2, blocking collectives: none -> 26.4 us  [the longest x1 17 us: local(): came = lax.all_to_all(sent, PLANE, 0, 0, tiled=True)]
    ppermute x0 -> x4, starting transfers between devices: none -> 21.4 us  [the longest x1 8.79 us: local(): w_other = lax.ppermute(w_own, 'c', SWAP)]
  transfers between devices with their start and end apart: 3 -> 6, of which waited for: 3 -> 3; matrix products, arithmetic and copies ran while one was open for 1% -> 13% of each run, Pallas kernels for 0% -> 0%
where the time goes in v1:
time: 164 us; the launch traced here: 163 us
  waiting for transfers between devices  49.7 us (30%)
  starting transfers between devices  33.6 us (20%)
  blocking collectives  26.4 us (16%)
  local copies, waits for them, and re-layouts  16.3 us (10%)
  other arithmetic  13.4 us (8%)
  between operations  12.4 us (8%)
  matrix products  11 us (7%)
    all_to_all x1, waiting for transfers between devices, local(): lax.all_to_all(send, PLANE, 0, 0, tiled=True).reshape(YL * Z * rows, width)  21.9 us
    all_to_all x1, blocking collectives, local(): came = lax.all_to_all(sent, PLANE, 0, 0, tiled=True)  17 us
    all_to_all x1, waiting for transfers between devices, local(): back = lax.all_to_all(out, 'x', 0, 0, tiled=True)  14.1 us
    ppermute x1, waiting for transfers between devices, local(): d1, p1, s1, _, _ = decode(lax.ppermute(half, 'yh', SWAP))  13.6 us
    all_to_all x1, blocking collectives, local(): lax.all_to_all(jnp.broadcast_to(grad[None], (X,) + grad.shape), 'x', 0, 0...  9.36 us
    ppermute x1, starting transfers between devices, local(): w_other = lax.ppermute(w_own, 'c', SWAP)  8.79 us
    all_to_all x1, starting transfers between devices, local(): lax.all_to_all(send, PLANE, 0, 0, tiled=True).reshape(YL * Z * rows, width)  8.22 us
    ppermute x1, starting transfers between devices, local(): lax.ppermute(jnp.concatenate([enc(g_other), bias(g_other)], axis=0), 'c',...  5.37 us
  transfers between devices with their start and end apart: 6, of which 3 were waited for; matrix products, arithmetic and copies ran while one was open for 13% of the time, Pallas kernels for 0%

profile of v1, /device:TPU:1, one launch (start us, length us, event | category | flops | bytes accessed | tf_op | source)
XLA Modules:
  0.0 162.7 jit_solution(6987214252801223720)
XLA Ops:
  0.6 8.8 %collective-permute-start.1 = (bf16[512,2304]{1,0:T(8,128)(2,1)}, bf16[512,2304]{1,0:T(8,128)(2,1)}, u32[]{:S(2)}, u32[]{:S(2)}) collective-permute-start(bf16[512,2304]{1,0:T(8,128)(2,1)} %bitcast.126), channel_id=1, source_target_pairs={{0,8},{8,0},{1,9},{9,1},{2,10},{10,2},{3,11},{11,3},{4,12},{12,4},... | collective-permute-start | bytes 7077896 | tf_op jit(solution)/shard_map/ppermute | solution.py:50
  9.4 0.8 fusion.66
  10.2 1.4 abs_reduce_fusion.1
  12.3 0.9 concatenate.66
  13.1 0.9 concatenate.67
  14.0 1.2 broadcast_in_dim.17
  15.2 8.2 %all-to-all-start = ((bf16[32,8,2688]{2,1,0:T(8,128)(2,1)}), bf16[32,8,2688]{2,1,0:T(8,128)(2,1)S(1)}, u32[]{:S(2)}, u32[]{:S(2)}) async-start(bf16[32,8,2688]{2,1,0:T(8,128)(2,1)} %bitcast.5), calls=%async_computation | async-start | bytes 2752512 | tf_op jit(solution)/shard_map/all_to_all | solution.py:72
  23.5 1.0 fusion.30
  24.6 3.9 %concatenate.68 = bf16[368,512]{1,0:T(8,128)(2,1)} concatenate(bf16[288,512]{1,0:T(8,128)(2,1)S(1)} %copy-done, bf16[64,512]{1,0:T(8,128)(2,1)S(1)} %get-tuple-element.29, bf16[1,512]{1,0:T(2,128)(2,1)S(1)} %stack.27, bf16[1,512]{1,0:T(2,128)(2,1)S(1)} %stack.28, bf16[1,512]{1,0:T(2,128)(2,1)S(1)} %stack.29, bf16[13,512]{1,0:T(8,128)(2,1)S(1)} %broadcast_in_dim.18), dimensions={0} | concatenate | bytes 753664 | tf_op jit(solution)/shard_map/concatenate | solution.py:51
  28.5 2.2 %collective-permute-start = (bf16[368,512]{1,0:T(8,128)(2,1)}, bf16[368,512]{1,0:T(8,128)(2,1)}, u32[]{:S(2)}, u32[]{:S(2)}) collective-permute-start(bf16[368,512]{1,0:T(8,128)(2,1)} %concatenate.68), channel_id=1, source_target_pairs={{0,8},{8,0},{1,9},{9,1},{2,10},{10,2},{3,11},{11,3},{4,12},{12,4},... | collective-permute-start | bytes 1130504 | tf_op jit(solution)/shard_map/ppermute | solution.py:54
  30.7 0.6 fusion.56
  32.0 2.2 %fusion.1 = f32[512]{0:T(512)S(1)} fusion(bf16[1,512,2304]{2,1,0:T(8,128)(2,1)} %param.11), kind=kLoop, calls=%fused_computation.3 | loop fusion | flops 3538432 | bytes 2361344 | tf_op jit(solution)/shard_map/cd,cd->c/dot_general | solution.py:78
  34.2 2.2 %fusion = f32[512]{0:T(512)S(1)} fusion(bf16[512,2304]{1,0:T(8,128)(2,1)} %collective-permute-done.1), kind=kLoop, calls=%fused_computation.1 | loop fusion | flops 3538432 | bytes 2361344 | tf_op jit(solution)/shard_map/cd,cd->c/dot_general | solution.py:79
  36.4 0.6 fusion.51
  38.5 21.9 %all-to-all-done = bf16[32,8,2688]{2,1,0:T(8,128)(2,1)S(1)} async-done(((bf16[32,8,2688]{2,1,0:T(8,128)(2,1)}), bf16[32,8,2688]{2,1,0:T(8,128)(2,1)S(1)}, u32[]{:S(2)}, u32[]{:S(2)}) %all-to-all-start) | async-done | bytes 1376288 | tf_op jit(solution)/shard_map/all_to_all | solution.py:72
  60.3 0.3 fusion.34
  60.6 0.7 slice_reduce_fusion
  62.2 2.5 %fusion.2 = f32[4,64,512]{2,1,0:T(8,128)S(1)} fusion(bf16[4,64,2304]{2,1,0:T(8,128)(2,1)S(1)} %bitcast.129, bf16[1,512,2304]{2,1,0:T(8,128)(2,1)} %param.11), kind=kOutput, calls=%fused_computation.4 | convolution fusion | flops 603979776 | bytes 4063232 | tf_op jit(solution)/shard_map/dot_general | solution.py:88
  64.7 1.2 fusion.19
  66.0 2.5 %fusion.57 = f32[256,512]{1,0:T(8,128)S(1)} fusion(bf16[512,2304]{1,0:T(8,128)(2,1)} %collective-permute-done.1, bf16[256,2688]{1,0:T(8,128)(2,1)S(1)} %bitcast.118), kind=kOutput, calls=%fused_computation.112 | convolution fusion | flops 603979776 | bytes 4063232 | tf_op jit(solution)/shard_map/dot_general | solution.py:89
  68.6 0.2 concatenate.79
  68.9 1.4 pad_maximum_fusion
  70.2 4.0 %all-to-all-start.1 = ((f16[4,144,1024]{2,1,0:T(8,128)(2,1)}), f16[4,144,1024]{2,1,0:T(8,128)(2,1)S(1)}, u32[]{:S(2)}, u32[]{:S(2)}) async-start(f16[4,144,1024]{2,1,0:T(8,128)(2,1)} %pad_maximum_fusion), calls=%async_computation.1 | async-start | bytes 2359296 | tf_op jit(solution)/shard_map/all_to_all | solution.py:124
  74.3 0.7 slice_convert_fusion.1
  75.0 14.1 %all-to-all-done.1 = f16[4,144,1024]{2,1,0:T(8,128)(2,1)S(1)} async-done(((f16[4,144,1024]{2,1,0:T(8,128)(2,1)}), f16[4,144,1024]{2,1,0:T(8,128)(2,1)S(1)}, u32[]{:S(2)}, u32[]{:S(2)}) %all-to-all-start.1) | async-done | bytes 1179680 | tf_op jit(solution)/shard_map/all_to_all | solution.py:124
  89.1 0.3 slice_bitcast_fusion
  89.4 0.5 fusion.65
  90.6 0.5 fusion.64
  93.1 0.5 fusion.63
  94.3 0.5 fusion.62
  97.6 3.4 %concatenate.81 = f16[144,1024]{1,0:T(8,128)(2,1)} concatenate(f16[64,1024]{1,0:T(8,128)(2,1)S(1)} %fusion.17, f16[64,1024]{1,0:T(8,128)(2,1)S(1)} %bitcast_convert_fusion, f16[1,1024]{1,0:T(2,128)(2,1)S(1)} %fusion.54, f16[1,1024]{1,0:T(2,128)(2,1)S(1)} %get-tuple-element.20, f16[1,1024]{1,0:T(2,128)(2,1)S(1)} %stack_broadcast_in_dim.14, ...), dimensions={0} | concatenate | bytes 589824 | tf_op jit(solution)/shard_map/concatenate | solution.py:140
  101.0 5.0 %collective-permute-start.2 = (f16[144,1024]{1,0:T(8,128)(2,1)}, f16[144,1024]{1,0:T(8,128)(2,1)S(1)}, u32[]{:S(2)}, u32[]{:S(2)}) collective-permute-start(f16[144,1024]{1,0:T(8,128)(2,1)} %concatenate.81), channel_id=1, source_target_pairs={{0,4},{4,0},{1,5},{5,1},{2,6},{6,2},{3,7},{7,3},{8,12},{12,8},{9,1... | collective-permute-start | bytes 884744 | tf_op jit(solution)/shard_map/ppermute | solution.py:148
  106.0 0.9 slice_convert_fusion
  106.8 13.6 %collective-permute-done.2 = f16[144,1024]{1,0:T(8,128)(2,1)S(1)} collective-permute-done((f16[144,1024]{1,0:T(8,128)(2,1)}, f16[144,1024]{1,0:T(8,128)(2,1)S(1)}, u32[]{:S(2)}, u32[]{:S(2)}) %collective-permute-start.2) | collective-permute-done | bytes 294944 | tf_op jit(solution)/shard_map/ppermute | solution.py:148
  120.5 0.5 fusion.61
  122.4 0.3 fusion.16
  122.8 9.4 %all_to_all.20 = bf16[4,64,1024]{2,1,0:T(8,128)(2,1)S(1)} all-to-all(bf16[4,64,1024]{2,1,0:T(8,128)(2,1)S(1)} %broadcast_in_dim.21), channel_id=1, replica_groups=mesh['yl'=4,'z'=8,'c'=2,'yh'=2,'x'=4] {'x'}, dimensions={0} | all-to-all | bytes 1048576 | tf_op jit(solution)/shard_map/all_to_all | solution.py:157
  132.2 0.3 fusion.24
  132.4 1.8 %abs_reduce_fusion = (f32[]{:T(128)}, f32[256,288]{0,1:T(8,128)S(1)}) fusion(f32[256,288]{0,1:T(8,128)S(1)} %fusion.24, bf16[368,512]{1,0:T(8,128)(2,1)} %collective-permute-done, bf16[256,1024]{1,0:T(8,128)(2,1)S(1)} %bitcast.122), kind=kOutput, calls=%fused_computation.23 | convolution fusion | flops 75718656 | bytes 1146884 | tf_op jit(solution)/shard_map/dot_general | solution.py:171
  135.0 0.3 fusion.22
  135.4 0.2 copy.79
  135.7 5.4 %collective-permute-start.3 = (f32[296,512]{1,0:T(8,128)S(1)}, f32[296,512]{1,0:T(8,128)}, u32[]{:S(2)}, u32[]{:S(2)}) collective-permute-start(f32[296,512]{1,0:T(8,128)S(1)} %pad_maximum_fusion.1), channel_id=1, source_target_pairs={{0,8},{8,0},{1,9},{9,1},{2,10},{10,2},{3,11},{11,3},{4,12},{12,4},... | collective-permute-start | bytes 1818632 | tf_op jit(solution)/shard_map/ppermute | solution.py:169
  141.2 17.0 %all_to_all.21 = f16[32,8,384]{2,1,0:T(8,128)(2,1)S(1)} all-to-all(f16[32,8,384]{2,1,0:T(8,128)(2,1)S(1)} %pad_bitcast_fusion), channel_id=1, replica_groups=mesh['yl'=4,'z'=8,'c'=2,'yh'=2,'x'=4] {'yl','z'}, dimensions={0} | all-to-all | bytes 393216 | tf_op jit(solution)/shard_map/all_to_all | solution.py:182
  158.3 0.1 copy.78
  158.7 0.6 copy.65
  159.3 0.7 slice.284
  160.0 0.6 add.296
  160.6 2.1 %slice_add_fusion = f32[288,512]{1,0:T(8,128)} fusion(f32[296,512]{1,0:T(8,128)} %collective-permute-done.3, bf16[256,1024]{1,0:T(8,128)(2,1)S(1)} %bitcast.125, bf16[256,2688]{1,0:T(8,128)(2,1)S(1)} %bitcast.120), kind=kOutput, calls=%fused_computation.13 | convolution fusion | flops 75644928 | bytes 1638400 | tf_op jit(solution)/shard_map/dot_general | solution.py:164
  (45 shorter events, 1.3 us)
Async XLA Ops:
  0.6 33.6 %collective-permute-start.1 = (bf16[512,2304]{1,0:T(8,128)(2,1)}, bf16[512,2304]{1,0:T(8,128)(2,1)}, u32[]{:S(2)}, u32[]{:S(2)}) collective-permute-start(bf16[512,2304]{1,0:T(8,128)(2,1)} %bitcast.126), channel_id=1, source_target_pairs={{0,8},{8,0},{1,9},{9,1},{2,10},{10,2},{3,11},{11,3},{4,12},{12,4},... | collective-permute-start | bytes 7077896 | tf_op jit(solution)/shard_map/ppermute | solution.py:50
  15.2 8.3 %copy-start.1 = (f32[512]{0:T(512)S(1)}, f32[512]{0:T(512)}, u32[]{:S(2)}) copy-start(f32[512]{0:T(512)} %param.9) | copy-start | bytes 6148
  15.2 9.3 %copy-start = (bf16[288,512]{1,0:T(8,128)(2,1)S(1)}, bf16[288,512]{1,0:T(8,128)(2,1)}, u32[]{:S(2)}) copy-start(bf16[288,512]{1,0:T(8,128)(2,1)} %param.8) | copy-start | bytes 884740
  15.2 15.5 %copy-start.2 = (s32[8]{0:T(128)S(1)}, s32[8]{0:T(128)}, u32[]{:S(2)}) copy-start(s32[8]{0:T(128)} %param.13) | copy-start | bytes 100
  15.2 45.1 %all-to-all-start = ((bf16[32,8,2688]{2,1,0:T(8,128)(2,1)}), bf16[32,8,2688]{2,1,0:T(8,128)(2,1)S(1)}, u32[]{:S(2)}, u32[]{:S(2)}) async-start(bf16[32,8,2688]{2,1,0:T(8,128)(2,1)} %bitcast.5), calls=%async_computation | async-start | bytes 2752512 | tf_op jit(solution)/shard_map/all_to_all | solution.py:72
  28.5 36.2 %collective-permute-start = (bf16[368,512]{1,0:T(8,128)(2,1)}, bf16[368,512]{1,0:T(8,128)(2,1)}, u32[]{:S(2)}, u32[]{:S(2)}) collective-permute-start(bf16[368,512]{1,0:T(8,128)(2,1)} %concatenate.68), channel_id=1, source_target_pairs={{0,8},{8,0},{1,9},{9,1},{2,10},{10,2},{3,11},{11,3},{4,12},{12,4},... | collective-permute-start | bytes 1130504 | tf_op jit(solution)/shard_map/ppermute | solution.py:54
  70.2 18.9 %all-to-all-start.1 = ((f16[4,144,1024]{2,1,0:T(8,128)(2,1)}), f16[4,144,1024]{2,1,0:T(8,128)(2,1)S(1)}, u32[]{:S(2)}, u32[]{:S(2)}) async-start(f16[4,144,1024]{2,1,0:T(8,128)(2,1)} %pad_maximum_fusion), calls=%async_computation.1 | async-start | bytes 2359296 | tf_op jit(solution)/shard_map/all_to_all | solution.py:124
  101.0 19.5 %collective-permute-start.2 = (f16[144,1024]{1,0:T(8,128)(2,1)}, f16[144,1024]{1,0:T(8,128)(2,1)S(1)}, u32[]{:S(2)}, u32[]{:S(2)}) collective-permute-start(f16[144,1024]{1,0:T(8,128)(2,1)} %concatenate.81), channel_id=1, source_target_pairs={{0,4},{4,0},{1,5},{5,1},{2,6},{6,2},{3,7},{7,3},{8,12},{12,8},{9,1... | collective-permute-start | bytes 884744 | tf_op jit(solution)/shard_map/ppermute | solution.py:148
  135.7 23.6 %collective-permute-start.3 = (f32[296,512]{1,0:T(8,128)S(1)}, f32[296,512]{1,0:T(8,128)}, u32[]{:S(2)}, u32[]{:S(2)}) collective-permute-start(f32[296,512]{1,0:T(8,128)S(1)} %pad_maximum_fusion.1), channel_id=1, source_target_pairs={{0,8},{8,0},{1,9},{9,1},{2,10},{10,2},{3,11},{11,3},{4,12},{12,4},... | collective-permute-start | bytes 1818632 | tf_op jit(solution)/shard_map/ppermute | solution.py:169

commit v2 on v0

v2 whole, which is shorter than its diff:
```python
import jax
import jax.numpy as jnp
from jax import lax
from jax.sharding import Mesh, PartitionSpec as P

S = 2
penalty = 1.0
sharpness = 1.0

YL, Z, C, YH, X = 4, 8, 2, 2, 4
AXES = ("yl", "z", "c", "yh", "x")
LAT = ("yl", "z", "c")
TGT = ("yh", "x")
PLANE = ("yl", "z")
SUMS = ("x", "yh")
PEERS = YL * Z
SLOTS = YH * X
LANES = 384
EXTRA = 8
PRE_SCALE = 64.0
TOP = 14.0


def exponent(bound):
    return jnp.ceil(jnp.log2(jnp.maximum(bound, 1e-30)))


def split_bf16(v):
    hi = v.astype(jnp.bfloat16)
    rest = v - hi.astype(jnp.float32)
    mid = rest.astype(jnp.bfloat16)
    low = (rest - mid.astype(jnp.float32)).astype(jnp.bfloat16)
    return jnp.stack([hi, mid, low])


def swap(value, axis, size, distance):
    return lax.ppermute(value, axis, [(i, i ^ distance) for i in range(size)])


def local(inputs, w_enc, b_enc, masks, w_dec, errors, target_of):
    f32, bf16, f16 = jnp.float32, jnp.bfloat16, jnp.float16
    yl, z, core = (lax.axis_index(a) for a in LAT)
    yh, x = lax.axis_index("yh"), lax.axis_index("x")
    place = x * YH + yh
    source = yl * S // YL
    feats, lats = w_enc.shape
    depth = w_dec.shape[2]
    rows = inputs.shape[0]
    wide = PEERS * rows
    chunk = wide // SLOTS
    both_lats = C * lats
    pad = LANES - feats
    dims = (((1,), (1,)), ((), ()))
    rows_dims = (((0,), (0,)), ((), ()))

    errs = lax.all_to_all(
        jnp.broadcast_to(errors, (PEERS, rows, depth)), PLANE, 0, 0, tiled=True
    ).reshape(wide, depth)

    top_err = jnp.max(jnp.abs(errors[0].astype(f32))) * 1.01
    top_lanes = jnp.broadcast_to(top_err.astype(bf16), (rows, S, pad))
    held = jnp.transpose(jnp.concatenate([inputs, top_lanes], axis=2), (1, 0, 2))
    mine = lax.dynamic_index_in_dim(held, source, 0, keepdims=True)
    theirs = swap(lax.dynamic_index_in_dim(held, 1 - source, 0, keepdims=True), "yl", YL, 2)
    low = source == 0
    held = jnp.concatenate([jnp.where(low, mine, theirs), jnp.where(low, theirs, mine)], axis=0)
    for axis, size, at, distance in (("z", Z, z, 1), ("z", Z, z, 2), ("z", Z, z, 4), ("yl", YL, yl, 1)):
        theirs = swap(held, axis, size, distance)
        low = (at & distance) == 0
        held = jnp.concatenate([jnp.where(low, held, theirs), jnp.where(low, theirs, held)], axis=1)
    own = held.reshape(wide, LANES)
    top_err = jnp.max(own[:, feats : feats + 1].astype(f32))
    lane = lax.broadcasted_iota(jnp.int32, (wide, LANES), 1)
    own_ones = jnp.where(lane < feats, own, jnp.ones_like(own))

    gates6 = masks.reshape(SLOTS, chunk // rows, C, rows, lats)
    gates5 = lax.dynamic_index_in_dim(gates6, place, 0, keepdims=False)
    gates_own = lax.dynamic_index_in_dim(gates5, core, 1, keepdims=False).reshape(chunk, lats)
    gates_send = lax.dynamic_index_in_dim(gates5, 1 - core, 1, keepdims=False).reshape(chunk, lats)
    w_own = w_dec[0]
    pack = jnp.concatenate(
        [
            w_enc,
            jnp.zeros((pad, lats), bf16),
            gates_send.astype(bf16),
            split_bf16(b_enc),
            jnp.zeros((13, lats), bf16),
        ],
        axis=0,
    )
    pack_other = swap(pack, "c", C, 1)
    w_other = swap(w_own, "c", C, 1)
    w_both = jnp.concatenate([w_own, w_other], axis=0)
    enc_both = jnp.concatenate([pack[:LANES], pack_other[:LANES]], axis=1)
    gates_other = pack_other[LANES : LANES + chunk].astype(f32)
    gates = jnp.concatenate([gates_own.astype(f32), gates_other], axis=1)
    bias_rows = pack_other[LANES + chunk : LANES + chunk + 3].astype(f32)
    b_both = jnp.concatenate([b_enc, bias_rows[0] + bias_rows[1] + bias_rows[2]])

    slots = jnp.arange(target_of.shape[0], dtype=jnp.int32)
    layer = jnp.sum(jnp.where(slots == yh * X + x, target_of, 0))
    flag = (layer >= source).astype(f32)
    squares = flag * jnp.einsum("cd,cd->c", w_both, w_both, preferred_element_type=f32)

    top_sq = jnp.max(squares)
    e_term = exponent(jnp.sqrt(depth * 1.01 * top_sq) * top_err)
    e_sq = exponent(top_sq)

    def lines(sq, e, tops):
        scaled = sq * jnp.exp2(TOP - e)
        hi = scaled.astype(f16)
        rest = (scaled - hi.astype(f32)).astype(f16)
        table = [hi[None], rest[None], jnp.broadcast_to(e.astype(f16), (1, both_lats)), tops.astype(f16)]
        spare = EXTRA - 3 - tops.shape[0]
        return jnp.concatenate(table + [jnp.zeros((spare, both_lats), f16)], axis=0)

    def unlines(table):
        return (table[0] + table[1]) * jnp.exp2(table[2] - TOP), table[2, 0]

    partial_pre = jnp.dot(own, enc_both, preferred_element_type=f32) * PRE_SCALE
    extra = lines(squares, e_sq, jnp.broadcast_to(e_term, (1, both_lats)))
    pre_out = jnp.concatenate(
        [
            partial_pre.astype(f16).reshape(X, YH * chunk, both_lats),
            jnp.broadcast_to(extra[None], (X, EXTRA, both_lats)),
        ],
        axis=1,
    )
    blocks = [lax.dynamic_index_in_dim(pre_out, x, 0, keepdims=False)]
    for k in range(1, X):
        blocks.append(swap(lax.dynamic_index_in_dim(pre_out, x ^ k, 0, keepdims=False), "x", X, k))
    blocks = [b.astype(f32) for b in blocks]
    pre = sum(b[: YH * chunk] for b in blocks)
    sq, e_sq = 0.0, -100.0
    tops = jnp.zeros((X, both_lats), f32)
    for k in range(X):
        table = blocks[k][YH * chunk :]
        sq_k, e_k = unlines(table)
        sq, e_sq = sq + sq_k, jnp.maximum(e_sq, e_k)
        tops = tops + jnp.where(lax.broadcasted_iota(jnp.int32, (X, 1), 0) == (x ^ k), table[3:4], 0.0)
    pre = pre.reshape(YH, chunk, both_lats)
    half = jnp.concatenate(
        [
            lax.dynamic_index_in_dim(pre, 1 - yh, 0, keepdims=False).astype(f16),
            lines(sq, e_sq + 2.0, tops),
        ],
        axis=0,
    )
    half = swap(half, "yh", YH, 1).astype(f32)
    pre = lax.dynamic_index_in_dim(pre, yh, 0, keepdims=False) + half[:chunk]
    pre = pre * (1.0 / PRE_SCALE) + b_both[None, :]
    sumsq = sq + unlines(half[chunk:])[0]
    tops_far = half[chunk + 3 : chunk + 3 + X]
    first = yh == 0
    tops = jnp.stack([jnp.where(first, tops, tops_far), jnp.where(first, tops_far, tops)], axis=1)
    unscale = jnp.exp2(tops.reshape(SLOTS, 1, both_lats) - TOP)
    norm = jnp.sqrt(sumsq)[None, :]
    tanh_val = jnp.tanh(sharpness * (gates * pre) * norm)
    pull = penalty * sharpness * norm * (1.0 - tanh_val * tanh_val)

    term = lax.dot_general(errs, w_both, dims, preferred_element_type=f32)
    term = (term * (flag * jnp.exp2(TOP - e_term))).astype(f16).reshape(SLOTS, chunk, both_lats)
    terms = lax.all_to_all(term, SUMS, 0, 0, tiled=True)
    dact = jnp.sum(terms.astype(f32) * unscale, axis=0)
    grad = (gates * (dact + pull)).astype(bf16)

    grad = lax.all_to_all(
        jnp.broadcast_to(grad[None], (SLOTS, chunk, both_lats)), SUMS, 0, 0, tiled=True
    ).reshape(wide, both_lats)

    part = lax.dot_general(grad, enc_both, dims, preferred_element_type=f32)
    e_part = exponent(jnp.max(jnp.abs(part)))
    sent = jnp.where(lane < feats, part * jnp.exp2(TOP - e_part), e_part).astype(f16)
    sent, grad = lax.optimization_barrier((sent, grad))
    came = lax.all_to_all(sent.reshape(PEERS, rows, LANES), PLANE, 0, 0, tiled=True)
    came = came.reshape(wide, LANES)

    enc = lax.dot_general(own_ones, grad, rows_dims, preferred_element_type=f32)
    away = swap(enc[: feats + 8, lats:], "c", C, 1)
    grad_enc = enc[:feats, :lats] + away[:feats]
    grad_bias = enc[feats, :lats] + away[feats]

    spread = (lax.broadcasted_iota(jnp.int32, (LANES, feats), 0) == feats).astype(bf16)
    e_rows = jnp.dot(came.astype(bf16), spread, preferred_element_type=f32)
    values = came[:, :feats].astype(f32) * jnp.exp2(e_rows - TOP)
    sums = jnp.sum(values.reshape(S, PEERS // S, rows, feats), axis=1)
    return (grad_enc, grad_bias, jnp.transpose(sums, (1, 0, 2)))


def solution(mesh):
    fine = Mesh(mesh.devices.reshape(YL, Z, C, YH, X), AXES)
    return jax.shard_map(
        local,
        mesh=fine,
        in_specs=(
            P(LAT, None, TGT),
            P(TGT, LAT),
            P(LAT),
            P(None, LAT),
            P(TGT, LAT, None),
            P(TGT, LAT, None),
            P(),
        ),
        out_specs=(P(TGT, LAT), P(LAT), P(LAT, None, TGT)),
        check_vma=False,
    )
```

time: 831 us -> 192 us (0.23)
  the two profiles are of different devices: /device:TPU:1 before, /device:TPU:8 now
where the time goes in v2:
time: 192 us; the launch traced here: 191 us
  starting transfers between devices  84 us (44%)
  waiting for transfers between devices  53.3 us (28%)
  other arithmetic  20.4 us (11%)
  local copies, waits for them, and re-layouts  17 us (9%)
  between operations  8.06 us (4%)
  matrix products  7.95 us (4%)
    ppermute x12, starting transfers between devices, swap(): return lax.ppermute(value, axis, [(i, i ^ distance) for i in range(size)])  45.7 us
    ppermute x12, waiting for transfers between devices, swap(): return lax.ppermute(value, axis, [(i, i ^ distance) for i in range(size)])  30.9 us
    all_to_all x1, waiting for transfers between devices, local(): lax.all_to_all(jnp.broadcast_to(grad[None], (SLOTS, chunk, both_lats)), S...  15.3 us
    all_to_all x1, starting transfers between devices, local(): lax.all_to_all(jnp.broadcast_to(errors, (PEERS, rows, depth)), PLANE, 0,...  14 us
    all_to_all x1, starting transfers between devices, local(): lax.all_to_all(jnp.broadcast_to(grad[None], (SLOTS, chunk, both_lats)), S...  9.6 us
    all_to_all x1, starting transfers between devices, local(): lax.all_to_all(sent.reshape(PEERS, rows, LANES), PLANE, 0, 0, tiled=True)  7.48 us
    all_to_all x1, starting transfers between devices, local(): terms = lax.all_to_all(term, SUMS, 0, 0, tiled=True)  7.22 us
    all_to_all x1, waiting for transfers between devices, local(): lax.all_to_all(sent.reshape(PEERS, rows, LANES), PLANE, 0, 0, tiled=True)  7.19 us
  transfers between devices with their start and end apart: 16, of which 7 were waited for; matrix products, arithmetic and copies ran while one was open for 21% of the time, Pallas kernels for 0%

profile of v2, /device:TPU:8, one launch (start us, length us, event | category | flops | bytes accessed | tf_op | source)
XLA Modules:
  0.0 190.7 jit_solution(14019780427007001756)
XLA Ops:
  0.7 2.1 %collective-permute-start.6 = (bf16[512,2304]{1,0:T(8,128)(2,1)}, bf16[512,2304]{1,0:T(8,128)(2,1)}, u32[]{:S(2)}, u32[]{:S(2)}) collective-permute-start(bf16[512,2304]{1,0:T(8,128)(2,1)} %bitcast.73), channel_id=1, source_target_pairs={{0,8},{8,0},{1,9},{9,1},{2,10},{10,2},{3,11},{11,3},{4,12},{12,4},... | collective-permute-start | bytes 7077896 | tf_op jit(solution)/shard_map/ppermute | solution.py:37
  2.7 1.9 broadcast_in_dim.124
  4.6 14.0 %all-to-all-start = ((bf16[32,8,2304]{2,1,0:T(8,128)(2,1)}), bf16[32,8,2304]{2,1,0:T(8,128)(2,1)S(1)}, u32[]{:S(2)}, u32[]{:S(2)}) async-start(bf16[32,8,2304]{2,1,0:T(8,128)(2,1)} %broadcast_in_dim.124), calls=%async_computation | async-start | bytes 2359296 | tf_op jit(solution)/shard_map/all_to_all | solution.py:56
  18.6 0.6 abs_reduce_fusion.1
  19.9 4.3 %collective-permute-start = (bf16[1,8,384]{2,1,0:T(8,128)(2,1)S(1)}, bf16[1,8,384]{2,1,0:T(8,128)(2,1)S(1)}, u32[]{:S(2)}, u32[]{:S(2)}) collective-permute-start(bf16[1,8,384]{2,1,0:T(8,128)(2,1)S(1)} %fusion.44), channel_id=1, source_target_pairs={{0,256},{128,384},{256,0},{384,128},{1,257},{129,385},{257,1},{385... | collective-permute-start | bytes 18440 | tf_op jit(solution)/shard_map/ppermute | solution.py:37
  24.3 20.8 %collective-permute-done = bf16[1,8,384]{2,1,0:T(8,128)(2,1)S(1)} collective-permute-done((bf16[1,8,384]{2,1,0:T(8,128)(2,1)S(1)}, bf16[1,8,384]{2,1,0:T(8,128)(2,1)S(1)}, u32[]{:S(2)}, u32[]{:S(2)}) %collective-permute-start) | collective-permute-done | bytes 6176 | tf_op jit(solution)/shard_map/ppermute | solution.py:37
  45.1 3.3 %collective-permute-start.1 = (bf16[2,8,384]{2,1,0:T(8,128)(2,1)S(1)}, bf16[2,8,384]{2,1,0:T(8,128)(2,1)S(1)}, u32[]{:S(2)}, u32[]{:S(2)}) collective-permute-start(bf16[2,8,384]{2,1,0:T(8,128)(2,1)S(1)} %pad_maximum_fusion.10), channel_id=1, source_target_pairs={{0,16},{16,0},{32,48},{48,32},{64,80},{80,64},{96,112},{112,96},{1... | collective-permute-start | bytes 36872 | tf_op jit(solution)/shard_map/ppermute | solution.py:37
  48.4 1.5 convert_bitcast_fusion
  50.0 4.5 %concatenate.51 = bf16[432,512]{1,0:T(8,128)(2,1)} concatenate(bf16[288,512]{1,0:T(8,128)(2,1)S(1)} %copy-done.6, bf16[96,512]{1,0:T(8,128)(2,1)S(1)} %broadcast_in_dim.122, bf16[32,512]{1,0:T(8,128)(2,1)S(1)} %get-tuple-element.13, bf16[1,512]{1,0:T(2,128)(2,1)S(1)} %stack.18, bf16[1,512]{1,0:T(2,128)(2,1)S(1)} %stack.19, bf16[1,512]{1,0:T(2,128)(2,1)S(1)} %stack.20, ...), dimensions={0} | concatenate | bytes 884736 | tf_op jit(solution)/shard_map/concatenate | solution.py:81
  54.6 1.9 %collective-permute-start.5 = (bf16[432,512]{1,0:T(8,128)(2,1)}, bf16[432,512]{1,0:T(8,128)(2,1)}, u32[]{:S(2)}, u32[]{:S(2)}) collective-permute-start(bf16[432,512]{1,0:T(8,128)(2,1)} %concatenate.51), channel_id=1, source_target_pairs={{0,8},{8,0},{1,9},{9,1},{2,10},{10,2},{3,11},{11,3},{4,12},{12,4},... | collective-permute-start | bytes 1327112 | tf_op jit(solution)/shard_map/ppermute | solution.py:37
  56.5 4.0 %collective-permute-start.2 = (bf16[2,16,384]{2,1,0:T(8,128)(2,1)S(1)}, bf16[2,16,384]{2,1,0:T(8,128)(2,1)S(1)}, u32[]{:S(2)}, u32[]{:S(2)}) collective-permute-start(bf16[2,16,384]{2,1,0:T(8,128)(2,1)S(1)} %pad_maximum_fusion.9), channel_id=1, source_target_pairs={{0,32},{16,48},{32,0},{48,16},{64,96},{80,112},{96,64},{112,80},{1... | collective-permute-start | bytes 73736 | tf_op jit(solution)/shard_map/ppermute | solution.py:37
  60.6 0.6 fusion.66
  61.2 2.3 %collective-permute-done.2 = bf16[2,16,384]{2,1,0:T(8,128)(2,1)S(1)} collective-permute-done((bf16[2,16,384]{2,1,0:T(8,128)(2,1)S(1)}, bf16[2,16,384]{2,1,0:T(8,128)(2,1)S(1)}, u32[]{:S(2)}, u32[]{:S(2)}) %collective-permute-start.2) | collective-permute-done | bytes 24608 | tf_op jit(solution)/shard_map/ppermute | solution.py:37
  63.5 5.6 %collective-permute-start.3 = (bf16[2,32,384]{2,1,0:T(8,128)(2,1)S(1)}, bf16[2,32,384]{2,1,0:T(8,128)(2,1)S(1)}, u32[]{:S(2)}, u32[]{:S(2)}) collective-permute-start(bf16[2,32,384]{2,1,0:T(8,128)(2,1)S(1)} %pad_maximum_fusion.8), channel_id=1, source_target_pairs={{0,64},{16,80},{32,96},{48,112},{64,0},{80,16},{96,32},{112,48},{1... | collective-permute-start | bytes 147464 | tf_op jit(solution)/shard_map/ppermute | solution.py:37
  70.4 3.4 %collective-permute-done.3 = bf16[2,32,384]{2,1,0:T(8,128)(2,1)S(1)} collective-permute-done((bf16[2,32,384]{2,1,0:T(8,128)(2,1)S(1)}, bf16[2,32,384]{2,1,0:T(8,128)(2,1)S(1)}, u32[]{:S(2)}, u32[]{:S(2)}) %collective-permute-start.3) | collective-permute-done | bytes 49184 | tf_op jit(solution)/shard_map/ppermute | solution.py:37
  73.8 5.0 %collective-permute-start.4 = (bf16[2,64,384]{2,1,0:T(8,128)(2,1)S(1)}, bf16[2,64,384]{2,1,0:T(8,128)(2,1)S(1)}, u32[]{:S(2)}, u32[]{:S(2)}) collective-permute-start(bf16[2,64,384]{2,1,0:T(8,128)(2,1)S(1)} %pad_maximum_fusion.7), channel_id=1, source_target_pairs={{0,128},{128,0},{256,384},{384,256},{1,129},{129,1},{257,385},{385... | collective-permute-start | bytes 294920 | tf_op jit(solution)/shard_map/ppermute | solution.py:37
  79.4 2.0 %collective-permute-done.4 = bf16[2,64,384]{2,1,0:T(8,128)(2,1)S(1)} collective-permute-done((bf16[2,64,384]{2,1,0:T(8,128)(2,1)S(1)}, bf16[2,64,384]{2,1,0:T(8,128)(2,1)S(1)}, u32[]{:S(2)}, u32[]{:S(2)}) %collective-permute-start.4) | collective-permute-done | bytes 98336 | tf_op jit(solution)/shard_map/ppermute | solution.py:37
  81.5 0.7 slice_reduce_fusion
  82.1 1.1 slice.208
  83.2 0.7 slice_convert_fusion.1
  84.5 1.4 slice_convert_fusion
  85.9 2.2 %fusion.5 = f16[256,1024]{1,0:T(8,128)(2,1)} fusion(bf16[256,384]{1,0:T(8,128)(2,1)S(1)} %bitcast.81, bf16[288,512]{1,0:T(8,128)(2,1)} %param.8, bf16[384,512]{1,0:T(8,128)(2,1)S(1)} %slice.208), kind=kOutput, calls=%fused_computation.9 | convolution fusion | flops 204210176 | bytes 1409024 | tf_op jit(solution)/shard_map/dot_general | solution.py:120
  88.1 2.7 %fusion = f32[1024]{0:T(1024)S(1)} fusion(bf16[512,2304]{1,0:T(8,128)(2,1)} %collective-permute-done.6, bf16[512,2304]{1,0:T(8,128)(2,1)S(1)} %bitcast.74), kind=kLoop, calls=%fused_computation.1 | loop fusion | flops 14154752 | bytes 4722688 | tf_op jit(solution)/shard_map/cd,cd->c/dot_general | solution.py:103
  96.5 0.8 concatenate.56
  97.2 2.3 %fusion.77 = (f32[72,1024]{1,0:T(8,128)}, f16[72,1024]{1,0:T(8,128)(2,1)}, f16[72,1024]{1,0:T(8,128)(2,1)}, f16[72,1024]{1,0:T(8,128)(2,1)}, f32[1,72,1024]{2,1,0:T(8,128)}) fusion(s32[]{:T(128)S(6)} %select_n.173, f16[4,8,1024]{2,1,0:T(8,128)(2,1)S(1)} %broadcast_in_dim.132, f16[4,64,1024]{2,1,0:T(8,128)(2,1)} %bitcast.86, s32[]{:T(128)S(6)} %select_n.175, ...), kind=kLoop, calls=%fused_computation.153 | loop fusion | flops 516096 | bytes 1622032 | tf_op jit(solution)/shard_map/convert_element_type | solution.py:132
  99.5 4.7 %collective-permute-start.9 = (f16[72,1024]{1,0:T(8,128)(2,1)}, f16[72,1024]{1,0:T(8,128)(2,1)}, u32[]{:S(2)}, u32[]{:S(2)}) collective-permute-start(f16[72,1024]{1,0:T(8,128)(2,1)} %get-tuple-element.17), channel_id=1, source_target_pairs={{0,3},{1,2},{2,1},{3,0},{4,7},{5,6},{6,5},{7,4},{8,11},{9,10},{10,... | collective-permute-start | bytes 442376 | tf_op jit(solution)/shard_map/ppermute | solution.py:37
  104.2 2.7 %collective-permute-start.8 = (f16[72,1024]{1,0:T(8,128)(2,1)}, f16[72,1024]{1,0:T(8,128)(2,1)}, u32[]{:S(2)}, u32[]{:S(2)}) collective-permute-start(f16[72,1024]{1,0:T(8,128)(2,1)} %get-tuple-element.16), channel_id=1, source_target_pairs={{0,2},{1,3},{2,0},{3,1},{4,6},{5,7},{6,4},{7,5},{8,10},{9,11},{10,... | collective-permute-start | bytes 442376 | tf_op jit(solution)/shard_map/ppermute | solution.py:37
  106.9 2.5 %collective-permute-start.7 = (f16[72,1024]{1,0:T(8,128)(2,1)}, f16[72,1024]{1,0:T(8,128)(2,1)}, u32[]{:S(2)}, u32[]{:S(2)}) collective-permute-start(f16[72,1024]{1,0:T(8,128)(2,1)} %get-tuple-element.15), channel_id=1, source_target_pairs={{0,1},{1,0},{2,3},{3,2},{4,5},{5,4},{6,7},{7,6},{8,9},{9,8},{10,11... | collective-permute-start | bytes 442376 | tf_op jit(solution)/shard_map/ppermute | solution.py:37
  109.3 3.9 %fusion.4 = f16[1024,256]{0,1:T(8,128)(2,1)} fusion(bf16[512,2304]{1,0:T(8,128)(2,1)} %collective-permute-done.6, bf16[512,2304]{1,0:T(8,128)(2,1)S(1)} %bitcast.75, bf16[32,8,2304]{2,1,0:T(8,128)(2,1)S(1)} %all-to-all-done, f32[]{:T(128)S(6)} %mul.134), kind=kOutput, calls=%fused_computation.8 | convolution fusion | flops 1217921024 | bytes 6422532 | tf_op jit(solution)/shard_map/dot_general | solution.py:161
  113.3 7.2 %all-to-all-start.1 = ((f16[8,32,1024]{2,1,0:T(8,128)(2,1)}), f16[8,32,1024]{2,1,0:T(8,128)(2,1)S(1)}, u32[]{:S(2)}, u32[]{:S(2)}) async-start(f16[8,32,1024]{2,1,0:T(8,128)(2,1)} %bitcast.85), calls=%async_computation.1 | async-start | bytes 1048576 | tf_op jit(solution)/shard_map/all_to_all | solution.py:163
  120.5 1.2 slice.229
  121.7 0.8 slice.209
  123.2 0.9 convert_element_type.150
  124.6 0.9 convert_element_type.151
  126.0 0.9 convert_element_type.152
  129.9 7.8 %collective-permute-start.10 = (f16[40,1024]{1,0:T(8,128)(2,1)S(1)}, f16[40,1024]{1,0:T(8,128)(2,1)S(1)}, u32[]{:S(2)}, u32[]{:S(2)}) collective-permute-start(f16[40,1024]{1,0:T(8,128)(2,1)S(1)} %concatenate.58), channel_id=1, source_target_pairs={{0,4},{4,0},{1,5},{5,1},{2,6},{6,2},{3,7},{7,3},{8,12},{12,8},{9,1... | collective-permute-start | bytes 245768 | tf_op jit(solution)/shard_map/ppermute | solution.py:37
  137.8 2.4 %collective-permute-done.10 = f16[40,1024]{1,0:T(8,128)(2,1)S(1)} collective-permute-done((f16[40,1024]{1,0:T(8,128)(2,1)S(1)}, f16[40,1024]{1,0:T(8,128)(2,1)S(1)}, u32[]{:S(2)}, u32[]{:S(2)}) %collective-permute-start.10) | collective-permute-done | bytes 81952 | tf_op jit(solution)/shard_map/ppermute | solution.py:37
  140.6 0.9 broadcast_in_dim.147
  141.5 9.6 %all-to-all-start.2 = ((bf16[8,32,1024]{2,1,0:T(8,128)(2,1)}), bf16[8,32,1024]{2,1,0:T(8,128)(2,1)S(1)}, u32[]{:S(2)}, u32[]{:S(2)}) async-start(bf16[8,32,1024]{2,1,0:T(8,128)(2,1)} %broadcast_in_dim.147), calls=%async_computation.2 | async-start | bytes 1048576 | tf_op jit(solution)/shard_map/all_to_all | solution.py:167
  151.1 15.3 %all-to-all-done.2 = bf16[8,32,1024]{2,1,0:T(8,128)(2,1)S(1)} async-done(((bf16[8,32,1024]{2,1,0:T(8,128)(2,1)}), bf16[8,32,1024]{2,1,0:T(8,128)(2,1)S(1)}, u32[]{:S(2)}, u32[]{:S(2)}) %all-to-all-start.2) | async-done | bytes 524320 | tf_op jit(solution)/shard_map/all_to_all | solution.py:167
  166.4 1.1 abs_reduce_fusion
  168.2 0.7 select_convert_fusion
  168.9 7.5 %all-to-all-start.3 = ((f16[32,8,384]{2,1,0:T(8,128)(2,1)}), f16[32,8,384]{2,1,0:T(8,128)(2,1)S(1)}, u32[]{:S(2)}, u32[]{:S(2)}) async-start(f16[32,8,384]{2,1,0:T(8,128)(2,1)} %bitcast.33), calls=%async_computation.3 | async-start | bytes 393216 | tf_op jit(solution)/shard_map/all_to_all | solution.py:175
  176.9 1.9 %collective-permute-start.11 = (f32[296,512]{1,0:T(8,128)S(1)}, f32[296,512]{1,0:T(8,128)}, u32[]{:S(2)}, u32[]{:S(2)}) collective-permute-start(f32[296,512]{1,0:T(8,128)S(1)} %slice.243), channel_id=1, source_target_pairs={{0,8},{8,0},{1,9},{9,1},{2,10},{10,2},{3,11},{11,3},{4,12},{12,4},... | collective-permute-start | bytes 1818632 | tf_op jit(solution)/shard_map/ppermute | solution.py:37
  178.8 7.2 %all-to-all-done.3 = f16[32,8,384]{2,1,0:T(8,128)(2,1)S(1)} async-done(((f16[32,8,384]{2,1,0:T(8,128)(2,1)}), f16[32,8,384]{2,1,0:T(8,128)(2,1)S(1)}, u32[]{:S(2)}, u32[]{:S(2)}) %all-to-all-start.3) | async-done | bytes 196640 | tf_op jit(solution)/shard_map/all_to_all | solution.py:175
  186.8 0.6 copy.19
  187.4 2.0 %slice_add_fusion = f32[288,512]{1,0:T(8,128)} fusion(f32[296,512]{1,0:T(8,128)} %collective-permute-done.11, f32[384,1024]{1,0:T(8,128)S(1)} %fusion.16), kind=kLoop, calls=%fused_computation.21 | loop fusion | flops 147456 | bytes 1769472 | tf_op jit(solution)/shard_map/add | solution.py:180
  189.4 1.3 slice_add_fusion.15
  (106 shorter events, 9.3 us)
Async XLA Ops:
  0.6 18.0 %copy-start.10 = (bf16[1,8,2304]{2,1,0:T(8,128)(2,1)S(1)}, bf16[1,8,2304]{2,1,0:T(8,128)(2,1)}, u32[]{:S(2)}) copy-start(bf16[1,8,2304]{2,1,0:T(8,128)(2,1)} %param.12) | copy-start | bytes 110596
  0.6 18.6 %copy-start.11 = (bf16[8,2,288]{2,1,0:T(2,128)(2,1)S(1)}, bf16[8,2,288]{2,1,0:T(2,128)(2,1)}, u32[]{:S(2)}) copy-start(bf16[8,2,288]{2,1,0:T(2,128)(2,1)} %param.7) | copy-start | bytes 27652
  0.7 23.6 %copy-start.12 = (f32[512]{0:T(512)S(1)}, f32[512]{0:T(512)}, u32[]{:S(2)}) copy-start(f32[512]{0:T(512)} %param.9) | copy-start | bytes 6148
  0.7 49.3 %copy-start.6 = (bf16[288,512]{1,0:T(8,128)(2,1)S(1)}, bf16[288,512]{1,0:T(8,128)(2,1)}, u32[]{:S(2)}) copy-start(bf16[288,512]{1,0:T(8,128)(2,1)} %param.8) | copy-start | bytes 884740
  0.7 87.5 %collective-permute-start.6 = (bf16[512,2304]{1,0:T(8,128)(2,1)}, bf16[512,2304]{1,0:T(8,128)(2,1)}, u32[]{:S(2)}, u32[]{:S(2)}) collective-permute-start(bf16[512,2304]{1,0:T(8,128)(2,1)} %bitcast.73), channel_id=1, source_target_pairs={{0,8},{8,0},{1,9},{9,1},{2,10},{10,2},{3,11},{11,3},{4,12},{12,4},... | collective-permute-start | bytes 7077896 | tf_op jit(solution)/shard_map/ppermute | solution.py:37
  2.7 57.8 %copy-start.19 = (s32[8]{0:T(128)S(1)}, s32[8]{0:T(128)}, u32[]{:S(2)}) copy-start(s32[8]{0:T(128)} %param.13) | copy-start | bytes 100
  4.6 104.7 %all-to-all-start = ((bf16[32,8,2304]{2,1,0:T(8,128)(2,1)}), bf16[32,8,2304]{2,1,0:T(8,128)(2,1)S(1)}, u32[]{:S(2)}, u32[]{:S(2)}) async-start(bf16[32,8,2304]{2,1,0:T(8,128)(2,1)} %broadcast_in_dim.124), calls=%async_computation | async-start | bytes 2359296 | tf_op jit(solution)/shard_map/all_to_all | solution.py:56
  19.9 25.2 %collective-permute-start = (bf16[1,8,384]{2,1,0:T(8,128)(2,1)S(1)}, bf16[1,8,384]{2,1,0:T(8,128)(2,1)S(1)}, u32[]{:S(2)}, u32[]{:S(2)}) collective-permute-start(bf16[1,8,384]{2,1,0:T(8,128)(2,1)S(1)} %fusion.44), channel_id=1, source_target_pairs={{0,256},{128,384},{256,0},{384,128},{1,257},{129,385},{257,1},{385... | collective-permute-start | bytes 18440 | tf_op jit(solution)/shard_map/ppermute | solution.py:37
  45.1 11.4 %collective-permute-start.1 = (bf16[2,8,384]{2,1,0:T(8,128)(2,1)S(1)}, bf16[2,8,384]{2,1,0:T(8,128)(2,1)S(1)}, u32[]{:S(2)}, u32[]{:S(2)}) collective-permute-start(bf16[2,8,384]{2,1,0:T(8,128)(2,1)S(1)} %pad_maximum_fusion.10), channel_id=1, source_target_pairs={{0,16},{16,0},{32,48},{48,32},{64,80},{80,64},{96,112},{112,96},{1... | collective-permute-start | bytes 36872 | tf_op jit(solution)/shard_map/ppermute | solution.py:37
  54.6 27.6 %collective-permute-start.5 = (bf16[432,512]{1,0:T(8,128)(2,1)}, bf16[432,512]{1,0:T(8,128)(2,1)}, u32[]{:S(2)}, u32[]{:S(2)}) collective-permute-start(bf16[432,512]{1,0:T(8,128)(2,1)} %concatenate.51), channel_id=1, source_target_pairs={{0,8},{8,0},{1,9},{9,1},{2,10},{10,2},{3,11},{11,3},{4,12},{12,4},... | collective-permute-start | bytes 1327112 | tf_op jit(solution)/shard_map/ppermute | solution.py:37
  56.5 6.9 %collective-permute-start.2 = (bf16[2,16,384]{2,1,0:T(8,128)(2,1)S(1)}, bf16[2,16,384]{2,1,0:T(8,128)(2,1)S(1)}, u32[]{:S(2)}, u32[]{:S(2)}) collective-permute-start(bf16[2,16,384]{2,1,0:T(8,128)(2,1)S(1)} %pad_maximum_fusion.9), channel_id=1, source_target_pairs={{0,32},{16,48},{32,0},{48,16},{64,96},{80,112},{96,64},{112,80},{1... | collective-permute-start | bytes 73736 | tf_op jit(solution)/shard_map/ppermute | solution.py:37
  63.5 10.3 %collective-permute-start.3 = (bf16[2,32,384]{2,1,0:T(8,128)(2,1)S(1)}, bf16[2,32,384]{2,1,0:T(8,128)(2,1)S(1)}, u32[]{:S(2)}, u32[]{:S(2)}) collective-permute-start(bf16[2,32,384]{2,1,0:T(8,128)(2,1)S(1)} %pad_maximum_fusion.8), channel_id=1, source_target_pairs={{0,64},{16,80},{32,96},{48,112},{64,0},{80,16},{96,32},{112,48},{1... | collective-permute-start | bytes 147464 | tf_op jit(solution)/shard_map/ppermute | solution.py:37
  73.8 7.5 %collective-permute-start.4 = (bf16[2,64,384]{2,1,0:T(8,128)(2,1)S(1)}, bf16[2,64,384]{2,1,0:T(8,128)(2,1)S(1)}, u32[]{:S(2)}, u32[]{:S(2)}) collective-permute-start(bf16[2,64,384]{2,1,0:T(8,128)(2,1)S(1)} %pad_maximum_fusion.7), channel_id=1, source_target_pairs={{0,128},{128,0},{256,384},{384,256},{1,129},{129,1},{257,385},{385... | collective-permute-start | bytes 294920 | tf_op jit(solution)/shard_map/ppermute | solution.py:37
  81.4 6.7 %copy-start = (bf16[1,512,2304]{2,1,0:T(8,128)(2,1)S(1)}, bf16[1,512,2304]{2,1,0:T(8,128)(2,1)}, u32[]{:S(2)}) copy-start(bf16[1,512,2304]{2,1,0:T(8,128)(2,1)} %param.11) | copy-start | bytes 7077892
  81.4 4.5 %copy-start.2 = (bf16[2,128,384]{2,1,0:T(8,128)(2,1)}, bf16[2,128,384]{2,1,0:T(8,128)(2,1)S(1)}, u32[]{:S(2)}) copy-start(bf16[2,128,384]{2,1,0:T(8,128)(2,1)S(1)} %pad_maximum_fusion.6) | copy-start | bytes 589828
  83.2 4.9 %copy-start.4 = (bf16[384,512]{1,0:T(8,128)(2,1)}, bf16[384,512]{1,0:T(8,128)(2,1)S(1)}, u32[]{:S(2)}) copy-start(bf16[384,512]{1,0:T(8,128)(2,1)S(1)} %slice.208) | copy-start | bytes 1179652
  99.5 26.5 %collective-permute-start.9 = (f16[72,1024]{1,0:T(8,128)(2,1)}, f16[72,1024]{1,0:T(8,128)(2,1)}, u32[]{:S(2)}, u32[]{:S(2)}) collective-permute-start(f16[72,1024]{1,0:T(8,128)(2,1)} %get-tuple-element.17), channel_id=1, source_target_pairs={{0,3},{1,2},{2,1},{3,0},{4,7},{5,6},{6,5},{7,4},{8,11},{9,10},{10,... | collective-permute-start | bytes 442376 | tf_op jit(solution)/shard_map/ppermute | solution.py:37
  104.2 20.5 %collective-permute-start.8 = (f16[72,1024]{1,0:T(8,128)(2,1)}, f16[72,1024]{1,0:T(8,128)(2,1)}, u32[]{:S(2)}, u32[]{:S(2)}) collective-permute-start(f16[72,1024]{1,0:T(8,128)(2,1)} %get-tuple-element.16), channel_id=1, source_target_pairs={{0,2},{1,3},{2,0},{3,1},{4,6},{5,7},{6,4},{7,5},{8,10},{9,11},{10,... | collective-permute-start | bytes 442376 | tf_op jit(solution)/shard_map/ppermute | solution.py:37
  106.9 16.3 %collective-permute-start.7 = (f16[72,1024]{1,0:T(8,128)(2,1)}, f16[72,1024]{1,0:T(8,128)(2,1)}, u32[]{:S(2)}, u32[]{:S(2)}) collective-permute-start(f16[72,1024]{1,0:T(8,128)(2,1)} %get-tuple-element.15), channel_id=1, source_target_pairs={{0,1},{1,0},{2,3},{3,2},{4,5},{5,4},{6,7},{7,6},{8,9},{9,8},{10,11... | collective-permute-start | bytes 442376 | tf_op jit(solution)/shard_map/ppermute | solution.py:37
  113.2 13.7 %copy-start.1 = (f32[1,72,1024]{2,1,0:T(8,128)S(1)}, f32[1,72,1024]{2,1,0:T(8,128)}, u32[]{:S(2)}) copy-start(f32[1,72,1024]{2,1,0:T(8,128)} %get-tuple-element.18) | copy-start | bytes 884740
  113.2 16.5 %copy-start.15 = (pred[4]{0:T(512)(128)(4,1)S(1)}, pred[4]{0:T(512)(128)(4,1)}, u32[]{:S(2)}) copy-start(pred[4]{0:T(512)(128)(4,1)} %get-tuple-element.41) | copy-start | bytes 16
  113.2 16.5 %copy-start.16 = (pred[4]{0:T(512)(128)(4,1)S(1)}, pred[4]{0:T(512)(128)(4,1)}, u32[]{:S(2)}) copy-start(pred[4]{0:T(512)(128)(4,1)} %get-tuple-element.42) | copy-start | bytes 16
  113.2 16.5 %copy-start.17 = (pred[4]{0:T(512)(128)(4,1)S(1)}, pred[4]{0:T(512)(128)(4,1)}, u32[]{:S(2)}) copy-start(pred[4]{0:T(512)(128)(4,1)} %get-tuple-element.43) | copy-start | bytes 16
  113.2 16.5 %copy-start.18 = (pred[4]{0:T(512)(128)(4,1)S(1)}, pred[4]{0:T(512)(128)(4,1)}, u32[]{:S(2)}) copy-start(pred[4]{0:T(512)(128)(4,1)} %get-tuple-element.44) | copy-start | bytes 16
  113.3 24.5 %copy-start.13 = (f32[512]{0:T(512)S(1)}, f32[512]{0:T(512)}, u32[]{:S(2)}) copy-start(f32[512]{0:T(512)} %param.9) | copy-start | bytes 6148
  113.3 24.5 %copy-start.14 = (f32[1,512]{1,0:T(1,128)S(1)}, f32[1,512]{1,0:T(1,128)}, u32[]{:S(2)}) copy-start(f32[1,512]{1,0:T(1,128)} %slice_add_fusion.16) | copy-start | bytes 6148
  113.3 27.1 %all-to-all-start.1 = ((f16[8,32,1024]{2,1,0:T(8,128)(2,1)}), f16[8,32,1024]{2,1,0:T(8,128)(2,1)S(1)}, u32[]{:S(2)}, u32[]{:S(2)}) async-start(f16[8,32,1024]{2,1,0:T(8,128)(2,1)} %bitcast.85), calls=%async_computation.1 | async-start | bytes 1048576 | tf_op jit(solution)/shard_map/all_to_all | solution.py:163
  120.5 20.1 %copy-start.8 = (f32[32,512]{1,0:T(8,128)S(1)}, f32[32,512]{1,0:T(8,128)}, u32[]{:S(2)}) copy-start(f32[32,512]{1,0:T(8,128)} %get-tuple-element.12) | copy-start | bytes 196612
  120.5 20.1 %copy-start.9 = (f32[32,512]{1,0:T(8,128)S(1)}, f32[32,512]{1,0:T(8,128)}, u32[]{:S(2)}) copy-start(f32[32,512]{1,0:T(8,128)} %slice_convert_fusion) | copy-start | bytes 196612
  127.0 39.4 %copy-start.5 = (bf16[384,512]{1,0:T(8,128)(2,1)S(1)}, bf16[384,512]{1,0:T(8,128)(2,1)}, u32[]{:S(2)}) copy-start(bf16[384,512]{1,0:T(8,128)(2,1)} %copy-done.4) | copy-start | bytes 1179652
  127.0 39.4 %copy-start.7 = (bf16[288,512]{1,0:T(8,128)(2,1)S(1)}, bf16[288,512]{1,0:T(8,128)(2,1)}, u32[]{:S(2)}) copy-start(bf16[288,512]{1,0:T(8,128)(2,1)} %param.8) | copy-start | bytes 884740
  129.9 10.2 %collective-permute-start.10 = (f16[40,1024]{1,0:T(8,128)(2,1)S(1)}, f16[40,1024]{1,0:T(8,128)(2,1)S(1)}, u32[]{:S(2)}, u32[]{:S(2)}) collective-permute-start(f16[40,1024]{1,0:T(8,128)(2,1)S(1)} %concatenate.58), channel_id=1, source_target_pairs={{0,4},{4,0},{1,5},{5,1},{2,6},{6,2},{3,7},{7,3},{8,12},{12,8},{9,1... | collective-permute-start | bytes 245768 | tf_op jit(solution)/shard_map/ppermute | solution.py:37
  141.5 24.9 %all-to-all-start.2 = ((bf16[8,32,1024]{2,1,0:T(8,128)(2,1)}), bf16[8,32,1024]{2,1,0:T(8,128)(2,1)S(1)}, u32[]{:S(2)}, u32[]{:S(2)}) async-start(bf16[8,32,1024]{2,1,0:T(8,128)(2,1)} %broadcast_in_dim.147), calls=%async_computation.2 | async-start | bytes 1048576 | tf_op jit(solution)/shard_map/all_to_all | solution.py:167
  151.1 25.3 %copy-start.3 = (bf16[2,128,384]{2,1,0:T(8,128)(2,1)S(1)}, bf16[2,128,384]{2,1,0:T(8,128)(2,1)}, u32[]{:S(2)}) copy-start(bf16[2,128,384]{2,1,0:T(8,128)(2,1)} %copy-done.2) | copy-start | bytes 589828
  168.9 17.1 %all-to-all-start.3 = ((f16[32,8,384]{2,1,0:T(8,128)(2,1)}), f16[32,8,384]{2,1,0:T(8,128)(2,1)S(1)}, u32[]{:S(2)}, u32[]{:S(2)}) async-start(f16[32,8,384]{2,1,0:T(8,128)(2,1)} %bitcast.33), calls=%async_computation.3 | async-start | bytes 393216 | tf_op jit(solution)/shard_map/all_to_all | solution.py:175
  176.9 10.6 %collective-permute-start.11 = (f32[296,512]{1,0:T(8,128)S(1)}, f32[296,512]{1,0:T(8,128)}, u32[]{:S(2)}, u32[]{:S(2)}) collective-permute-start(f32[296,512]{1,0:T(8,128)S(1)} %slice.243), channel_id=1, source_target_pairs={{0,8},{8,0},{1,9},{9,1},{2,10},{10,2},{3,11},{11,3},{4,12},{12,4},... | collective-permute-start | bytes 1818632 | tf_op jit(solution)/shard_map/ppermute | solution.py:37

commit v3 on v2

--- a/solution.py
+++ b/solution.py
@@ -39,7 +39,7 @@
 
 def local(inputs, w_enc, b_enc, masks, w_dec, errors, target_of):
     f32, bf16, f16 = jnp.float32, jnp.bfloat16, jnp.float16
-    yl, z, core = (lax.axis_index(a) for a in LAT)
+    yl, core = lax.axis_index("yl"), lax.axis_index("c")
     yh, x = lax.axis_index("yh"), lax.axis_index("x")
     place = x * YH + yh
     source = yl * S // YL
@@ -53,21 +53,14 @@
     dims = (((1,), (1,)), ((), ()))
     rows_dims = (((0,), (0,)), ((), ()))
 
+    top_err = jnp.max(jnp.abs(errors[0].astype(f32))) * 1.01
+    top_lanes = jnp.broadcast_to(top_err.astype(bf16), (rows, pad))
+    held = [jnp.concatenate([inputs[:, s], top_lanes], axis=1)[None] for s in range(S)]
+    held = jnp.concatenate([jnp.broadcast_to(h, (PEERS // S, rows, LANES)) for h in held], axis=0)
+    held = lax.all_to_all(held, PLANE, 0, 0, tiled=True)
     errs = lax.all_to_all(
         jnp.broadcast_to(errors, (PEERS, rows, depth)), PLANE, 0, 0, tiled=True
     ).reshape(wide, depth)
-
-    top_err = jnp.max(jnp.abs(errors[0].astype(f32))) * 1.01
-    top_lanes = jnp.broadcast_to(top_err.astype(bf16), (rows, S, pad))
-    held = jnp.transpose(jnp.concatenate([inputs, top_lanes], axis=2), (1, 0, 2))
-    mine = lax.dynamic_index_in_dim(held, source, 0, keepdims=True)
-    theirs = swap(lax.dynamic_index_in_dim(held, 1 - source, 0, keepdims=True), "yl", YL, 2)
-    low = source == 0
-    held = jnp.concatenate([jnp.where(low, mine, theirs), jnp.where(low, theirs, mine)], axis=0)
-    for axis, size, at, distance in (("z", Z, z, 1), ("z", Z, z, 2), ("z", Z, z, 4), ("yl", YL, yl, 1)):
-        theirs = swap(held, axis, size, distance)
-        low = (at & distance) == 0
-        held = jnp.concatenate([jnp.where(low, held, theirs), jnp.where(low, theirs, held)], axis=1)
     own = held.reshape(wide, LANES)
     top_err = jnp.max(own[:, feats : feats + 1].astype(f32))
     lane = lax.broadcasted_iota(jnp.int32, (wide, LANES), 1)

time: 192 us -> 164 us (0.85)
  starting transfers between devices: 84 us -> 55.2 us
  waiting for transfers between devices: 53.3 us -> 27.4 us
  blocking collectives: 0 us -> 24.3 us
    ppermute x12 -> x7, waiting for transfers between devices: 30.9 us -> 3.37 us  [swap(): return lax.ppermute(value, axis, [(i, i ^ distance) for i in range(size)])]
    all_to_all x0 -> x1, blocking collectives: none -> 24.3 us  [local(): held = lax.all_to_all(held, PLANE, 0, 0, tiled=True)]
    ppermute x12 -> x7, starting transfers between devices: 45.7 us -> 23.5 us  [swap(): return lax.ppermute(value, axis, [(i, i ^ distance) for i in range(size)])]
    all_to_all x1, starting transfers between devices: 14 us -> 5.46 us  [local(): lax.all_to_all(jnp.broadcast_to(errors, (PEERS, rows, depth)), PLANE, 0,...]
    all_to_all x1, starting transfers between devices: 7.48 us -> 9.8 us  [local(): lax.all_to_all(sent.reshape(PEERS, rows, LANES), PLANE, 0, 0, tiled=True)]
  transfers between devices with their start and end apart: 16 -> 11, of which waited for: 7 -> 3; matrix products, arithmetic and copies ran while one was open for 21% -> 26% of each run, Pallas kernels for 0% -> 0%
where the time goes in v3:
time: 164 us; the launch traced here: 163 us
  starting transfers between devices  55.2 us (34%)
  waiting for transfers between devices  27.4 us (17%)
  blocking collectives  24.3 us (15%)
  other arithmetic  21.9 us (13%)
  local copies, waits for them, and re-layouts  17.7 us (11%)
  matrix products  8.06 us (5%)
  between operations  7.85 us (5%)
    all_to_all x1, blocking collectives, local(): held = lax.all_to_all(held, PLANE, 0, 0, tiled=True)  24.3 us
    ppermute x7, starting transfers between devices, swap(): return lax.ppermute(value, axis, [(i, i ^ distance) for i in range(size)])  23.5 us
    all_to_all x1, waiting for transfers between devices, local(): lax.all_to_all(jnp.broadcast_to(grad[None], (SLOTS, chunk, both_lats)), S...  16.9 us
    all_to_all x1, starting transfers between devices, local(): lax.all_to_all(sent.reshape(PEERS, rows, LANES), PLANE, 0, 0, tiled=True)  9.8 us
    all_to_all x1, starting transfers between devices, local(): lax.all_to_all(jnp.broadcast_to(grad[None], (SLOTS, chunk, both_lats)), S...  9.47 us
    all_to_all x1, waiting for transfers between devices, local(): lax.all_to_all(sent.reshape(PEERS, rows, LANES), PLANE, 0, 0, tiled=True)  7.19 us
    all_to_all x1, starting transfers between devices, local(): terms = lax.all_to_all(term, SUMS, 0, 0, tiled=True)  6.99 us
    all_to_all x1, starting transfers between devices, local(): lax.all_to_all(jnp.broadcast_to(errors, (PEERS, rows, depth)), PLANE, 0,...  5.46 us
  transfers between devices with their start and end apart: 11, of which 3 were waited for; matrix products, arithmetic and copies ran while one was open for 26% of the time, Pallas kernels for 0%

profile of v3, /device:TPU:8, one launch (start us, length us, event | category | flops | bytes accessed | tf_op | source)
XLA Modules:
  0.0 162.5 jit_solution(18080508705202479225)
XLA Ops:
  0.6 1.9 %collective-permute-start.1 = (bf16[512,2304]{1,0:T(8,128)(2,1)}, bf16[512,2304]{1,0:T(8,128)(2,1)}, u32[]{:S(2)}, u32[]{:S(2)}) collective-permute-start(bf16[512,2304]{1,0:T(8,128)(2,1)} %bitcast.74), channel_id=1, source_target_pairs={{0,8},{8,0},{1,9},{9,1},{2,10},{10,2},{3,11},{11,3},{4,12},{12,4},... | collective-permute-start | bytes 7077896 | tf_op jit(solution)/shard_map/ppermute | solution.py:37
  2.6 0.8 fusion.80
  3.4 1.4 abs_reduce_fusion.1
  5.5 24.3 %all_to_all.25 = bf16[32,8,384]{2,1,0:T(8,128)(2,1)} all-to-all(bf16[32,8,384]{2,1,0:T(8,128)(2,1)S(1)} %pad_maximum_fusion.6), channel_id=1, replica_groups=mesh['yl'=4,'z'=8,'c'=2,'yh'=2,'x'=4] {'yl','z'}, dimensions={0} | all-to-all | bytes 393216 | tf_op jit(solution)/shard_map/all_to_all | solution.py:60
  29.9 1.9 %broadcast_in_dim.138 = bf16[32,8,2304]{2,1,0:T(8,128)(2,1)} broadcast(bf16[8,2304]{1,0:T(8,128)(2,1)} %bitcast.86), dimensions={1,2} | broadcast | bytes 1216512 | tf_op jit(solution)/shard_map/broadcast_in_dim | solution.py:62
  31.8 5.5 %all-to-all-start.1 = ((bf16[32,8,2304]{2,1,0:T(8,128)(2,1)}), bf16[32,8,2304]{2,1,0:T(8,128)(2,1)S(1)}, u32[]{:S(2)}, u32[]{:S(2)}) async-start(bf16[32,8,2304]{2,1,0:T(8,128)(2,1)} %broadcast_in_dim.138), calls=%async_computation.1 | async-start | bytes 2359296 | tf_op jit(solution)/shard_map/all_to_all | solution.py:61
  37.3 1.5 convert_bitcast_fusion
  38.9 4.5 %concatenate.39 = bf16[432,512]{1,0:T(8,128)(2,1)} concatenate(bf16[288,512]{1,0:T(8,128)(2,1)S(1)} %copy-done.5, bf16[96,512]{1,0:T(8,128)(2,1)S(1)} %broadcast_in_dim.136, bf16[32,512]{1,0:T(8,128)(2,1)S(1)} %get-tuple-element.13, bf16[1,512]{1,0:T(2,128)(2,1)S(1)} %stack.18, bf16[1,512]{1,0:T(2,128)(2,1)S(1)} %stack.19, bf16[1,512]{1,0:T(2,128)(2,1)S(1)} %stack.20, ...), dimensions={0} | concatenate | bytes 884736 | tf_op jit(solution)/shard_map/concatenate | solution.py:74
  43.4 2.0 %collective-permute-start = (bf16[432,512]{1,0:T(8,128)(2,1)}, bf16[432,512]{1,0:T(8,128)(2,1)}, u32[]{:S(2)}, u32[]{:S(2)}) collective-permute-start(bf16[432,512]{1,0:T(8,128)(2,1)} %concatenate.39), channel_id=1, source_target_pairs={{0,8},{8,0},{1,9},{9,1},{2,10},{10,2},{3,11},{11,3},{4,12},{12,4},... | collective-permute-start | bytes 1327112 | tf_op jit(solution)/shard_map/ppermute | solution.py:37
  45.5 0.6 fusion.64
  46.8 0.6 iota_compare_fusion.3
  48.0 1.5 slice_reduce_fusion
  49.5 1.0 slice.216
  50.6 0.7 slice_convert_fusion.1
  51.9 1.4 slice_convert_fusion
  53.3 2.3 %fusion.5 = f16[256,1024]{1,0:T(8,128)(2,1)} fusion(bf16[288,512]{1,0:T(8,128)(2,1)} %param.8, bf16[384,512]{1,0:T(8,128)(2,1)S(1)} %slice.216, bf16[32,8,384]{2,1,0:T(8,128)(2,1)} %all_to_all.25), kind=kOutput, calls=%fused_computation.9 | convolution fusion | flops 204210176 | bytes 1409024 | tf_op jit(solution)/shard_map/dot_general | solution.py:113
  55.6 2.7 %fusion = f32[1024]{0:T(1024)S(1)} fusion(bf16[512,2304]{1,0:T(8,128)(2,1)} %collective-permute-done.1, bf16[512,2304]{1,0:T(8,128)(2,1)S(1)} %bitcast.75), kind=kLoop, calls=%fused_computation.1 | loop fusion | flops 14154752 | bytes 4722688 | tf_op jit(solution)/shard_map/cd,cd->c/dot_general | solution.py:96
  58.2 0.6 multiply_reduce_fusion.1
  60.9 0.6 broadcast_in_dim.141
  61.5 0.6 broadcast_in_dim.142
  62.1 0.6 broadcast_in_dim.143
  62.7 0.6 broadcast_in_dim.144
  63.3 0.6 broadcast_in_dim.145
  63.9 0.8 concatenate.44
  64.7 2.3 %fusion.77 = (f32[72,1024]{1,0:T(8,128)}, f16[72,1024]{1,0:T(8,128)(2,1)}, f16[72,1024]{1,0:T(8,128)(2,1)}, f16[72,1024]{1,0:T(8,128)(2,1)}, f32[1,72,1024]{2,1,0:T(8,128)}) fusion(s32[]{:T(128)S(6)} %select_n.89, f16[4,8,1024]{2,1,0:T(8,128)(2,1)S(1)} %broadcast_in_dim.146, f16[4,64,1024]{2,1,0:T(8,128)(2,1)} %bitcast.85, s32[]{:T(128)S(6)} %select_n.91, ...), kind=kLoop, calls=%fused_computation.139 | loop fusion | flops 516096 | bytes 1622032 | tf_op jit(solution)/shard_map/convert_element_type | solution.py:125
  67.0 4.6 %collective-permute-start.4 = (f16[72,1024]{1,0:T(8,128)(2,1)}, f16[72,1024]{1,0:T(8,128)(2,1)}, u32[]{:S(2)}, u32[]{:S(2)}) collective-permute-start(f16[72,1024]{1,0:T(8,128)(2,1)} %get-tuple-element.17), channel_id=1, source_target_pairs={{0,3},{1,2},{2,1},{3,0},{4,7},{5,6},{6,5},{7,4},{8,11},{9,10},{10,... | collective-permute-start | bytes 442376 | tf_op jit(solution)/shard_map/ppermute | solution.py:37
  71.6 2.7 %collective-permute-start.3 = (f16[72,1024]{1,0:T(8,128)(2,1)}, f16[72,1024]{1,0:T(8,128)(2,1)}, u32[]{:S(2)}, u32[]{:S(2)}) collective-permute-start(f16[72,1024]{1,0:T(8,128)(2,1)} %get-tuple-element.16), channel_id=1, source_target_pairs={{0,2},{1,3},{2,0},{3,1},{4,6},{5,7},{6,4},{7,5},{8,10},{9,11},{10,... | collective-permute-start | bytes 442376 | tf_op jit(solution)/shard_map/ppermute | solution.py:37
  74.3 2.4 %collective-permute-start.2 = (f16[72,1024]{1,0:T(8,128)(2,1)}, f16[72,1024]{1,0:T(8,128)(2,1)}, u32[]{:S(2)}, u32[]{:S(2)}) collective-permute-start(f16[72,1024]{1,0:T(8,128)(2,1)} %get-tuple-element.15), channel_id=1, source_target_pairs={{0,1},{1,0},{2,3},{3,2},{4,5},{5,4},{6,7},{7,6},{8,9},{9,8},{10,11... | collective-permute-start | bytes 442376 | tf_op jit(solution)/shard_map/ppermute | solution.py:37
  76.8 3.9 %fusion.4 = f16[1024,256]{0,1:T(8,128)(2,1)} fusion(bf16[512,2304]{1,0:T(8,128)(2,1)} %collective-permute-done.1, bf16[512,2304]{1,0:T(8,128)(2,1)S(1)} %bitcast.76, bf16[32,8,2304]{2,1,0:T(8,128)(2,1)S(1)} %all-to-all-done.1, f32[]{:T(128)S(6)} %mul.134), kind=kOutput, calls=%fused_computation.8 | convolution fusion | flops 1217921024 | bytes 6422532 | tf_op jit(solution)/shard_map/dot_general | solution.py:154
  80.7 7.0 %all-to-all-start.2 = ((f16[8,32,1024]{2,1,0:T(8,128)(2,1)}), f16[8,32,1024]{2,1,0:T(8,128)(2,1)S(1)}, u32[]{:S(2)}, u32[]{:S(2)}) async-start(f16[8,32,1024]{2,1,0:T(8,128)(2,1)} %bitcast.84), calls=%async_computation.2 | async-start | bytes 1048576 | tf_op jit(solution)/shard_map/all_to_all | solution.py:156
  87.7 1.2 slice.237
  89.0 0.8 slice.217
  90.4 0.9 convert_element_type.150
  91.9 0.9 convert_element_type.151
  93.3 0.9 convert_element_type.152
  97.0 7.8 %collective-permute-start.5 = (f16[40,1024]{1,0:T(8,128)(2,1)S(1)}, f16[40,1024]{1,0:T(8,128)(2,1)S(1)}, u32[]{:S(2)}, u32[]{:S(2)}) collective-permute-start(f16[40,1024]{1,0:T(8,128)(2,1)S(1)} %concatenate.46), channel_id=1, source_target_pairs={{0,4},{4,0},{1,5},{5,1},{2,6},{6,2},{3,7},{7,3},{8,12},{12,8},{9,1... | collective-permute-start | bytes 245768 | tf_op jit(solution)/shard_map/ppermute | solution.py:37
  104.9 3.4 %collective-permute-done.5 = f16[40,1024]{1,0:T(8,128)(2,1)S(1)} collective-permute-done((f16[40,1024]{1,0:T(8,128)(2,1)S(1)}, f16[40,1024]{1,0:T(8,128)(2,1)S(1)}, u32[]{:S(2)}, u32[]{:S(2)}) %collective-permute-start.5) | collective-permute-done | bytes 81952 | tf_op jit(solution)/shard_map/ppermute | solution.py:37
  108.7 0.9 broadcast_in_dim.161
  109.5 9.5 %all-to-all-start.3 = ((bf16[8,32,1024]{2,1,0:T(8,128)(2,1)}), bf16[8,32,1024]{2,1,0:T(8,128)(2,1)S(1)}, u32[]{:S(2)}, u32[]{:S(2)}) async-start(bf16[8,32,1024]{2,1,0:T(8,128)(2,1)} %broadcast_in_dim.161), calls=%async_computation.3 | async-start | bytes 1048576 | tf_op jit(solution)/shard_map/all_to_all | solution.py:160
  119.0 16.9 %all-to-all-done.3 = bf16[8,32,1024]{2,1,0:T(8,128)(2,1)S(1)} async-done(((bf16[8,32,1024]{2,1,0:T(8,128)(2,1)}), bf16[8,32,1024]{2,1,0:T(8,128)(2,1)S(1)}, u32[]{:S(2)}, u32[]{:S(2)}) %all-to-all-start.3) | async-done | bytes 524320 | tf_op jit(solution)/shard_map/all_to_all | solution.py:160
  135.9 1.1 abs_reduce_fusion
  137.7 0.7 select_convert_fusion
  138.4 9.8 %all-to-all-start.4 = ((f16[32,8,384]{2,1,0:T(8,128)(2,1)}), f16[32,8,384]{2,1,0:T(8,128)(2,1)S(1)}, u32[]{:S(2)}, u32[]{:S(2)}) async-start(f16[32,8,384]{2,1,0:T(8,128)(2,1)} %bitcast.33), calls=%async_computation.4 | async-start | bytes 393216 | tf_op jit(solution)/shard_map/all_to_all | solution.py:168
  148.7 1.9 %collective-permute-start.6 = (f32[296,512]{1,0:T(8,128)S(1)}, f32[296,512]{1,0:T(8,128)}, u32[]{:S(2)}, u32[]{:S(2)}) collective-permute-start(f32[296,512]{1,0:T(8,128)S(1)} %slice.251), channel_id=1, source_target_pairs={{0,8},{8,0},{1,9},{9,1},{2,10},{10,2},{3,11},{11,3},{4,12},{12,4},... | collective-permute-start | bytes 1818632 | tf_op jit(solution)/shard_map/ppermute | solution.py:37
  150.6 7.2 %all-to-all-done.4 = f16[32,8,384]{2,1,0:T(8,128)(2,1)S(1)} async-done(((f16[32,8,384]{2,1,0:T(8,128)(2,1)}), f16[32,8,384]{2,1,0:T(8,128)(2,1)S(1)}, u32[]{:S(2)}, u32[]{:S(2)}) %all-to-all-start.4) | async-done | bytes 196640 | tf_op jit(solution)/shard_map/all_to_all | solution.py:168
  158.6 0.6 copy.21
  159.3 2.0 %slice_add_fusion = f32[288,512]{1,0:T(8,128)} fusion(f32[296,512]{1,0:T(8,128)} %collective-permute-done.6, f32[384,1024]{1,0:T(8,128)S(1)} %fusion.16), kind=kLoop, calls=%fused_computation.21 | loop fusion | flops 147456 | bytes 1769472 | tf_op jit(solution)/shard_map/add | solution.py:173
  161.2 1.3 slice_add_fusion.15
  (86 shorter events, 4.9 us)
Async XLA Ops:
  0.6 36.6 %copy-start.9 = (f32[512]{0:T(512)S(1)}, f32[512]{0:T(512)}, u32[]{:S(2)}) copy-start(f32[512]{0:T(512)} %param.9) | copy-start | bytes 6148
  0.6 54.9 %collective-permute-start.1 = (bf16[512,2304]{1,0:T(8,128)(2,1)}, bf16[512,2304]{1,0:T(8,128)(2,1)}, u32[]{:S(2)}, u32[]{:S(2)}) collective-permute-start(bf16[512,2304]{1,0:T(8,128)(2,1)} %bitcast.74), channel_id=1, source_target_pairs={{0,8},{8,0},{1,9},{9,1},{2,10},{10,2},{3,11},{11,3},{4,12},{12,4},... | collective-permute-start | bytes 7077896 | tf_op jit(solution)/shard_map/ppermute | solution.py:37
  5.5 33.4 %copy-start.5 = (bf16[288,512]{1,0:T(8,128)(2,1)S(1)}, bf16[288,512]{1,0:T(8,128)(2,1)}, u32[]{:S(2)}) copy-start(bf16[288,512]{1,0:T(8,128)(2,1)} %param.8) | copy-start | bytes 884740
  29.9 15.6 %copy-start.16 = (s32[8]{0:T(128)S(1)}, s32[8]{0:T(128)}, u32[]{:S(2)}) copy-start(s32[8]{0:T(128)} %param.13) | copy-start | bytes 100
  31.8 45.0 %all-to-all-start.1 = ((bf16[32,8,2304]{2,1,0:T(8,128)(2,1)}), bf16[32,8,2304]{2,1,0:T(8,128)(2,1)S(1)}, u32[]{:S(2)}, u32[]{:S(2)}) async-start(bf16[32,8,2304]{2,1,0:T(8,128)(2,1)} %broadcast_in_dim.138), calls=%async_computation.1 | async-start | bytes 2359296 | tf_op jit(solution)/shard_map/all_to_all | solution.py:61
  43.4 12.1 %copy-start = (bf16[1,512,2304]{2,1,0:T(8,128)(2,1)S(1)}, bf16[1,512,2304]{2,1,0:T(8,128)(2,1)}, u32[]{:S(2)}) copy-start(bf16[1,512,2304]{2,1,0:T(8,128)(2,1)} %param.11) | copy-start | bytes 7077892
  43.4 6.1 %collective-permute-start = (bf16[432,512]{1,0:T(8,128)(2,1)}, bf16[432,512]{1,0:T(8,128)(2,1)}, u32[]{:S(2)}, u32[]{:S(2)}) collective-permute-start(bf16[432,512]{1,0:T(8,128)(2,1)} %concatenate.39), channel_id=1, source_target_pairs={{0,8},{8,0},{1,9},{9,1},{2,10},{10,2},{3,11},{11,3},{4,12},{12,4},... | collective-permute-start | bytes 1327112 | tf_op jit(solution)/shard_map/ppermute | solution.py:37
  50.6 2.7 %copy-start.3 = (bf16[384,512]{1,0:T(8,128)(2,1)}, bf16[384,512]{1,0:T(8,128)(2,1)S(1)}, u32[]{:S(2)}) copy-start(bf16[384,512]{1,0:T(8,128)(2,1)S(1)} %slice.216) | copy-start | bytes 1179652
  67.0 26.3 %collective-permute-start.4 = (f16[72,1024]{1,0:T(8,128)(2,1)}, f16[72,1024]{1,0:T(8,128)(2,1)}, u32[]{:S(2)}, u32[]{:S(2)}) collective-permute-start(f16[72,1024]{1,0:T(8,128)(2,1)} %get-tuple-element.17), channel_id=1, source_target_pairs={{0,3},{1,2},{2,1},{3,0},{4,7},{5,6},{6,5},{7,4},{8,11},{9,10},{10,... | collective-permute-start | bytes 442376 | tf_op jit(solution)/shard_map/ppermute | solution.py:37
  71.6 20.2 %collective-permute-start.3 = (f16[72,1024]{1,0:T(8,128)(2,1)}, f16[72,1024]{1,0:T(8,128)(2,1)}, u32[]{:S(2)}, u32[]{:S(2)}) collective-permute-start(f16[72,1024]{1,0:T(8,128)(2,1)} %get-tuple-element.16), channel_id=1, source_target_pairs={{0,2},{1,3},{2,0},{3,1},{4,6},{5,7},{6,4},{7,5},{8,10},{9,11},{10,... | collective-permute-start | bytes 442376 | tf_op jit(solution)/shard_map/ppermute | solution.py:37
  74.3 16.1 %collective-permute-start.2 = (f16[72,1024]{1,0:T(8,128)(2,1)}, f16[72,1024]{1,0:T(8,128)(2,1)}, u32[]{:S(2)}, u32[]{:S(2)}) collective-permute-start(f16[72,1024]{1,0:T(8,128)(2,1)} %get-tuple-element.15), channel_id=1, source_target_pairs={{0,1},{1,0},{2,3},{3,2},{4,5},{5,4},{6,7},{7,6},{8,9},{9,8},{10,11... | collective-permute-start | bytes 442376 | tf_op jit(solution)/shard_map/ppermute | solution.py:37
  80.7 13.5 %copy-start.1 = (f32[1,72,1024]{2,1,0:T(8,128)S(1)}, f32[1,72,1024]{2,1,0:T(8,128)}, u32[]{:S(2)}) copy-start(f32[1,72,1024]{2,1,0:T(8,128)} %get-tuple-element.18) | copy-start | bytes 884740
  80.7 16.1 %copy-start.12 = (pred[4]{0:T(512)(128)(4,1)S(1)}, pred[4]{0:T(512)(128)(4,1)}, u32[]{:S(2)}) copy-start(pred[4]{0:T(512)(128)(4,1)} %get-tuple-element.35) | copy-start | bytes 16
  80.7 16.1 %copy-start.13 = (pred[4]{0:T(512)(128)(4,1)S(1)}, pred[4]{0:T(512)(128)(4,1)}, u32[]{:S(2)}) copy-start(pred[4]{0:T(512)(128)(4,1)} %get-tuple-element.36) | copy-start | bytes 16
  80.7 16.1 %copy-start.14 = (pred[4]{0:T(512)(128)(4,1)S(1)}, pred[4]{0:T(512)(128)(4,1)}, u32[]{:S(2)}) copy-start(pred[4]{0:T(512)(128)(4,1)} %get-tuple-element.37) | copy-start | bytes 16
  80.7 16.1 %copy-start.15 = (pred[4]{0:T(512)(128)(4,1)S(1)}, pred[4]{0:T(512)(128)(4,1)}, u32[]{:S(2)}) copy-start(pred[4]{0:T(512)(128)(4,1)} %get-tuple-element.38) | copy-start | bytes 16
  80.7 24.1 %copy-start.10 = (f32[512]{0:T(512)S(1)}, f32[512]{0:T(512)}, u32[]{:S(2)}) copy-start(f32[512]{0:T(512)} %param.9) | copy-start | bytes 6148
  80.7 24.1 %copy-start.11 = (f32[1,512]{1,0:T(1,128)S(1)}, f32[1,512]{1,0:T(1,128)}, u32[]{:S(2)}) copy-start(f32[1,512]{1,0:T(1,128)} %slice_add_fusion.16) | copy-start | bytes 6148
  80.7 27.7 %all-to-all-start.2 = ((f16[8,32,1024]{2,1,0:T(8,128)(2,1)}), f16[8,32,1024]{2,1,0:T(8,128)(2,1)S(1)}, u32[]{:S(2)}, u32[]{:S(2)}) async-start(f16[8,32,1024]{2,1,0:T(8,128)(2,1)} %bitcast.84), calls=%async_computation.2 | async-start | bytes 1048576 | tf_op jit(solution)/shard_map/all_to_all | solution.py:156
  87.7 20.9 %copy-start.7 = (f32[32,512]{1,0:T(8,128)S(1)}, f32[32,512]{1,0:T(8,128)}, u32[]{:S(2)}) copy-start(f32[32,512]{1,0:T(8,128)} %get-tuple-element.12) | copy-start | bytes 196612
  87.7 20.9 %copy-start.8 = (f32[32,512]{1,0:T(8,128)S(1)}, f32[32,512]{1,0:T(8,128)}, u32[]{:S(2)}) copy-start(f32[32,512]{1,0:T(8,128)} %slice_convert_fusion) | copy-start | bytes 196612
  94.2 41.6 %copy-start.4 = (bf16[384,512]{1,0:T(8,128)(2,1)S(1)}, bf16[384,512]{1,0:T(8,128)(2,1)}, u32[]{:S(2)}) copy-start(bf16[384,512]{1,0:T(8,128)(2,1)} %copy-done.3) | copy-start | bytes 1179652
  94.3 41.6 %copy-start.6 = (bf16[288,512]{1,0:T(8,128)(2,1)S(1)}, bf16[288,512]{1,0:T(8,128)(2,1)}, u32[]{:S(2)}) copy-start(bf16[288,512]{1,0:T(8,128)(2,1)} %param.8) | copy-start | bytes 884740
  97.0 11.2 %collective-permute-start.5 = (f16[40,1024]{1,0:T(8,128)(2,1)S(1)}, f16[40,1024]{1,0:T(8,128)(2,1)S(1)}, u32[]{:S(2)}, u32[]{:S(2)}) collective-permute-start(f16[40,1024]{1,0:T(8,128)(2,1)S(1)} %concatenate.46), channel_id=1, source_target_pairs={{0,4},{4,0},{1,5},{5,1},{2,6},{6,2},{3,7},{7,3},{8,12},{12,8},{9,1... | collective-permute-start | bytes 245768 | tf_op jit(solution)/shard_map/ppermute | solution.py:37
  109.5 26.3 %all-to-all-start.3 = ((bf16[8,32,1024]{2,1,0:T(8,128)(2,1)}), bf16[8,32,1024]{2,1,0:T(8,128)(2,1)S(1)}, u32[]{:S(2)}, u32[]{:S(2)}) async-start(bf16[8,32,1024]{2,1,0:T(8,128)(2,1)} %broadcast_in_dim.161), calls=%async_computation.3 | async-start | bytes 1048576 | tf_op jit(solution)/shard_map/all_to_all | solution.py:160
  119.0 29.2 %copy-start.2 = (bf16[32,8,384]{2,1,0:T(8,128)(2,1)S(1)}, bf16[32,8,384]{2,1,0:T(8,128)(2,1)}, u32[]{:S(2)}) copy-start(bf16[32,8,384]{2,1,0:T(8,128)(2,1)} %all_to_all.25) | copy-start | bytes 589828
  138.4 19.4 %all-to-all-start.4 = ((f16[32,8,384]{2,1,0:T(8,128)(2,1)}), f16[32,8,384]{2,1,0:T(8,128)(2,1)S(1)}, u32[]{:S(2)}, u32[]{:S(2)}) async-start(f16[32,8,384]{2,1,0:T(8,128)(2,1)} %bitcast.33), calls=%async_computation.4 | async-start | bytes 393216 | tf_op jit(solution)/shard_map/all_to_all | solution.py:168
  148.7 10.6 %collective-permute-start.6 = (f32[296,512]{1,0:T(8,128)S(1)}, f32[296,512]{1,0:T(8,128)}, u32[]{:S(2)}, u32[]{:S(2)}) collective-permute-start(f32[296,512]{1,0:T(8,128)S(1)} %slice.251), channel_id=1, source_target_pairs={{0,8},{8,0},{1,9},{9,1},{2,10},{10,2},{3,11},{11,3},{4,12},{12,4},... | collective-permute-start | bytes 1818632 | tf_op jit(solution)/shard_map/ppermute | solution.py:37

commit v4 on v3

v4 whole, which is shorter than its diff:
```python
import functools

import jax
import jax.numpy as jnp
from jax import lax
from jax.experimental import pallas as pl
from jax.experimental.pallas import tpu as pltpu
from jax.sharding import Mesh, PartitionSpec as P

S = 2
penalty = 1.0
sharpness = 1.0

YL, Z, C, YH, X = 4, 8, 2, 2, 4
AXES = ("yl", "z", "c", "yh", "x")
LAT = ("yl", "z", "c")
TGT = ("yh", "x")
PLANE = ("yl", "z")
PEERS = YL * Z
SLOTS = YH * X
LANES = 384
EXTRA = 8
PRE_SCALE = 128.0
TOP = 14.0
SWAP = [(0, 1), (1, 0)]
f32, bf16, f16 = jnp.float32, jnp.bfloat16, jnp.float16
BY_LAST = (((1,), (1,)), ((), ()))
BY_FIRST = (((0,), (0,)), ((), ()))
PARAMS = pltpu.CompilerParams(vmem_limit_bytes=40 * 1024 * 1024)


def exponent(bound):
    return jnp.ceil(jnp.log2(jnp.maximum(bound, 1e-30)))


def split_bf16(v):
    hi = v.astype(bf16)
    rest = v - hi.astype(f32)
    mid = rest.astype(bf16)
    low = (rest - mid.astype(f32)).astype(bf16)
    return jnp.stack([hi, mid, low])


def call(body, outs, *args):
    shapes = [jax.ShapeDtypeStruct(*o) for o in outs]
    return pl.pallas_call(body, out_shape=shapes, compiler_params=PARAMS)(*args)


def forward(feats, got, w_own, w_other, enc_both, lines, base, out, ones_out):
    wide = got.shape[0]
    depth = w_own.shape[1]
    lats = w_own.shape[0]
    chunk = wide // SLOTS
    errs = got[:, :depth]
    own = got[:, depth:]
    lane = lax.broadcasted_iota(jnp.int32, own.shape, 1)
    own32 = own.astype(f32)
    ones_out[...] = jnp.where(lane < feats, own32, 1.0).astype(bf16)
    top_err = jnp.max(jnp.where(lane == feats, own32, 0.0), axis=(0, 1), keepdims=True)
    e_term = exponent(base[:, 0:1] * top_err)
    scale = base[:, 1:2] * jnp.exp2(TOP - e_term)
    for h, w in enumerate((w_own, w_other)):
        term = lax.dot_general(errs, w[...], BY_LAST, preferred_element_type=f32) * scale
        out[:, :chunk, h * lats : (h + 1) * lats] = term.reshape(SLOTS, chunk, lats)
    pre = jnp.dot(own, enc_both[...], preferred_element_type=f32) * PRE_SCALE
    out[:, chunk : 2 * chunk, :] = pre.reshape(SLOTS, chunk, C * lats)
    row = lax.broadcasted_iota(jnp.int32, lines.shape, 0)
    extra = jnp.where(row == 3, jnp.broadcast_to(e_term, lines.shape), lines[...])
    for i in range(SLOTS):
        out[i, 2 * chunk :, :] = extra


def middle(back, gates, bias, out):
    chunk = gates.shape[0]
    dact = jnp.zeros(gates.shape, f32)
    pre = jnp.zeros(gates.shape, f32)
    sumsq = jnp.zeros((1, gates.shape[1]), f32)
    at = 2 * chunk
    for i in range(SLOTS):
        dact += back[i, :chunk, :] * jnp.exp2(back[i, at + 3 : at + 4, :] - TOP)
        pre += back[i, chunk:at, :]
        squares = back[i, at : at + 1, :] + back[i, at + 1 : at + 2, :]
        sumsq += squares * jnp.exp2(back[i, at + 2 : at + 3, :] - TOP)
    pre = pre * (1.0 / PRE_SCALE) + bias[...]
    norm = jnp.sqrt(sumsq)
    tanh_val = jnp.tanh(sharpness * (gates[...] * pre) * norm)
    grad = gates[...] * (dact + penalty * sharpness * norm * (1.0 - tanh_val * tanh_val))
    grad = grad.astype(bf16)
    for i in range(SLOTS):
        out[i] = grad


def backward(feats, grad, enc_both, own_ones, sent, keep, away):
    lats = keep.shape[1]
    part = lax.dot_general(grad[...], enc_both[...], BY_LAST, preferred_element_type=f32)
    e_part = exponent(jnp.max(jnp.abs(part), axis=(0, 1), keepdims=True))
    lane = lax.broadcasted_iota(jnp.int32, part.shape, 1)
    sent[...] = jnp.where(lane < feats, part * jnp.exp2(TOP - e_part), jnp.broadcast_to(e_part, part.shape))
    enc = lax.dot_general(own_ones[...], grad[...], BY_FIRST, preferred_element_type=f32)
    keep[...] = enc[: keep.shape[0], :lats]
    away[...] = enc[: away.shape[0], lats:]


def finish(came, keep, far, grad_in, grad_enc, grad_bias):
    rows, _, feats = grad_in.shape
    values = came[:, :feats] * jnp.exp2(came[:, feats : feats + 1] - TOP)
    values = values.reshape(S, PEERS // S, rows, feats)
    for s in range(S):
        grad_in[:, s, :] = jnp.sum(values[s], axis=0)
    both = keep[...] + far[...]
    grad_enc[...] = both[:feats]
    grad_bias[...] = both[feats : feats + 1]


def local(inputs, w_enc, b_enc, masks, w_dec, errors, target_of):
    yl, core = lax.axis_index("yl"), lax.axis_index("c")
    slot = lax.axis_index("yh") * X + lax.axis_index("x")
    source = yl * S // YL
    feats, lats = w_enc.shape
    depth = w_dec.shape[2]
    rows = inputs.shape[0]
    wide = PEERS * rows
    chunk = wide // SLOTS
    both_lats = C * lats
    pad = LANES - feats

    top_err = jnp.max(jnp.abs(errors[0].astype(f32))) * 1.01
    top_lanes = jnp.broadcast_to(top_err.astype(bf16), (rows, pad))
    held = [jnp.concatenate([errors[0], inputs[:, s], top_lanes], axis=1)[None] for s in range(S)]
    held = jnp.concatenate([jnp.broadcast_to(h, (PEERS // S, rows, depth + LANES)) for h in held], axis=0)
    got = lax.all_to_all(held, PLANE, 0, 0, tiled=True).reshape(wide, depth + LANES)

    gates6 = masks.reshape(SLOTS, chunk // rows, C, rows, lats)
    gates5 = lax.dynamic_index_in_dim(gates6, slot, 0, keepdims=False)
    gates_own = lax.dynamic_index_in_dim(gates5, core, 1, keepdims=False).reshape(chunk, lats)
    gates_send = lax.dynamic_index_in_dim(gates5, 1 - core, 1, keepdims=False).reshape(chunk, lats)
    w_own = w_dec[0]
    w_other = lax.ppermute(w_own, "c", SWAP)
    pack = jnp.concatenate(
        [
            w_enc,
            jnp.zeros((pad, lats), bf16),
            gates_send.astype(bf16),
            split_bf16(b_enc),
            jnp.zeros((13, lats), bf16),
        ],
        axis=0,
    )
    pack_other = lax.ppermute(pack, "c", SWAP)
    enc_both = jnp.concatenate([pack[:LANES], pack_other[:LANES]], axis=1)
    gates_other = pack_other[LANES : LANES + chunk].astype(f32)
    gates = jnp.concatenate([gates_own.astype(f32), gates_other], axis=1)
    bias_rows = pack_other[LANES + chunk : LANES + chunk + 3].astype(f32)
    b_both = jnp.concatenate([b_enc, bias_rows[0] + bias_rows[1] + bias_rows[2]])[None]

    slots = jnp.arange(target_of.shape[0], dtype=jnp.int32)
    layer = jnp.sum(jnp.where(slots == slot, target_of, 0))
    flag = (layer >= source).astype(f32)
    square = lambda w: jnp.einsum("cd,cd->c", w, w, preferred_element_type=f32)
    squares = flag * jnp.concatenate([square(w_own), square(w_other)])
    top_sq = jnp.max(squares)
    e_sq = exponent(top_sq)
    scaled = squares * jnp.exp2(TOP - e_sq)
    hi = scaled.astype(f16).astype(f32)
    lines = jnp.concatenate(
        [
            hi[None],
            (scaled - hi)[None],
            jnp.broadcast_to(e_sq, (1, both_lats)),
            jnp.zeros((EXTRA - 3, both_lats), f32),
        ],
        axis=0,
    )
    base = jnp.stack([jnp.sqrt(depth * 1.01 * top_sq), flag])[None]
    lines, base, enc_both, gates, b_both, w_other, got = lax.optimization_barrier(
        (lines, base, enc_both, gates, b_both, w_other, got)
    )

    out, own_ones = call(
        functools.partial(forward, feats),
        [((SLOTS, 2 * chunk + EXTRA, both_lats), f32), ((wide, LANES), bf16)],
        got, w_own, w_other, enc_both, lines, base,
    )
    back = lax.all_to_all(out.astype(f16), TGT, 0, 0, tiled=True).astype(f32)
    (grad,) = call(middle, [((SLOTS, chunk, both_lats), bf16)], back, gates, b_both)
    grad = lax.all_to_all(grad, TGT, 0, 0, tiled=True).reshape(wide, both_lats)
    sent, keep, away = call(
        functools.partial(backward, feats),
        [((wide, LANES), f32), ((feats + 8, lats), f32), ((feats + 8, lats), f32)],
        grad, enc_both, own_ones,
    )
    far = lax.ppermute(away, "c", SWAP)
    came = lax.all_to_all(sent.astype(f16).reshape(PEERS, rows, LANES), PLANE, 0, 0, tiled=True)
    grad_in, grad_enc, grad_bias = call(
        finish,
        [((rows, S, feats), f32), ((feats, lats), f32), ((1, lats), f32)],
        came.astype(f32).reshape(wide, LANES), keep, far,
    )
    return (grad_enc, grad_bias[0], grad_in)


def solution(mesh):
    fine = Mesh(mesh.devices.reshape(YL, Z, C, YH, X), AXES)
    return jax.shard_map(
        local,
        mesh=fine,
        in_specs=(
            P(LAT, None, TGT),
            P(TGT, LAT),
            P(LAT),
            P(None, LAT),
            P(TGT, LAT, None),
            P(TGT, LAT, None),
            P(),
        ),
        out_specs=(P(TGT, LAT), P(LAT), P(LAT, None, TGT)),
        check_vma=False,
    )
```

time: 164 us -> 141 us (0.86)
  the two profiles are of different devices: /device:TPU:8 before, /device:TPU:1 now
where the time goes in v4:
time: 141 us; the launch traced here: 140 us
  blocking collectives  53.1 us (38%)
  starting transfers between devices  32 us (23%)
  waiting for transfers between devices  31.4 us (22%)
  other arithmetic  10.3 us (7%)
  Pallas kernels  5.6 us (4%)
  local copies, waits for them, and re-layouts  3.83 us (3%)
  between operations  3.67 us (3%)
    all_to_all x1, blocking collectives, local(): back = lax.all_to_all(out.astype(f16), TGT, 0, 0, tiled=True).astype(f32)  36.3 us
    all_to_all x1, waiting for transfers between devices, local(): lax.all_to_all(held, PLANE, 0, 0, tiled=True).reshape(wide, depth + LANES)  24.7 us
    all_to_all x1, blocking collectives, local(): grad = lax.all_to_all(grad, TGT, 0, 0, tiled=True).reshape(wide, both_lats)  16.8 us
    all_to_all x1, starting transfers between devices, local(): lax.all_to_all(sent.astype(f16).reshape(PEERS, rows, LANES), PLANE, 0, 0,...  9.53 us
    ppermute x1, starting transfers between devices, local(): w_other = lax.ppermute(w_own, 'c', SWAP)  8.79 us
    all_to_all x1, starting transfers between devices, local(): lax.all_to_all(held, PLANE, 0, 0, tiled=True).reshape(wide, depth + LANES)  8.48 us
    all_to_all x1, waiting for transfers between devices, local(): lax.all_to_all(sent.astype(f16).reshape(PEERS, rows, LANES), PLANE, 0, 0,...  6.7 us
    pallas_call x4, Pallas kernels, call(): return pl.pallas_call(body, out_shape=shapes, compiler_params=PARAMS)(*args)  5.6 us
  transfers between devices with their start and end apart: 5, of which 2 were waited for; matrix products, arithmetic and copies ran while one was open for 9% of the time, Pallas kernels for 0%

profile of v4, /device:TPU:1, one launch (start us, length us, event | category | flops | bytes accessed | tf_op | source)
XLA Modules:
  0.0 139.8 jit_solution(3763261304811566384)
XLA Ops:
  0.6 8.8 %collective-permute-start = (bf16[512,2304]{1,0:T(8,128)(2,1)}, bf16[512,2304]{1,0:T(8,128)(2,1)}, u32[]{:S(2)}, u32[]{:S(2)}) collective-permute-start(bf16[512,2304]{1,0:T(8,128)(2,1)} %bitcast.38), channel_id=1, source_target_pairs={{0,8},{8,0},{1,9},{9,1},{2,10},{10,2},{3,11},{11,3},{4,12},{12,4},... | collective-permute-start | bytes 7077896 | tf_op jit(solution)/shard_map/ppermute | solution.py:138
  9.4 1.4 abs_reduce_fusion
  10.8 0.8 fusion.12
  12.3 0.9 concatenate.58
  13.2 0.9 concatenate.57
  14.1 1.2 pad_maximum_fusion
  15.4 0.0 copy-start.5
  15.4 0.0 copy-start.1
  15.4 0.0 copy-start.6
  15.4 0.0 copy-start
  15.4 8.5 %all-to-all-start = ((bf16[32,8,2688]{2,1,0:T(8,128)(2,1)}), bf16[32,8,2688]{2,1,0:T(8,128)(2,1)}, u32[]{:S(2)}, u32[]{:S(2)}) async-start(bf16[32,8,2688]{2,1,0:T(8,128)(2,1)} %pad_maximum_fusion), calls=%async_computation | async-start | bytes 2752512 | tf_op jit(solution)/shard_map/all_to_all | solution.py:131
  23.9 0.0 copy-done.5
  23.9 1.5 %fusion.4 = (f32[32,512]{1,0:T(8,128)}, bf16[32,512]{1,0:T(8,128)(2,1)S(1)}) fusion(s32[8,4,2,8,512]{4,3,2,1,0:T(8,128)} %bitcast.46, s32[]{:T(128)S(6)} %select_n.29, s32[]{:T(128)S(6)} %select_n.33, s32[]{:T(128)S(6)} %select_n.31), kind=kLoop, calls=%fused_computation.13 | loop fusion | flops 32768 | bytes 229388 | tf_op jit(solution)/shard_map/convert_element_type | solution.py:152
  25.5 0.0 copy-done.1
  25.5 0.3 concatenate.53
  25.8 2.2 %collective-permute-start.1 = (bf16[432,512]{1,0:T(8,128)(2,1)S(1)}, bf16[432,512]{1,0:T(8,128)(2,1)S(1)}, u32[]{:S(2)}, u32[]{:S(2)}) collective-permute-start(bf16[432,512]{1,0:T(8,128)(2,1)S(1)} %concatenate.53), channel_id=1, source_target_pairs={{0,8},{8,0},{1,9},{9,1},{2,10},{10,2},{3,11},{11,3},{4,12},{12,4},... | collective-permute-start | bytes 1327112 | tf_op jit(solution)/shard_map/ppermute | solution.py:149
  28.0 0.0 copy-done.6
  28.0 0.6 fusion.10
  29.3 0.1 pad.14.clone
  29.4 0.0 copy-done
  29.4 0.5 fusion.1
  29.9 0.0 collective-permute-done.1
  29.9 0.0 copy-start.3
  30.0 0.7 copy-done.3
  30.7 0.8 slice_convert_fusion
  31.5 0.0 copy-done.4
  31.5 0.0 copy-done.2
  31.5 0.1 fusion.3.enc_both
  31.6 0.0 collective-permute-done.w_other
  31.6 2.2 %fusion = f32[512]{0:T(512)S(1)} fusion(bf16[512,2304]{1,0:T(8,128)(2,1)} %collective-permute-done.w_other), kind=kLoop, calls=%fused_computation.1 | loop fusion | flops 3538432 | bytes 2361344 | tf_op jit(solution)/shard_map/cd,cd->c/dot_general | solution.py:159
  33.8 0.6 fusion.7
  35.8 0.1 pad.13.clone
  35.9 0.1 maximum_bitcast_fusion.base
  36.0 0.1 maximum_maximum_fusion.lines
  36.1 24.7 %all-to-all-done = bf16[32,8,2688]{2,1,0:T(8,128)(2,1)} async-done(((bf16[32,8,2688]{2,1,0:T(8,128)(2,1)}), bf16[32,8,2688]{2,1,0:T(8,128)(2,1)}, u32[]{:S(2)}, u32[]{:S(2)}) %all-to-all-start) | async-done | bytes 1376288 | tf_op jit(solution)/shard_map/all_to_all | solution.py:131
  60.7 3.8 %shard_map.94 = (f32[8,72,1024]{2,1,0:T(8,128)S(1)}, bf16[256,384]{1,0:T(8,128)(2,1)S(1)}) custom-call(bf16[256,2688]{1,0:T(8,128)(2,1)} %bitcast.14.got, bf16[512,2304]{1,0:T(8,128)(2,1)S(1)} %bitcast.39, bf16[512,2304]{1,0:T(8,128)(2,1)} %collective-permute-done.w_other, bf16[384,1024]{1,0:T(8,128)(2,1)S(1)} %fusion.3.enc_both, ...), custom_call_target="tpu_custom_call" | custom-call | tf_op jit(solution)/shard_map/pallas_call | solution.py:46
  64.5 0.2 convert_element_type.96
  64.7 36.3 %all_to_all.20 = f16[8,72,1024]{2,1,0:T(8,128)(2,1)S(1)} all-to-all(f16[8,72,1024]{2,1,0:T(8,128)(2,1)S(1)} %convert_element_type.96), channel_id=1, replica_groups=mesh['yl'=4,'z'=8,'c'=2,'yh'=2,'x'=4] {'yh','x'}, dimensions={0} | all-to-all | bytes 2359296 | tf_op jit(solution)/shard_map/all_to_all | solution.py:184
  101.0 0.2 convert_element_type.97.back
  101.2 0.2 shard_map.95
  101.4 16.8 %all_to_all.21 = bf16[8,32,1024]{2,1,0:T(8,128)(2,1)S(1)} all-to-all(bf16[8,32,1024]{2,1,0:T(8,128)(2,1)S(1)} %shard_map.95), channel_id=1, replica_groups=mesh['yl'=4,'z'=8,'c'=2,'yh'=2,'x'=4] {'yh','x'}, dimensions={0} | all-to-all | bytes 1048576 | tf_op jit(solution)/shard_map/all_to_all | solution.py:186
  118.3 0.7 shard_map.96
  118.9 0.7 convert_bitcast_fusion
  119.6 9.5 %all-to-all-start.3 = ((f16[32,8,384]{2,1,0:T(8,128)(2,1)}), f16[32,8,384]{2,1,0:T(8,128)(2,1)S(1)}, u32[]{:S(2)}, u32[]{:S(2)}) async-start(f16[32,8,384]{2,1,0:T(8,128)(2,1)} %convert_bitcast_fusion), calls=%async_computation.3 | async-start | bytes 393216 | tf_op jit(solution)/shard_map/all_to_all | solution.py:193
  129.2 3.0 %collective-permute-start.2 = (f32[296,512]{1,0:T(8,128)S(1)}, f32[296,512]{1,0:T(8,128)S(1)}, u32[]{:S(2)}, u32[]{:S(2)}) collective-permute-start(f32[296,512]{1,0:T(8,128)S(1)} %get-tuple-element.29), channel_id=1, source_target_pairs={{0,8},{8,0},{1,9},{9,1},{2,10},{10,2},{3,11},{11,3},{4,12},{12,4},... | collective-permute-start | bytes 1818632 | tf_op jit(solution)/shard_map/ppermute | solution.py:192
  132.1 6.7 %all-to-all-done.3 = f16[32,8,384]{2,1,0:T(8,128)(2,1)S(1)} async-done(((f16[32,8,384]{2,1,0:T(8,128)(2,1)}), f16[32,8,384]{2,1,0:T(8,128)(2,1)S(1)}, u32[]{:S(2)}, u32[]{:S(2)}) %all-to-all-start.3) | async-done | bytes 196640 | tf_op jit(solution)/shard_map/all_to_all | solution.py:193
  138.9 0.0 collective-permute-done.2.far
  138.9 1.0 shard_map.97
  (21 shorter events, 0.2 us)
Async XLA Ops:
  0.6 30.9 %collective-permute-start = (bf16[512,2304]{1,0:T(8,128)(2,1)}, bf16[512,2304]{1,0:T(8,128)(2,1)}, u32[]{:S(2)}, u32[]{:S(2)}) collective-permute-start(bf16[512,2304]{1,0:T(8,128)(2,1)} %bitcast.38), channel_id=1, source_target_pairs={{0,8},{8,0},{1,9},{9,1},{2,10},{10,2},{3,11},{11,3},{4,12},{12,4},... | collective-permute-start | bytes 7077896 | tf_op jit(solution)/shard_map/ppermute | solution.py:138
  15.4 8.5 %copy-start.5 = (f32[512]{0:T(512)S(1)}, f32[512]{0:T(512)}, u32[]{:S(2)}) copy-start(f32[512]{0:T(512)} %param.9) | copy-start | bytes 6148
  15.4 10.1 %copy-start.1 = (bf16[288,512]{1,0:T(8,128)(2,1)S(1)}, bf16[288,512]{1,0:T(8,128)(2,1)}, u32[]{:S(2)}) copy-start(bf16[288,512]{1,0:T(8,128)(2,1)} %param.8) | copy-start | bytes 884740
  15.4 12.6 %copy-start.6 = (s32[8]{0:T(128)S(1)}, s32[8]{0:T(128)}, u32[]{:S(2)}) copy-start(s32[8]{0:T(128)} %param.13) | copy-start | bytes 100
  15.4 14.0 %copy-start = (bf16[1,512,2304]{2,1,0:T(8,128)(2,1)S(1)}, bf16[1,512,2304]{2,1,0:T(8,128)(2,1)}, u32[]{:S(2)}) copy-start(bf16[1,512,2304]{2,1,0:T(8,128)(2,1)} %param.11) | copy-start | bytes 7077892
  15.4 45.4 %all-to-all-start = ((bf16[32,8,2688]{2,1,0:T(8,128)(2,1)}), bf16[32,8,2688]{2,1,0:T(8,128)(2,1)}, u32[]{:S(2)}, u32[]{:S(2)}) async-start(bf16[32,8,2688]{2,1,0:T(8,128)(2,1)} %pad_maximum_fusion), calls=%async_computation | async-start | bytes 2752512 | tf_op jit(solution)/shard_map/all_to_all | solution.py:131
  25.8 4.2 %collective-permute-start.1 = (bf16[432,512]{1,0:T(8,128)(2,1)S(1)}, bf16[432,512]{1,0:T(8,128)(2,1)S(1)}, u32[]{:S(2)}, u32[]{:S(2)}) collective-permute-start(bf16[432,512]{1,0:T(8,128)(2,1)S(1)} %concatenate.53), channel_id=1, source_target_pairs={{0,8},{8,0},{1,9},{9,1},{2,10},{10,2},{3,11},{11,3},{4,12},{12,4},... | collective-permute-start | bytes 1327112 | tf_op jit(solution)/shard_map/ppermute | solution.py:149
  29.4 2.1 %copy-start.4 = (f32[32,512]{1,0:T(8,128)S(1)}, f32[32,512]{1,0:T(8,128)}, u32[]{:S(2)}) copy-start(f32[32,512]{1,0:T(8,128)} %get-tuple-element.35) | copy-start | bytes 196612
  29.4 2.1 %copy-start.2 = (bf16[288,512]{1,0:T(8,128)(2,1)S(1)}, bf16[288,512]{1,0:T(8,128)(2,1)}, u32[]{:S(2)}) copy-start(bf16[288,512]{1,0:T(8,128)(2,1)} %param.8) | copy-start | bytes 884740
  29.9 0.8 copy-start.3
  119.6 19.2 %all-to-all-start.3 = ((f16[32,8,384]{2,1,0:T(8,128)(2,1)}), f16[32,8,384]{2,1,0:T(8,128)(2,1)S(1)}, u32[]{:S(2)}, u32[]{:S(2)}) async-start(f16[32,8,384]{2,1,0:T(8,128)(2,1)} %convert_bitcast_fusion), calls=%async_computation.3 | async-start | bytes 393216 | tf_op jit(solution)/shard_map/all_to_all | solution.py:193
  129.2 9.7 %collective-permute-start.2 = (f32[296,512]{1,0:T(8,128)S(1)}, f32[296,512]{1,0:T(8,128)S(1)}, u32[]{:S(2)}, u32[]{:S(2)}) collective-permute-start(f32[296,512]{1,0:T(8,128)S(1)} %get-tuple-element.29), channel_id=1, source_target_pairs={{0,8},{8,0},{1,9},{9,1},{2,10},{10,2},{3,11},{11,3},{4,12},{12,4},... | collective-permute-start | bytes 1818632 | tf_op jit(solution)/shard_map/ppermute | solution.py:192

commit v5 on v4

--- a/solution.py
+++ b/solution.py
@@ -20,7 +20,7 @@
 SLOTS = YH * X
 LANES = 384
 EXTRA = 8
-PRE_SCALE = 128.0
+PRE_SCALE = 64.0
 TOP = 14.0
 SWAP = [(0, 1), (1, 0)]
 f32, bf16, f16 = jnp.float32, jnp.bfloat16, jnp.float16
@@ -46,11 +46,23 @@
     return pl.pallas_call(body, out_shape=shapes, compiler_params=PARAMS)(*args)
 
 
+def prepare(errors, inputs, out):
+    rows, depth = errors.shape
+    errs = errors[...]
+    top_err = jnp.max(jnp.abs(errs.astype(f32)), axis=(0, 1), keepdims=True) * 1.01
+    pad = jnp.broadcast_to(top_err, (rows, LANES - inputs.shape[2]))
+    for s in range(S):
+        last = jnp.concatenate([inputs[:, s, :].astype(f32), pad], axis=1).astype(bf16)
+        for i in range(PEERS // S):
+            out[s * (PEERS // S) + i, :, :depth] = errs
+            out[s * (PEERS // S) + i, :, depth:] = last
+
+
 def forward(feats, got, w_own, w_other, enc_both, lines, base, out, ones_out):
     wide = got.shape[0]
     depth = w_own.shape[1]
     lats = w_own.shape[0]
-    chunk = wide // SLOTS
+    chunk = wide // X
     errs = got[:, :depth]
     own = got[:, depth:]
     lane = lax.broadcasted_iota(jnp.int32, own.shape, 1)
@@ -61,32 +73,53 @@
     scale = base[:, 1:2] * jnp.exp2(TOP - e_term)
     for h, w in enumerate((w_own, w_other)):
         term = lax.dot_general(errs, w[...], BY_LAST, preferred_element_type=f32) * scale
-        out[:, :chunk, h * lats : (h + 1) * lats] = term.reshape(SLOTS, chunk, lats)
+        out[:, :chunk, h * lats : (h + 1) * lats] = term.reshape(X, chunk, lats)
     pre = jnp.dot(own, enc_both[...], preferred_element_type=f32) * PRE_SCALE
-    out[:, chunk : 2 * chunk, :] = pre.reshape(SLOTS, chunk, C * lats)
+    out[:, chunk : 2 * chunk, :] = pre.reshape(X, chunk, C * lats)
     row = lax.broadcasted_iota(jnp.int32, lines.shape, 0)
     extra = jnp.where(row == 3, jnp.broadcast_to(e_term, lines.shape), lines[...])
-    for i in range(SLOTS):
+    for i in range(X):
         out[i, 2 * chunk :, :] = extra
 
 
-def middle(back, gates, bias, out):
+def along_x(back, out):
+    chunk = (back.shape[1] - EXTRA) // 2
+    at = 2 * chunk
+    line = lambda i, k: back[i, at + k : at + k + 1, :]
+    e_sq, e_term = line(0, 2), line(0, 3)
+    for i in range(1, X):
+        e_sq, e_term = jnp.maximum(e_sq, line(i, 2)), jnp.maximum(e_term, line(i, 3))
+    e_sq, e_term = e_sq + 2.0, e_term + 2.0
+    dact, pre, squares = 0.0, 0.0, 0.0
+    for i in range(X):
+        dact += back[i, :chunk, :] * jnp.exp2(line(i, 3) - e_term)
+        pre += back[i, chunk:at, :]
+        squares += (line(i, 0) + line(i, 1)) * jnp.exp2(line(i, 2) - e_sq)
+    out[:chunk, :] = dact
+    out[chunk:at, :] = pre
+    hi = squares.astype(bf16).astype(f32)
+    out[at : at + 1, :] = hi
+    out[at + 1 : at + 2, :] = squares - hi
+    out[at + 2 : at + 3, :] = e_sq
+    out[at + 3 : at + 4, :] = e_term
+    out[at + 4 :, :] = jnp.zeros((EXTRA - 4, out.shape[1]), f32)
+
+
+def middle(one, two, gates, bias, out):
     chunk = gates.shape[0]
-    dact = jnp.zeros(gates.shape, f32)
-    pre = jnp.zeros(gates.shape, f32)
-    sumsq = jnp.zeros((1, gates.shape[1]), f32)
+    dact, pre, sumsq = 0.0, 0.0, 0.0
     at = 2 * chunk
-    for i in range(SLOTS):
-        dact += back[i, :chunk, :] * jnp.exp2(back[i, at + 3 : at + 4, :] - TOP)
-        pre += back[i, chunk:at, :]
-        squares = back[i, at : at + 1, :] + back[i, at + 1 : at + 2, :]
-        sumsq += squares * jnp.exp2(back[i, at + 2 : at + 3, :] - TOP)
+    for half in (one, two):
+        dact += half[:chunk, :] * jnp.exp2(half[at + 3 : at + 4, :] - TOP)
+        pre += half[chunk:at, :]
+        squares = half[at : at + 1, :] + half[at + 1 : at + 2, :]
+        sumsq += squares * jnp.exp2(half[at + 2 : at + 3, :] - TOP)
     pre = pre * (1.0 / PRE_SCALE) + bias[...]
     norm = jnp.sqrt(sumsq)
     tanh_val = jnp.tanh(sharpness * (gates[...] * pre) * norm)
     grad = gates[...] * (dact + penalty * sharpness * norm * (1.0 - tanh_val * tanh_val))
     grad = grad.astype(bf16)
-    for i in range(SLOTS):
+    for i in range(X):
         out[i] = grad
 
 
@@ -114,27 +147,29 @@
 
 def local(inputs, w_enc, b_enc, masks, w_dec, errors, target_of):
     yl, core = lax.axis_index("yl"), lax.axis_index("c")
-    slot = lax.axis_index("yh") * X + lax.axis_index("x")
+    x = lax.axis_index("x")
+    slot = lax.axis_index("yh") * X + x
     source = yl * S // YL
     feats, lats = w_enc.shape
     depth = w_dec.shape[2]
     rows = inputs.shape[0]
     wide = PEERS * rows
-    chunk = wide // SLOTS
+    chunk = wide // X
     both_lats = C * lats
     pad = LANES - feats
 
-    top_err = jnp.max(jnp.abs(errors[0].astype(f32))) * 1.01
-    top_lanes = jnp.broadcast_to(top_err.astype(bf16), (rows, pad))
-    held = [jnp.concatenate([errors[0], inputs[:, s], top_lanes], axis=1)[None] for s in range(S)]
-    held = jnp.concatenate([jnp.broadcast_to(h, (PEERS // S, rows, depth + LANES)) for h in held], axis=0)
+    held = pl.pallas_call(
+        prepare, out_shape=pltpu.HBM((PEERS, rows, depth + LANES), bf16), compiler_params=PARAMS
+    )(errors[0], inputs)
+    held, masks, w_dec = lax.optimization_barrier((held, masks, w_dec))
     got = lax.all_to_all(held, PLANE, 0, 0, tiled=True).reshape(wide, depth + LANES)
 
-    gates6 = masks.reshape(SLOTS, chunk // rows, C, rows, lats)
-    gates5 = lax.dynamic_index_in_dim(gates6, slot, 0, keepdims=False)
+    gates6 = masks.reshape(X, chunk // rows, C, rows, lats)
+    gates5 = lax.dynamic_index_in_dim(gates6, x, 0, keepdims=False)
     gates_own = lax.dynamic_index_in_dim(gates5, core, 1, keepdims=False).reshape(chunk, lats)
     gates_send = lax.dynamic_index_in_dim(gates5, 1 - core, 1, keepdims=False).reshape(chunk, lats)
     w_own = w_dec[0]
+    square = jnp.einsum("cd,cd->c", w_own, w_own, preferred_element_type=f32)
     w_other = lax.ppermute(w_own, "c", SWAP)
     pack = jnp.concatenate(
         [
@@ -142,7 +177,8 @@
             jnp.zeros((pad, lats), bf16),
             gates_send.astype(bf16),
             split_bf16(b_enc),
-            jnp.zeros((13, lats), bf16),
+            split_bf16(square),
+            jnp.zeros((10, lats), bf16),
         ],
         axis=0,
     )
@@ -150,14 +186,13 @@
     enc_both = jnp.concatenate([pack[:LANES], pack_other[:LANES]], axis=1)
     gates_other = pack_other[LANES : LANES + chunk].astype(f32)
     gates = jnp.concatenate([gates_own.astype(f32), gates_other], axis=1)
-    bias_rows = pack_other[LANES + chunk : LANES + chunk + 3].astype(f32)
-    b_both = jnp.concatenate([b_enc, bias_rows[0] + bias_rows[1] + bias_rows[2]])[None]
+    parts = jnp.sum(pack_other[LANES + chunk : LANES + chunk + 6].astype(f32).reshape(2, 3, lats), axis=1)
+    b_both = jnp.concatenate([b_enc, parts[0]])[None]
 
     slots = jnp.arange(target_of.shape[0], dtype=jnp.int32)
     layer = jnp.sum(jnp.where(slots == slot, target_of, 0))
     flag = (layer >= source).astype(f32)
-    square = lambda w: jnp.einsum("cd,cd->c", w, w, preferred_element_type=f32)
-    squares = flag * jnp.concatenate([square(w_own), square(w_other)])
+    squares = flag * jnp.concatenate([square, parts[1]])
     top_sq = jnp.max(squares)
     e_sq = exponent(top_sq)
     scaled = squares * jnp.exp2(TOP - e_sq)
@@ -178,12 +213,17 @@
 
     out, own_ones = call(
         functools.partial(forward, feats),
-        [((SLOTS, 2 * chunk + EXTRA, both_lats), f32), ((wide, LANES), bf16)],
+        [((X, 2 * chunk + EXTRA, both_lats), f32), ((wide, LANES), bf16)],
         got, w_own, w_other, enc_both, lines, base,
     )
-    back = lax.all_to_all(out.astype(f16), TGT, 0, 0, tiled=True).astype(f32)
-    (grad,) = call(middle, [((SLOTS, chunk, both_lats), bf16)], back, gates, b_both)
-    grad = lax.all_to_all(grad, TGT, 0, 0, tiled=True).reshape(wide, both_lats)
+    back = lax.all_to_all(out.astype(f16), "x", 0, 0, tiled=True).astype(f32)
+    (half,) = call(along_x, [((2 * chunk + EXTRA, both_lats), f32)], back)
+    half = lax.optimization_barrier(half.astype(f16))
+    partner = lax.ppermute(half, "yh", SWAP)
+    (grad,) = call(
+        middle, [((X, chunk, both_lats), bf16)], half.astype(f32), partner.astype(f32), gates, b_both
+    )
+    grad = lax.all_to_all(grad, "x", 0, 0, tiled=True).reshape(wide, both_lats)
     sent, keep, away = call(
         functools.partial(backward, feats),
         [((wide, LANES), f32), ((feats + 8, lats), f32), ((feats + 8, lats), f32)],

time: 141 us -> 125 us (0.89)
  the two profiles are of different devices: /device:TPU:1 before, /device:TPU:2 now
where the time goes in v5:
time: 125 us; the launch traced here: 124 us
  waiting for transfers between devices  43.7 us (35%)
  starting transfers between devices  34.5 us (28%)
  blocking collectives  26.3 us (21%)
  Pallas kernels  7.01 us (6%)
  other arithmetic  6.84 us (5%)
  between operations  3.06 us (2%)
  local copies, waits for them, and re-layouts  3.02 us (2%)
    all_to_all x1, waiting for transfers between devices, local(): lax.all_to_all(held, PLANE, 0, 0, tiled=True).reshape(wide, depth + LANES)  21.5 us
    all_to_all x1, blocking collectives, local(): back = lax.all_to_all(out.astype(f16), 'x', 0, 0, tiled=True).astype(f32)  15.8 us
    all_to_all x1, starting transfers between devices, local(): lax.all_to_all(held, PLANE, 0, 0, tiled=True).reshape(wide, depth + LANES)  14 us
    ppermute x1, waiting for transfers between devices, local(): partner = lax.ppermute(half, 'yh', SWAP)  13.2 us
    all_to_all x1, blocking collectives, local(): grad = lax.all_to_all(grad, 'x', 0, 0, tiled=True).reshape(wide, both_lats)  10.5 us
    all_to_all x1, starting transfers between devices, local(): lax.all_to_all(sent.astype(f16).reshape(PEERS, rows, LANES), PLANE, 0, 0,...  9.11 us
    all_to_all x1, waiting for transfers between devices, local(): lax.all_to_all(sent.astype(f16).reshape(PEERS, rows, LANES), PLANE, 0, 0,...  8.83 us
    pallas_call x5, Pallas kernels, call(): return pl.pallas_call(body, out_shape=shapes, compiler_params=PARAMS)(*args)  5.71 us
  transfers between devices with their start and end apart: 6, of which 4 were waited for; matrix products, arithmetic and copies ran while one was open for 6% of the time, Pallas kernels for 0%

profile of v5, /device:TPU:2, one launch (start us, length us, event | category | flops | bytes accessed | tf_op | source)
XLA Modules:
  0.0 124.5 jit_solution(8540924412785150836)
XLA Ops:
  0.6 0.0 copy-start.1
  0.6 0.8 copy-done.1
  1.4 0.0 copy-start.2
  1.4 0.7 copy-done.2
  2.1 1.3 %shard_map.94 = bf16[32,8,2688]{2,1,0:T(8,128)(2,1)} custom-call(bf16[8,2304]{1,0:T(8,128)(2,1)S(1)} %bitcast.36, bf16[8,2,288]{2,1,0:T(2,128)(2,1)S(1)} %copy-done.2), custom_call_target="tpu_custom_call" | custom-call | tf_op jit(solution)/shard_map/pallas_call | solution.py:161
  3.4 0.0 copy-start
  3.4 14.0 %all-to-all-start = ((bf16[32,8,2688]{2,1,0:T(8,128)(2,1)}), bf16[32,8,2688]{2,1,0:T(8,128)(2,1)}, u32[]{:S(2)}, u32[]{:S(2)}) async-start(bf16[32,8,2688]{2,1,0:T(8,128)(2,1)} %shard_map.94), calls=%async_computation | async-start | bytes 2752512 | tf_op jit(solution)/shard_map/all_to_all | solution.py:165
  17.4 0.0 copy-start.4
  17.4 0.0 copy-start.3
  17.4 0.0 copy-done
  17.4 0.0 copy-start.5
  17.5 2.1 %collective-permute-start.1 = (bf16[512,2304]{1,0:T(8,128)(2,1)S(1)}, bf16[512,2304]{1,0:T(8,128)(2,1)}, u32[]{:S(2)}, u32[]{:S(2)}) collective-permute-start(bf16[512,2304]{1,0:T(8,128)(2,1)S(1)} %bitcast.33), channel_id=1, source_target_pairs={{0,8},{8,0},{1,9},{9,1},{2,10},{10,2},{3,11},{11,3},{4,12},{12,4},... | collective-permute-start | bytes 7077896 | tf_op jit(solution)/shard_map/ppermute | solution.py:173
  19.5 0.5 fusion
  20.0 0.0 copy-done.4
  20.2 1.0 fusion.3
  21.2 0.0 copy-done.3
  21.2 0.3 concatenate.37
  21.5 2.4 %collective-permute-start = (bf16[464,512]{1,0:T(8,128)(2,1)S(1)}, bf16[464,512]{1,0:T(8,128)(2,1)}, u32[]{:S(2)}, u32[]{:S(2)}) collective-permute-start(bf16[464,512]{1,0:T(8,128)(2,1)S(1)} %concatenate.37), channel_id=1, source_target_pairs={{0,8},{8,0},{1,9},{9,1},{2,10},{10,2},{3,11},{11,3},{4,12},{12,4},... | collective-permute-start | bytes 1425416 | tf_op jit(solution)/shard_map/ppermute | solution.py:185
  23.9 0.0 copy-done.5
  24.0 0.6 fusion.10
  25.2 0.1 pad.12.clone
  25.3 0.2 collective-permute-done
  25.5 0.7 slice_convert_fusion.1
  26.2 0.6 fusion.6
  28.3 0.1 pad.11.clone
  28.4 1.0 slice.24
  29.4 0.1 maximum_bitcast_fusion.base
  29.5 0.9 slice_convert_fusion
  30.4 1.1 fusion.2.enc_both
  31.4 0.1 maximum_maximum_fusion.lines
  31.5 0.0 collective-permute-done.1.w_other
  31.5 21.5 %all-to-all-done = bf16[32,8,2688]{2,1,0:T(8,128)(2,1)} async-done(((bf16[32,8,2688]{2,1,0:T(8,128)(2,1)}), bf16[32,8,2688]{2,1,0:T(8,128)(2,1)}, u32[]{:S(2)}, u32[]{:S(2)}) %all-to-all-start) | async-done | bytes 1376288 | tf_op jit(solution)/shard_map/all_to_all | solution.py:165
  53.0 3.8 %shard_map.95 = (f32[4,136,1024]{2,1,0:T(8,128)S(1)}, bf16[256,384]{1,0:T(8,128)(2,1)S(1)}) custom-call(bf16[256,2688]{1,0:T(8,128)(2,1)} %bitcast.12.got, bf16[512,2304]{1,0:T(8,128)(2,1)S(1)} %bitcast.34, bf16[512,2304]{1,0:T(8,128)(2,1)} %collective-permute-done.1.w_other, bf16[384,1024]{1,0:T(8,128)(2,1)S(1)} %fusion.2.enc_both, ...), custom_call_target="tpu_custom_call" | custom-call | tf_op jit(solution)/shard_map/pallas_call | solution.py:46
  56.8 0.2 convert_element_type.114
  57.0 15.8 %all_to_all.20 = f16[4,136,1024]{2,1,0:T(8,128)(2,1)S(1)} all-to-all(f16[4,136,1024]{2,1,0:T(8,128)(2,1)S(1)} %convert_element_type.114), channel_id=1, replica_groups=mesh['yl'=4,'z'=8,'c'=2,'yh'=2,'x'=4] {'x'}, dimensions={0} | all-to-all | bytes 2228224 | tf_op jit(solution)/shard_map/all_to_all | solution.py:219
  72.8 0.2 convert_element_type.115.back
  73.0 0.1 shard_map.96
  73.2 5.1 %collective-permute-start.2 = (f16[136,1024]{1,0:T(8,128)(2,1)S(1)}, f16[136,1024]{1,0:T(8,128)(2,1)S(1)}, u32[]{:S(2)}, u32[]{:S(2)}) collective-permute-start(f16[136,1024]{1,0:T(8,128)(2,1)S(1)} %convert_element_type.116), channel_id=1, source_target_pairs={{0,4},{4,0},{1,5},{5,1},{2,6},{6,2},{3,7},{7,3},{8,12},{12,8},{9,1... | collective-permute-start | bytes 835592 | tf_op jit(solution)/shard_map/ppermute | solution.py:222
  78.4 13.2 %collective-permute-done.2 = f16[136,1024]{1,0:T(8,128)(2,1)S(1)} collective-permute-done((f16[136,1024]{1,0:T(8,128)(2,1)S(1)}, f16[136,1024]{1,0:T(8,128)(2,1)S(1)}, u32[]{:S(2)}, u32[]{:S(2)}) %collective-permute-start.2) | collective-permute-done | bytes 278560 | tf_op jit(solution)/shard_map/ppermute | solution.py:222
  91.6 0.2 shard_map.97
  91.8 10.5 %all_to_all.21 = bf16[4,64,1024]{2,1,0:T(8,128)(2,1)S(1)} all-to-all(bf16[4,64,1024]{2,1,0:T(8,128)(2,1)S(1)} %shard_map.97), channel_id=1, replica_groups=mesh['yl'=4,'z'=8,'c'=2,'yh'=2,'x'=4] {'x'}, dimensions={0} | all-to-all | bytes 1048576 | tf_op jit(solution)/shard_map/all_to_all | solution.py:226
  102.2 0.7 shard_map.98
  102.9 0.7 convert_bitcast_fusion
  103.6 9.1 %all-to-all-start.3 = ((f16[32,8,384]{2,1,0:T(8,128)(2,1)}), f16[32,8,384]{2,1,0:T(8,128)(2,1)S(1)}, u32[]{:S(2)}, u32[]{:S(2)}) async-start(f16[32,8,384]{2,1,0:T(8,128)(2,1)} %convert_bitcast_fusion), calls=%async_computation.3 | async-start | bytes 393216 | tf_op jit(solution)/shard_map/all_to_all | solution.py:233
  112.7 1.9 %collective-permute-start.3 = (f32[296,512]{1,0:T(8,128)S(1)}, f32[296,512]{1,0:T(8,128)S(1)}, u32[]{:S(2)}, u32[]{:S(2)}) collective-permute-start(f32[296,512]{1,0:T(8,128)S(1)} %get-tuple-element.35), channel_id=1, source_target_pairs={{0,8},{8,0},{1,9},{9,1},{2,10},{10,2},{3,11},{11,3},{4,12},{12,4},... | collective-permute-start | bytes 1818632 | tf_op jit(solution)/shard_map/ppermute | solution.py:232
  114.6 8.8 %all-to-all-done.3 = f16[32,8,384]{2,1,0:T(8,128)(2,1)S(1)} async-done(((f16[32,8,384]{2,1,0:T(8,128)(2,1)}), f16[32,8,384]{2,1,0:T(8,128)(2,1)S(1)}, u32[]{:S(2)}, u32[]{:S(2)}) %all-to-all-start.3) | async-done | bytes 196640 | tf_op jit(solution)/shard_map/all_to_all | solution.py:233
  123.5 0.0 collective-permute-done.3.far
  123.5 1.0 shard_map.99
  (22 shorter events, 0.3 us)
Async XLA Ops:
  0.6 0.8 copy-start.1
  1.4 0.7 copy-start.2
  3.4 14.0 %copy-start = (bf16[1,512,2304]{2,1,0:T(8,128)(2,1)S(1)}, bf16[1,512,2304]{2,1,0:T(8,128)(2,1)}, u32[]{:S(2)}) copy-start(bf16[1,512,2304]{2,1,0:T(8,128)(2,1)} %param.11) | copy-start | bytes 7077892
  3.4 49.6 %all-to-all-start = ((bf16[32,8,2688]{2,1,0:T(8,128)(2,1)}), bf16[32,8,2688]{2,1,0:T(8,128)(2,1)}, u32[]{:S(2)}, u32[]{:S(2)}) async-start(bf16[32,8,2688]{2,1,0:T(8,128)(2,1)} %shard_map.94), calls=%async_computation | async-start | bytes 2752512 | tf_op jit(solution)/shard_map/all_to_all | solution.py:165
  17.4 2.6 %copy-start.4 = (f32[512]{0:T(512)S(1)}, f32[512]{0:T(512)}, u32[]{:S(2)}) copy-start(f32[512]{0:T(512)} %param.9) | copy-start | bytes 6148
  17.4 3.8 %copy-start.3 = (bf16[288,512]{1,0:T(8,128)(2,1)S(1)}, bf16[288,512]{1,0:T(8,128)(2,1)}, u32[]{:S(2)}) copy-start(bf16[288,512]{1,0:T(8,128)(2,1)} %param.8) | copy-start | bytes 884740
  17.4 6.5 %copy-start.5 = (s32[8]{0:T(128)S(1)}, s32[8]{0:T(128)}, u32[]{:S(2)}) copy-start(s32[8]{0:T(128)} %param.13) | copy-start | bytes 100
  17.5 14.1 %collective-permute-start.1 = (bf16[512,2304]{1,0:T(8,128)(2,1)S(1)}, bf16[512,2304]{1,0:T(8,128)(2,1)}, u32[]{:S(2)}, u32[]{:S(2)}) collective-permute-start(bf16[512,2304]{1,0:T(8,128)(2,1)S(1)} %bitcast.33), channel_id=1, source_target_pairs={{0,8},{8,0},{1,9},{9,1},{2,10},{10,2},{3,11},{11,3},{4,12},{12,4},... | collective-permute-start | bytes 7077896 | tf_op jit(solution)/shard_map/ppermute | solution.py:173
  21.5 4.0 %collective-permute-start = (bf16[464,512]{1,0:T(8,128)(2,1)S(1)}, bf16[464,512]{1,0:T(8,128)(2,1)}, u32[]{:S(2)}, u32[]{:S(2)}) collective-permute-start(bf16[464,512]{1,0:T(8,128)(2,1)S(1)} %concatenate.37), channel_id=1, source_target_pairs={{0,8},{8,0},{1,9},{9,1},{2,10},{10,2},{3,11},{11,3},{4,12},{12,4},... | collective-permute-start | bytes 1425416 | tf_op jit(solution)/shard_map/ppermute | solution.py:185
  73.2 18.3 %collective-permute-start.2 = (f16[136,1024]{1,0:T(8,128)(2,1)S(1)}, f16[136,1024]{1,0:T(8,128)(2,1)S(1)}, u32[]{:S(2)}, u32[]{:S(2)}) collective-permute-start(f16[136,1024]{1,0:T(8,128)(2,1)S(1)} %convert_element_type.116), channel_id=1, source_target_pairs={{0,4},{4,0},{1,5},{5,1},{2,6},{6,2},{3,7},{7,3},{8,12},{12,8},{9,1... | collective-permute-start | bytes 835592 | tf_op jit(solution)/shard_map/ppermute | solution.py:222
  103.6 19.9 %all-to-all-start.3 = ((f16[32,8,384]{2,1,0:T(8,128)(2,1)}), f16[32,8,384]{2,1,0:T(8,128)(2,1)S(1)}, u32[]{:S(2)}, u32[]{:S(2)}) async-start(f16[32,8,384]{2,1,0:T(8,128)(2,1)} %convert_bitcast_fusion), calls=%async_computation.3 | async-start | bytes 393216 | tf_op jit(solution)/shard_map/all_to_all | solution.py:233
  112.7 10.8 %collective-permute-start.3 = (f32[296,512]{1,0:T(8,128)S(1)}, f32[296,512]{1,0:T(8,128)S(1)}, u32[]{:S(2)}, u32[]{:S(2)}) collective-permute-start(f32[296,512]{1,0:T(8,128)S(1)} %get-tuple-element.35), channel_id=1, source_target_pairs={{0,8},{8,0},{1,9},{9,1},{2,10},{10,2},{3,11},{11,3},{4,12},{12,4},... | collective-permute-start | bytes 1818632 | tf_op jit(solution)/shard_map/ppermute | solution.py:232

commit v6 on v5

--- a/solution.py
+++ b/solution.py
@@ -24,9 +24,10 @@
 TOP = 14.0
 SWAP = [(0, 1), (1, 0)]
 f32, bf16, f16 = jnp.float32, jnp.bfloat16, jnp.float16
+VMEM = pl.BlockSpec(memory_space=pltpu.VMEM)
 BY_LAST = (((1,), (1,)), ((), ()))
 BY_FIRST = (((0,), (0,)), ((), ()))
-PARAMS = pltpu.CompilerParams(vmem_limit_bytes=40 * 1024 * 1024)
+PARAMS = pltpu.CompilerParams(vmem_limit_bytes=24 * 1024 * 1024)
 
 
 def exponent(bound):
@@ -41,12 +42,20 @@
     return jnp.stack([hi, mid, low])
 
 
-def call(body, outs, *args):
+def call(body, outs, *args, **kinds):
     shapes = [jax.ShapeDtypeStruct(*o) for o in outs]
-    return pl.pallas_call(body, out_shape=shapes, compiler_params=PARAMS)(*args)
-
-
-def prepare(errors, inputs, out):
+    return pl.pallas_call(body, out_shape=shapes, compiler_params=PARAMS, **kinds)(*args)
+
+
+def prepare(errors_far, inputs_far, out, errors, inputs, arrived):
+    fetches = [
+        pltpu.make_async_copy(errors_far, errors, arrived.at[0]),
+        pltpu.make_async_copy(inputs_far, inputs, arrived.at[1]),
+    ]
+    for fetch in fetches:
+        fetch.start()
+    for fetch in fetches:
+        fetch.wait()
     rows, depth = errors.shape
     errs = errors[...]
     top_err = jnp.max(jnp.abs(errs.astype(f32)), axis=(0, 1), keepdims=True) * 1.01
@@ -58,10 +67,11 @@
             out[s * (PEERS // S) + i, :, depth:] = last
 
 
-def forward(feats, got, w_own, w_other, enc_both, lines, base, out, ones_out):
+def forward(feats, got, w_own, w_far, enc_both, lines, base, out, ones_out, w_other, arrived):
+    fetch = pltpu.make_async_copy(w_far, w_other, arrived)
+    fetch.start()
     wide = got.shape[0]
-    depth = w_own.shape[1]
-    lats = w_own.shape[0]
+    lats, depth = w_own.shape
     chunk = wide // X
     errs = got[:, :depth]
     own = got[:, depth:]
@@ -71,15 +81,17 @@
     top_err = jnp.max(jnp.where(lane == feats, own32, 0.0), axis=(0, 1), keepdims=True)
     e_term = exponent(base[:, 0:1] * top_err)
     scale = base[:, 1:2] * jnp.exp2(TOP - e_term)
-    for h, w in enumerate((w_own, w_other)):
-        term = lax.dot_general(errs, w[...], BY_LAST, preferred_element_type=f32) * scale
-        out[:, :chunk, h * lats : (h + 1) * lats] = term.reshape(X, chunk, lats)
     pre = jnp.dot(own, enc_both[...], preferred_element_type=f32) * PRE_SCALE
     out[:, chunk : 2 * chunk, :] = pre.reshape(X, chunk, C * lats)
     row = lax.broadcasted_iota(jnp.int32, lines.shape, 0)
     extra = jnp.where(row == 3, jnp.broadcast_to(e_term, lines.shape), lines[...])
     for i in range(X):
         out[i, 2 * chunk :, :] = extra
+    for h, w in enumerate((w_own, w_other)):
+        if h == 1:
+            fetch.wait()
+        term = lax.dot_general(errs, w[...], BY_LAST, preferred_element_type=f32) * scale
+        out[:, :chunk, h * lats : (h + 1) * lats] = term.reshape(X, chunk, lats)
 
 
 def along_x(back, out):
@@ -159,8 +171,16 @@
     pad = LANES - feats
 
     held = pl.pallas_call(
-        prepare, out_shape=pltpu.HBM((PEERS, rows, depth + LANES), bf16), compiler_params=PARAMS
-    )(errors[0], inputs)
+        prepare,
+        out_shape=pltpu.HBM((PEERS, rows, depth + LANES), bf16),
+        in_specs=[pl.BlockSpec(memory_space=pltpu.HBM)] * 2,
+        scratch_shapes=[
+            pltpu.VMEM(errors.shape[1:], bf16),
+            pltpu.VMEM(inputs.shape, bf16),
+            pltpu.SemaphoreType.DMA((2,)),
+        ],
+        compiler_params=PARAMS,
+    )(*(pltpu.with_memory_space_constraint(v, pltpu.HBM) for v in (errors[0], inputs)))
     held, masks, w_dec = lax.optimization_barrier((held, masks, w_dec))
     got = lax.all_to_all(held, PLANE, 0, 0, tiled=True).reshape(wide, depth + LANES)
 
@@ -215,6 +235,8 @@
         functools.partial(forward, feats),
         [((X, 2 * chunk + EXTRA, both_lats), f32), ((wide, LANES), bf16)],
         got, w_own, w_other, enc_both, lines, base,
+        in_specs=[VMEM, VMEM, pl.BlockSpec(memory_space=pl.ANY), VMEM, VMEM, VMEM],
+        scratch_shapes=[pltpu.VMEM((lats, depth), bf16), pltpu.SemaphoreType.DMA],
     )
     back = lax.all_to_all(out.astype(f16), "x", 0, 0, tiled=True).astype(f32)
     (half,) = call(along_x, [((2 * chunk + EXTRA, both_lats), f32)], back)

time: 125 us -> 125 us (level)
  local copies, waits for them, and re-layouts: 3.02 us -> 1.56 us
  Pallas kernels: 7.01 us -> 8.4 us
    unnamed x12 -> x8, local copies, waits for them, and re-layouts: 1.49 us -> 0.03 us
where the time goes in v6:
time: 125 us; the launch traced here: 124 us
  waiting for transfers between devices  43.7 us (35%)
  starting transfers between devices  34.6 us (28%)
  blocking collectives  26.3 us (21%)
  Pallas kernels  8.4 us (7%)
  other arithmetic  6.83 us (5%)
  between operations  3.06 us (2%)
  local copies, waits for them, and re-layouts  1.56 us (1%)
    all_to_all x1, waiting for transfers between devices, local(): lax.all_to_all(held, PLANE, 0, 0, tiled=True).reshape(wide, depth + LANES)  21.5 us
    all_to_all x1, blocking collectives, local(): back = lax.all_to_all(out.astype(f16), 'x', 0, 0, tiled=True).astype(f32)  15.8 us
    all_to_all x1, starting transfers between devices, local(): lax.all_to_all(held, PLANE, 0, 0, tiled=True).reshape(wide, depth + LANES)  14 us
    ppermute x1, waiting for transfers between devices, local(): partner = lax.ppermute(half, 'yh', SWAP)  13.2 us
    all_to_all x1, blocking collectives, local(): grad = lax.all_to_all(grad, 'x', 0, 0, tiled=True).reshape(wide, both_lats)  10.5 us
    all_to_all x1, starting transfers between devices, local(): lax.all_to_all(sent.astype(f16).reshape(PEERS, rows, LANES), PLANE, 0, 0,...  9.1 us
    all_to_all x1, waiting for transfers between devices, local(): lax.all_to_all(sent.astype(f16).reshape(PEERS, rows, LANES), PLANE, 0, 0,...  8.83 us
    pallas_call x5, Pallas kernels, call(): pl.pallas_call(body, out_shape=shapes, compiler_params=PARAMS, **kinds)  6.38 us
  transfers between devices with their start and end apart: 6, of which 4 were waited for; matrix products, arithmetic and copies ran while one was open for 6% of the time, Pallas kernels for 0%

profile of v6, /device:TPU:2, one launch (start us, length us, event | category | flops | bytes accessed | tf_op | source)
XLA Modules:
  0.0 124.4 jit_solution(10394646295860915768)
XLA Ops:
  0.6 2.0 %shard_map.94 = bf16[32,8,2688]{2,1,0:T(8,128)(2,1)} custom-call(bf16[8,2304]{1,0:T(8,128)(2,1)} %bitcast.38, bf16[8,2,288]{2,1,0:T(2,128)(2,1)} %inputs_far.1), custom_call_target="tpu_custom_call" | custom-call | tf_op jit(solution)/shard_map/pallas_call | solution.py:173
  2.7 0.0 copy-start
  2.7 14.0 %all-to-all-start = ((bf16[32,8,2688]{2,1,0:T(8,128)(2,1)}), bf16[32,8,2688]{2,1,0:T(8,128)(2,1)}, u32[]{:S(2)}, u32[]{:S(2)}) async-start(bf16[32,8,2688]{2,1,0:T(8,128)(2,1)} %shard_map.94), calls=%async_computation | async-start | bytes 2752512 | tf_op jit(solution)/shard_map/all_to_all | solution.py:185
  16.7 0.0 copy-start.2
  16.7 0.0 copy-start.1
  16.7 0.0 copy-done
  16.7 0.0 copy-start.3
  16.7 2.1 %collective-permute-start.1 = (bf16[512,2304]{1,0:T(8,128)(2,1)S(1)}, bf16[512,2304]{1,0:T(8,128)(2,1)}, u32[]{:S(2)}, u32[]{:S(2)}) collective-permute-start(bf16[512,2304]{1,0:T(8,128)(2,1)S(1)} %bitcast.33), channel_id=1, source_target_pairs={{0,8},{8,0},{1,9},{9,1},{2,10},{10,2},{3,11},{11,3},{4,12},{12,4},... | collective-permute-start | bytes 7077896 | tf_op jit(solution)/shard_map/ppermute | solution.py:193
  18.8 0.5 fusion
  19.3 0.0 copy-done.2
  19.4 1.0 fusion.3
  20.5 0.0 copy-done.1
  20.5 0.3 concatenate.37
  20.8 2.4 %collective-permute-start = (bf16[464,512]{1,0:T(8,128)(2,1)S(1)}, bf16[464,512]{1,0:T(8,128)(2,1)}, u32[]{:S(2)}, u32[]{:S(2)}) collective-permute-start(bf16[464,512]{1,0:T(8,128)(2,1)S(1)} %concatenate.37), channel_id=1, source_target_pairs={{0,8},{8,0},{1,9},{9,1},{2,10},{10,2},{3,11},{11,3},{4,12},{12,4},... | collective-permute-start | bytes 1425416 | tf_op jit(solution)/shard_map/ppermute | solution.py:205
  23.2 0.0 copy-done.3
  23.2 0.6 fusion.10
  24.5 0.1 pad.12.clone
  24.6 0.2 collective-permute-done
  24.8 0.7 slice_convert_fusion.1
  25.5 0.6 fusion.6
  27.6 0.1 pad.11.clone
  27.6 1.0 slice.24
  28.7 0.1 maximum_bitcast_fusion.base
  28.8 0.9 slice_convert_fusion
  29.6 1.1 fusion.2.enc_both
  30.7 0.1 maximum_maximum_fusion.lines
  30.8 0.0 collective-permute-done.1.w_far
  30.8 21.5 %all-to-all-done = bf16[32,8,2688]{2,1,0:T(8,128)(2,1)} async-done(((bf16[32,8,2688]{2,1,0:T(8,128)(2,1)}), bf16[32,8,2688]{2,1,0:T(8,128)(2,1)}, u32[]{:S(2)}, u32[]{:S(2)}) %all-to-all-start) | async-done | bytes 1376288 | tf_op jit(solution)/shard_map/all_to_all | solution.py:185
  52.3 4.5 %shard_map.95 = (f32[4,136,1024]{2,1,0:T(8,128)S(1)}, bf16[256,384]{1,0:T(8,128)(2,1)S(1)}) custom-call(bf16[256,2688]{1,0:T(8,128)(2,1)} %bitcast.12.got, bf16[512,2304]{1,0:T(8,128)(2,1)S(1)} %bitcast.34, bf16[512,2304]{1,0:T(8,128)(2,1)} %collective-permute-done.1.w_far, bf16[384,1024]{1,0:T(8,128)(2,1)S(1)} %fusion.2.enc_both, ...), custom_call_target="tpu_custom_call" | custom-call | tf_op jit(solution)/shard_map/pallas_call | solution.py:47
  56.8 0.2 convert_element_type.114
  56.9 15.8 %all_to_all.20 = f16[4,136,1024]{2,1,0:T(8,128)(2,1)S(1)} all-to-all(f16[4,136,1024]{2,1,0:T(8,128)(2,1)S(1)} %convert_element_type.114), channel_id=1, replica_groups=mesh['yl'=4,'z'=8,'c'=2,'yh'=2,'x'=4] {'x'}, dimensions={0} | all-to-all | bytes 2228224 | tf_op jit(solution)/shard_map/all_to_all | solution.py:241
  72.8 0.2 convert_element_type.115.back
  73.0 0.1 shard_map.96
  73.2 5.1 %collective-permute-start.2 = (f16[136,1024]{1,0:T(8,128)(2,1)S(1)}, f16[136,1024]{1,0:T(8,128)(2,1)S(1)}, u32[]{:S(2)}, u32[]{:S(2)}) collective-permute-start(f16[136,1024]{1,0:T(8,128)(2,1)S(1)} %convert_element_type.116), channel_id=1, source_target_pairs={{0,4},{4,0},{1,5},{5,1},{2,6},{6,2},{3,7},{7,3},{8,12},{12,8},{9,1... | collective-permute-start | bytes 835592 | tf_op jit(solution)/shard_map/ppermute | solution.py:244
  78.3 13.2 %collective-permute-done.2 = f16[136,1024]{1,0:T(8,128)(2,1)S(1)} collective-permute-done((f16[136,1024]{1,0:T(8,128)(2,1)S(1)}, f16[136,1024]{1,0:T(8,128)(2,1)S(1)}, u32[]{:S(2)}, u32[]{:S(2)}) %collective-permute-start.2) | collective-permute-done | bytes 278560 | tf_op jit(solution)/shard_map/ppermute | solution.py:244
  91.5 0.2 shard_map.97
  91.7 10.5 %all_to_all.21 = bf16[4,64,1024]{2,1,0:T(8,128)(2,1)S(1)} all-to-all(bf16[4,64,1024]{2,1,0:T(8,128)(2,1)S(1)} %shard_map.97), channel_id=1, replica_groups=mesh['yl'=4,'z'=8,'c'=2,'yh'=2,'x'=4] {'x'}, dimensions={0} | all-to-all | bytes 1048576 | tf_op jit(solution)/shard_map/all_to_all | solution.py:248
  102.2 0.7 shard_map.98
  102.8 0.7 convert_bitcast_fusion
  103.5 9.1 %all-to-all-start.3 = ((f16[32,8,384]{2,1,0:T(8,128)(2,1)}), f16[32,8,384]{2,1,0:T(8,128)(2,1)S(1)}, u32[]{:S(2)}, u32[]{:S(2)}) async-start(f16[32,8,384]{2,1,0:T(8,128)(2,1)} %convert_bitcast_fusion), calls=%async_computation.3 | async-start | bytes 393216 | tf_op jit(solution)/shard_map/all_to_all | solution.py:255
  112.7 1.9 %collective-permute-start.3 = (f32[296,512]{1,0:T(8,128)S(1)}, f32[296,512]{1,0:T(8,128)S(1)}, u32[]{:S(2)}, u32[]{:S(2)}) collective-permute-start(f32[296,512]{1,0:T(8,128)S(1)} %get-tuple-element.35), channel_id=1, source_target_pairs={{0,8},{8,0},{1,9},{9,1},{2,10},{10,2},{3,11},{11,3},{4,12},{12,4},... | collective-permute-start | bytes 1818632 | tf_op jit(solution)/shard_map/ppermute | solution.py:254
  114.6 8.8 %all-to-all-done.3 = f16[32,8,384]{2,1,0:T(8,128)(2,1)S(1)} async-done(((f16[32,8,384]{2,1,0:T(8,128)(2,1)}), f16[32,8,384]{2,1,0:T(8,128)(2,1)S(1)}, u32[]{:S(2)}, u32[]{:S(2)}) %all-to-all-start.3) | async-done | bytes 196640 | tf_op jit(solution)/shard_map/all_to_all | solution.py:255
  123.4 0.0 collective-permute-done.3.far
  123.5 1.0 shard_map.99
  (22 shorter events, 0.3 us)
Async XLA Ops:
  2.7 14.0 %copy-start = (bf16[1,512,2304]{2,1,0:T(8,128)(2,1)S(1)}, bf16[1,512,2304]{2,1,0:T(8,128)(2,1)}, u32[]{:S(2)}) copy-start(bf16[1,512,2304]{2,1,0:T(8,128)(2,1)} %param.11) | copy-start | bytes 7077892
  2.7 49.6 %all-to-all-start = ((bf16[32,8,2688]{2,1,0:T(8,128)(2,1)}), bf16[32,8,2688]{2,1,0:T(8,128)(2,1)}, u32[]{:S(2)}, u32[]{:S(2)}) async-start(bf16[32,8,2688]{2,1,0:T(8,128)(2,1)} %shard_map.94), calls=%async_computation | async-start | bytes 2752512 | tf_op jit(solution)/shard_map/all_to_all | solution.py:185
  16.7 2.6 %copy-start.2 = (f32[512]{0:T(512)S(1)}, f32[512]{0:T(512)}, u32[]{:S(2)}) copy-start(f32[512]{0:T(512)} %param.9) | copy-start | bytes 6148
  16.7 3.8 %copy-start.1 = (bf16[288,512]{1,0:T(8,128)(2,1)S(1)}, bf16[288,512]{1,0:T(8,128)(2,1)}, u32[]{:S(2)}) copy-start(bf16[288,512]{1,0:T(8,128)(2,1)} %param.8) | copy-start | bytes 884740
  16.7 6.5 %copy-start.3 = (s32[8]{0:T(128)S(1)}, s32[8]{0:T(128)}, u32[]{:S(2)}) copy-start(s32[8]{0:T(128)} %param.13) | copy-start | bytes 100
  16.7 14.1 %collective-permute-start.1 = (bf16[512,2304]{1,0:T(8,128)(2,1)S(1)}, bf16[512,2304]{1,0:T(8,128)(2,1)}, u32[]{:S(2)}, u32[]{:S(2)}) collective-permute-start(bf16[512,2304]{1,0:T(8,128)(2,1)S(1)} %bitcast.33), channel_id=1, source_target_pairs={{0,8},{8,0},{1,9},{9,1},{2,10},{10,2},{3,11},{11,3},{4,12},{12,4},... | collective-permute-start | bytes 7077896 | tf_op jit(solution)/shard_map/ppermute | solution.py:193
  20.8 4.0 %collective-permute-start = (bf16[464,512]{1,0:T(8,128)(2,1)S(1)}, bf16[464,512]{1,0:T(8,128)(2,1)}, u32[]{:S(2)}, u32[]{:S(2)}) collective-permute-start(bf16[464,512]{1,0:T(8,128)(2,1)S(1)} %concatenate.37), channel_id=1, source_target_pairs={{0,8},{8,0},{1,9},{9,1},{2,10},{10,2},{3,11},{11,3},{4,12},{12,4},... | collective-permute-start | bytes 1425416 | tf_op jit(solution)/shard_map/ppermute | solution.py:205
  73.2 18.3 %collective-permute-start.2 = (f16[136,1024]{1,0:T(8,128)(2,1)S(1)}, f16[136,1024]{1,0:T(8,128)(2,1)S(1)}, u32[]{:S(2)}, u32[]{:S(2)}) collective-permute-start(f16[136,1024]{1,0:T(8,128)(2,1)S(1)} %convert_element_type.116), channel_id=1, source_target_pairs={{0,4},{4,0},{1,5},{5,1},{2,6},{6,2},{3,7},{7,3},{8,12},{12,8},{9,1... | collective-permute-start | bytes 835592 | tf_op jit(solution)/shard_map/ppermute | solution.py:244
  103.5 19.9 %all-to-all-start.3 = ((f16[32,8,384]{2,1,0:T(8,128)(2,1)}), f16[32,8,384]{2,1,0:T(8,128)(2,1)S(1)}, u32[]{:S(2)}, u32[]{:S(2)}) async-start(f16[32,8,384]{2,1,0:T(8,128)(2,1)} %convert_bitcast_fusion), calls=%async_computation.3 | async-start | bytes 393216 | tf_op jit(solution)/shard_map/all_to_all | solution.py:255
  112.7 10.8 %collective-permute-start.3 = (f32[296,512]{1,0:T(8,128)S(1)}, f32[296,512]{1,0:T(8,128)S(1)}, u32[]{:S(2)}, u32[]{:S(2)}) collective-permute-start(f32[296,512]{1,0:T(8,128)S(1)} %get-tuple-element.35), channel_id=1, source_target_pairs={{0,8},{8,0},{1,9},{9,1},{2,10},{10,2},{3,11},{11,3},{4,12},{12,4},... | collective-permute-start | bytes 1818632 | tf_op jit(solution)/shard_map/ppermute | solution.py:254

commit v7 on v6

--- a/solution.py
+++ b/solution.py
@@ -24,7 +24,6 @@
 TOP = 14.0
 SWAP = [(0, 1), (1, 0)]
 f32, bf16, f16 = jnp.float32, jnp.bfloat16, jnp.float16
-VMEM = pl.BlockSpec(memory_space=pltpu.VMEM)
 BY_LAST = (((1,), (1,)), ((), ()))
 BY_FIRST = (((0,), (0,)), ((), ()))
 PARAMS = pltpu.CompilerParams(vmem_limit_bytes=24 * 1024 * 1024)
@@ -42,9 +41,9 @@
     return jnp.stack([hi, mid, low])
 
 
-def call(body, outs, *args, **kinds):
+def call(body, outs, *args):
     shapes = [jax.ShapeDtypeStruct(*o) for o in outs]
-    return pl.pallas_call(body, out_shape=shapes, compiler_params=PARAMS, **kinds)(*args)
+    return pl.pallas_call(body, out_shape=shapes, compiler_params=PARAMS)(*args)
 
 
 def prepare(errors_far, inputs_far, out, errors, inputs, arrived):
@@ -67,48 +66,51 @@
             out[s * (PEERS // S) + i, :, depth:] = last
 
 
-def forward(feats, got, w_own, w_far, enc_both, lines, base, out, ones_out, w_other, arrived):
-    fetch = pltpu.make_async_copy(w_far, w_other, arrived)
-    fetch.start()
-    wide = got.shape[0]
-    lats, depth = w_own.shape
+def first(feats, last, enc_both, lines, base, out, ones_out, tops):
+    wide = last.shape[0]
     chunk = wide // X
-    errs = got[:, :depth]
-    own = got[:, depth:]
+    own = last[...]
     lane = lax.broadcasted_iota(jnp.int32, own.shape, 1)
     own32 = own.astype(f32)
     ones_out[...] = jnp.where(lane < feats, own32, 1.0).astype(bf16)
     top_err = jnp.max(jnp.where(lane == feats, own32, 0.0), axis=(0, 1), keepdims=True)
     e_term = exponent(base[:, 0:1] * top_err)
-    scale = base[:, 1:2] * jnp.exp2(TOP - e_term)
+    tops[...] = jnp.broadcast_to(e_term, tops.shape)
     pre = jnp.dot(own, enc_both[...], preferred_element_type=f32) * PRE_SCALE
-    out[:, chunk : 2 * chunk, :] = pre.reshape(X, chunk, C * lats)
+    out[:, :chunk, :] = pre.reshape(X, chunk, enc_both.shape[1])
     row = lax.broadcasted_iota(jnp.int32, lines.shape, 0)
     extra = jnp.where(row == 3, jnp.broadcast_to(e_term, lines.shape), lines[...])
     for i in range(X):
-        out[i, 2 * chunk :, :] = extra
+        out[i, chunk:, :] = extra
+
+
+def terms(errs, w_own, w_far, tops, base, out, w_other, arrived):
+    fetch = pltpu.make_async_copy(w_far, w_other, arrived)
+    fetch.start()
+    lats = w_own.shape[0]
+    chunk = errs.shape[0] // X
+    scale = base[:, 1:2] * jnp.exp2(TOP - tops[0:1, 0:1])
     for h, w in enumerate((w_own, w_other)):
         if h == 1:
             fetch.wait()
-        term = lax.dot_general(errs, w[...], BY_LAST, preferred_element_type=f32) * scale
-        out[:, :chunk, h * lats : (h + 1) * lats] = term.reshape(X, chunk, lats)
-
-
-def along_x(back, out):
-    chunk = (back.shape[1] - EXTRA) // 2
-    at = 2 * chunk
+        term = lax.dot_general(errs[...], w[...], BY_LAST, preferred_element_type=f32) * scale
+        out[:, :, h * lats : (h + 1) * lats] = term.reshape(X, chunk, lats)
+
+
+def pre_along_x(back, out, weights):
+    at = back.shape[1] - EXTRA
     line = lambda i, k: back[i, at + k : at + k + 1, :]
     e_sq, e_term = line(0, 2), line(0, 3)
     for i in range(1, X):
         e_sq, e_term = jnp.maximum(e_sq, line(i, 2)), jnp.maximum(e_term, line(i, 3))
     e_sq, e_term = e_sq + 2.0, e_term + 2.0
-    dact, pre, squares = 0.0, 0.0, 0.0
+    pre, squares = 0.0, 0.0
     for i in range(X):
-        dact += back[i, :chunk, :] * jnp.exp2(line(i, 3) - e_term)
-        pre += back[i, chunk:at, :]
+        pre += back[i, :at, :]
         squares += (line(i, 0) + line(i, 1)) * jnp.exp2(line(i, 2) - e_sq)
-    out[:chunk, :] = dact
-    out[chunk:at, :] = pre
+        weights[i : i + 1, :] = jnp.exp2(line(i, 3) - e_term)
+    weights[X:, :] = jnp.zeros((EXTRA - X, out.shape[1]), f32)
+    out[:at, :] = pre
     hi = squares.astype(bf16).astype(f32)
     out[at : at + 1, :] = hi
     out[at + 1 : at + 2, :] = squares - hi
@@ -117,20 +119,31 @@
     out[at + 4 :, :] = jnp.zeros((EXTRA - 4, out.shape[1]), f32)
 
 
-def middle(one, two, gates, bias, out):
-    chunk = gates.shape[0]
-    dact, pre, sumsq = 0.0, 0.0, 0.0
-    at = 2 * chunk
-    for half in (one, two):
-        dact += half[:chunk, :] * jnp.exp2(half[at + 3 : at + 4, :] - TOP)
-        pre += half[chunk:at, :]
+def terms_along_x(back, weights, out):
+    total = 0.0
+    for i in range(X):
+        total += back[i] * weights[i : i + 1, :]
+    out[...] = total
+
+
+def penalties(one, two, gates, bias, out, weights):
+    at = gates.shape[0]
+    pre, sumsq = 0.0, 0.0
+    for k, half in enumerate((one, two)):
+        pre += half[:at, :]
         squares = half[at : at + 1, :] + half[at + 1 : at + 2, :]
         sumsq += squares * jnp.exp2(half[at + 2 : at + 3, :] - TOP)
+        weights[k : k + 1, :] = jnp.exp2(half[at + 3 : at + 4, :] - TOP)
+    weights[2:, :] = jnp.zeros((EXTRA - 2, gates.shape[1]), f32)
     pre = pre * (1.0 / PRE_SCALE) + bias[...]
     norm = jnp.sqrt(sumsq)
     tanh_val = jnp.tanh(sharpness * (gates[...] * pre) * norm)
-    grad = gates[...] * (dact + penalty * sharpness * norm * (1.0 - tanh_val * tanh_val))
-    grad = grad.astype(bf16)
+    out[...] = penalty * sharpness * norm * (1.0 - tanh_val * tanh_val)
+
+
+def gradient(one, two, weights, pull, gates, out):
+    dact = one[...] * weights[0:1, :] + two[...] * weights[1:2, :]
+    grad = (gates[...] * (dact + pull[...])).astype(bf16)
     for i in range(X):
         out[i] = grad
 
@@ -231,19 +244,64 @@
         (lines, base, enc_both, gates, b_both, w_other, got)
     )
 
-    out, own_ones = call(
-        functools.partial(forward, feats),
-        [((X, 2 * chunk + EXTRA, both_lats), f32), ((wide, LANES), bf16)],
-        got, w_own, w_other, enc_both, lines, base,
-        in_specs=[VMEM, VMEM, pl.BlockSpec(memory_space=pl.ANY), VMEM, VMEM, VMEM],
+    whole = lambda shape: pl.BlockSpec(shape, lambda i: (0,) * len(shape))
+    pre_out, own_ones, tops = pl.pallas_call(
+        functools.partial(first, feats),
+        grid=(1,),
+        in_specs=[
+            pl.BlockSpec((wide, LANES), lambda i: (0, depth // LANES)),
+            whole((LANES, both_lats)),
+            whole((EXTRA, both_lats)),
+            whole((1, 2)),
+        ],
+        out_specs=[whole((X, chunk + EXTRA, both_lats)), whole((wide, LANES)), whole((EXTRA, 128))],
+        out_shape=[
+            jax.ShapeDtypeStruct((X, chunk + EXTRA, both_lats), f32),
+            jax.ShapeDtypeStruct((wide, LANES), bf16),
+            jax.ShapeDtypeStruct((EXTRA, 128), f32),
+        ],
+        compiler_params=PARAMS,
+    )(got, enc_both, lines, base)
+    pre_in = lax.all_to_all(pre_out.astype(f16), "x", 0, 0, tiled=True).astype(f32)
+    term = pl.pallas_call(
+        terms,
+        grid=(1,),
+        in_specs=[
+            whole((wide, depth)),
+            whole((lats, depth)),
+            pl.BlockSpec(memory_space=pl.ANY),
+            whole((EXTRA, 128)),
+            whole((1, 2)),
+        ],
+        out_specs=whole((X, chunk, both_lats)),
+        out_shape=jax.ShapeDtypeStruct((X, chunk, both_lats), f32),
         scratch_shapes=[pltpu.VMEM((lats, depth), bf16), pltpu.SemaphoreType.DMA],
-    )
-    back = lax.all_to_all(out.astype(f16), "x", 0, 0, tiled=True).astype(f32)
-    (half,) = call(along_x, [((2 * chunk + EXTRA, both_lats), f32)], back)
+        compiler_params=PARAMS,
+        cost_estimate=pl.CostEstimate(
+            flops=2 * wide * depth * both_lats,
+            bytes_accessed=2 * (wide + both_lats) * depth + 4 * wide * both_lats,
+            transcendentals=0,
+        ),
+    )(got, w_own, w_other, tops, base)
+    terms_in = lax.all_to_all(term.astype(f16), "x", 0, 0, tiled=True).astype(f32)
+
+    half, weights = call(
+        pre_along_x, [((chunk + EXTRA, both_lats), f32), ((EXTRA, both_lats), f32)], pre_in
+    )
     half = lax.optimization_barrier(half.astype(f16))
     partner = lax.ppermute(half, "yh", SWAP)
+    (term_half,) = call(terms_along_x, [((chunk, both_lats), f32)], terms_in, weights)
+    term_half = lax.optimization_barrier(term_half.astype(f16))
+    term_partner = lax.ppermute(term_half, "yh", SWAP)
+    pull, weights = call(
+        penalties,
+        [((chunk, both_lats), f32), ((EXTRA, both_lats), f32)],
+        half.astype(f32), partner.astype(f32), gates, b_both,
+    )
     (grad,) = call(
-        middle, [((X, chunk, both_lats), bf16)], half.astype(f32), partner.astype(f32), gates, b_both
+        gradient,
+        [((X, chunk, both_lats), bf16)],
+        term_half.astype(f32), term_partner.astype(f32), weights, pull, gates,
     )
     grad = lax.all_to_all(grad, "x", 0, 0, tiled=True).reshape(wide, both_lats)
     sent, keep, away = call(

time: 125 us -> 127 us (1.016)
  blocking collectives: 26.3 us -> 10.6 us
  starting transfers between devices: 34.6 us -> 47.8 us
  waiting for transfers between devices: 43.7 us -> 46.6 us
  other arithmetic: 6.83 us -> 8.65 us
  Pallas kernels: 8.4 us -> 6.92 us
    all_to_all x1 -> x0, blocking collectives: 15.8 us -> none  [local(): back = lax.all_to_all(out.astype(f16), 'x', 0, 0, tiled=True).astype(f32)]
    ppermute x1, waiting for transfers between devices: 13.2 us -> 0.01 us  [local(): partner = lax.ppermute(half, 'yh', SWAP)]
    all_to_all x0 -> x2, starting transfers between devices: none -> 10.4 us  [the longest x1 5.56 us: local(): lax.all_to_all(term.astype(f16), 'x', 0, 0, tiled=True).astype(f32)]
    all_to_all x1, waiting for transfers between devices: 21.5 us -> 28 us  [local(): lax.all_to_all(held, PLANE, 0, 0, tiled=True).reshape(wide, depth + LANES)]
    ppermute x0 -> x1, waiting for transfers between devices: none -> 6.33 us  [local(): term_partner = lax.ppermute(term_half, 'yh', SWAP)]
    ppermute x0 -> x1, starting transfers between devices: none -> 6.23 us  [local(): term_partner = lax.ppermute(term_half, 'yh', SWAP)]
    all_to_all x1, starting transfers between devices: 9.1 us -> 5.19 us  [local(): lax.all_to_all(sent.astype(f16).reshape(PEERS, rows, LANES), PLANE, 0, 0,...]
    all_to_all x0 -> x2, waiting for transfers between devices: none -> 3.23 us  [the longest x1 2.94 us: local(): lax.all_to_all(pre_out.astype(f16), 'x', 0, 0, tiled=True).astype(f32)]
  transfers between devices with their start and end apart: 6 -> 9, of which waited for: 4 -> 6; matrix products, arithmetic and copies ran while one was open for 6% -> 6% of each run, Pallas kernels for 0% -> 2%
where the time goes in v7:
time: 127 us; the launch traced here: 126 us
  starting transfers between devices  47.8 us (38%)
  waiting for transfers between devices  46.6 us (37%)
  blocking collectives  10.6 us (8%)
  other arithmetic  8.65 us (7%)
  Pallas kernels  6.92 us (5%)
  between operations  3.11 us (2%)
  local copies, waits for them, and re-layouts  2.22 us (2%)
    all_to_all x1, waiting for transfers between devices, local(): lax.all_to_all(held, PLANE, 0, 0, tiled=True).reshape(wide, depth + LANES)  28 us
    all_to_all x1, starting transfers between devices, local(): lax.all_to_all(held, PLANE, 0, 0, tiled=True).reshape(wide, depth + LANES)  13.8 us
    all_to_all x1, blocking collectives, local(): grad = lax.all_to_all(grad, 'x', 0, 0, tiled=True).reshape(wide, both_lats)  10.6 us
    all_to_all x1, waiting for transfers between devices, local(): lax.all_to_all(sent.astype(f16).reshape(PEERS, rows, LANES), PLANE, 0, 0,...  8.83 us
    ppermute x1, waiting for transfers between devices, local(): term_partner = lax.ppermute(term_half, 'yh', SWAP)  6.33 us
    ppermute x1, starting transfers between devices, local(): partner = lax.ppermute(half, 'yh', SWAP)  6.23 us
    ppermute x1, starting transfers between devices, local(): term_partner = lax.ppermute(term_half, 'yh', SWAP)  6.23 us
    all_to_all x1, starting transfers between devices, local(): lax.all_to_all(term.astype(f16), 'x', 0, 0, tiled=True).astype(f32)  5.56 us
  transfers between devices with their start and end apart: 9, of which 6 were waited for; matrix products, arithmetic and copies ran while one was open for 6% of the time, Pallas kernels for 2%

profile of v7, /device:TPU:2, one launch (start us, length us, event | category | flops | bytes accessed | tf_op | source)
XLA Modules:
  0.0 125.8 jit_solution(2515357878866575945)
XLA Ops:
  0.6 2.0 %shard_map.94 = bf16[32,8,2688]{2,1,0:T(8,128)(2,1)} custom-call(bf16[8,2304]{1,0:T(8,128)(2,1)} %bitcast.40, bf16[8,2,288]{2,1,0:T(2,128)(2,1)} %inputs_far.1), custom_call_target="tpu_custom_call" | custom-call | tf_op jit(solution)/shard_map/pallas_call | solution.py:186
  2.6 1.9 %collective-permute-start.1 = (bf16[512,2304]{1,0:T(8,128)(2,1)}, bf16[512,2304]{1,0:T(8,128)(2,1)}, u32[]{:S(2)}, u32[]{:S(2)}) collective-permute-start(bf16[512,2304]{1,0:T(8,128)(2,1)} %bitcast.35), channel_id=1, source_target_pairs={{0,8},{8,0},{1,9},{9,1},{2,10},{10,2},{3,11},{11,3},{4,12},{12,4},... | collective-permute-start | bytes 7077896 | tf_op jit(solution)/shard_map/ppermute | solution.py:206
  4.6 13.8 %all-to-all-start = ((bf16[32,8,2688]{2,1,0:T(8,128)(2,1)}), bf16[32,8,2688]{2,1,0:T(8,128)(2,1)S(1)}, u32[]{:S(2)}, u32[]{:S(2)}) async-start(bf16[32,8,2688]{2,1,0:T(8,128)(2,1)} %shard_map.94), calls=%async_computation | async-start | bytes 2752512 | tf_op jit(solution)/shard_map/all_to_all | solution.py:198
  18.3 0.0 copy-start.2
  18.4 0.0 copy-start.1
  18.4 0.0 copy-start.3
  18.4 2.2 %fusion = f32[512]{0:T(512)S(1)} fusion(bf16[1,512,2304]{2,1,0:T(8,128)(2,1)} %param.11), kind=kLoop, calls=%fused_computation.1 | loop fusion | flops 3538432 | bytes 2361344 | tf_op jit(solution)/shard_map/cd,cd->c/dot_general | solution.py:205
  20.6 0.0 copy-done.2
  20.7 1.0 fusion.3
  21.8 0.3 concatenate.37
  22.1 2.1 %collective-permute-start = (bf16[464,512]{1,0:T(8,128)(2,1)S(1)}, bf16[464,512]{1,0:T(8,128)(2,1)S(1)}, u32[]{:S(2)}, u32[]{:S(2)}) collective-permute-start(bf16[464,512]{1,0:T(8,128)(2,1)S(1)} %concatenate.37), channel_id=1, source_target_pairs={{0,8},{8,0},{1,9},{9,1},{2,10},{10,2},{3,11},{11,3},{4,12},{12,4},... | collective-permute-start | bytes 1425416 | tf_op jit(solution)/shard_map/ppermute | solution.py:218
  24.2 0.6 fusion.10
  25.5 0.1 pad.12.clone
  25.6 0.2 collective-permute-done
  25.9 0.6 fusion.6
  27.9 0.1 pad.11.clone
  28.0 0.1 maximum_bitcast_fusion.base
  28.1 0.1 fusion.2.enc_both
  28.3 0.1 maximum_maximum_fusion.lines
  28.3 0.0 collective-permute-done.1.w_far
  28.3 28.0 %all-to-all-done = bf16[32,8,2688]{2,1,0:T(8,128)(2,1)S(1)} async-done(((bf16[32,8,2688]{2,1,0:T(8,128)(2,1)}), bf16[32,8,2688]{2,1,0:T(8,128)(2,1)S(1)}, u32[]{:S(2)}, u32[]{:S(2)}) %all-to-all-start) | async-done | bytes 1376288 | tf_op jit(solution)/shard_map/all_to_all | solution.py:198
  56.3 0.5 shard_map.95
  56.8 0.9 convert_element_type.131
  57.7 4.8 %all-to-all-start.2 = ((f16[4,72,1024]{2,1,0:T(8,128)(2,1)}), f16[4,72,1024]{2,1,0:T(8,128)(2,1)S(1)}, u32[]{:S(2)}, u32[]{:S(2)}) async-start(f16[4,72,1024]{2,1,0:T(8,128)(2,1)} %convert_element_type.131), calls=%async_computation.2 | async-start | bytes 1179648 | tf_op jit(solution)/shard_map/all_to_all | solution.py:265
  62.5 1.7 %copy-done = bf16[1,512,2304]{2,1,0:T(8,128)(2,1)S(1)} copy-done((bf16[1,512,2304]{2,1,0:T(8,128)(2,1)S(1)}, bf16[1,512,2304]{2,1,0:T(8,128)(2,1)}, u32[]{:S(2)}) %copy-start) | copy-done | bytes 2359320
  64.2 2.5 %shard_map.96 = f32[4,64,1024]{2,1,0:T(8,128)S(1)} custom-call(bf16[256,2688]{1,0:T(8,128)(2,1)S(1)} %bitcast.34, bf16[512,2304]{1,0:T(8,128)(2,1)S(1)} %bitcast.36, bf16[512,2304]{1,0:T(8,128)(2,1)} %collective-permute-done.1.w_far, f32[8,128]{1,0:T(8,128)S(1)} %get-tuple-element.34.tops, f32[1,2]{1,0:T(1,128)S(1)} %maximum_bitcast_fusion.base), custom_call_target="tpu_custom_call" | custom-call | flops 1207959552 | bytes 6946816 | tf_op jit(solution)/shard_map/pallas_call | solution.py:266
  66.7 0.9 convert_element_type.129
  67.6 2.9 %all-to-all-done.2 = f16[4,72,1024]{2,1,0:T(8,128)(2,1)S(1)} async-done(((f16[4,72,1024]{2,1,0:T(8,128)(2,1)}), f16[4,72,1024]{2,1,0:T(8,128)(2,1)S(1)}, u32[]{:S(2)}, u32[]{:S(2)}) %all-to-all-start.2) | async-done | bytes 589856 | tf_op jit(solution)/shard_map/all_to_all | solution.py:265
  70.5 5.6 %all-to-all-start.1 = ((f16[4,64,1024]{2,1,0:T(8,128)(2,1)}), f16[4,64,1024]{2,1,0:T(8,128)(2,1)}, u32[]{:S(2)}, u32[]{:S(2)}) async-start(f16[4,64,1024]{2,1,0:T(8,128)(2,1)} %convert_element_type.129), calls=%async_computation.1 | async-start | bytes 1048576 | tf_op jit(solution)/shard_map/all_to_all | solution.py:286
  76.1 0.1 convert_element_type.132.back
  76.2 0.1 shard_map.97
  76.3 6.2 %collective-permute-start.3 = (f16[72,1024]{1,0:T(8,128)(2,1)S(1)}, f16[72,1024]{1,0:T(8,128)(2,1)S(1)}, u32[]{:S(2)}, u32[]{:S(2)}) collective-permute-start(f16[72,1024]{1,0:T(8,128)(2,1)S(1)} %convert_element_type.136), channel_id=1, source_target_pairs={{0,4},{4,0},{1,5},{5,1},{2,6},{6,2},{3,7},{7,3},{8,12},{12,8},{9,1... | collective-permute-start | bytes 442376 | tf_op jit(solution)/shard_map/ppermute | solution.py:292
  82.5 0.3 all-to-all-done.1
  82.8 1.1 convert_element_type.130.back
  84.0 0.1 shard_map.98
  84.1 6.2 %collective-permute-start.2 = (f16[64,1024]{1,0:T(8,128)(2,1)S(1)}, f16[64,1024]{1,0:T(8,128)(2,1)S(1)}, u32[]{:S(2)}, u32[]{:S(2)}) collective-permute-start(f16[64,1024]{1,0:T(8,128)(2,1)S(1)} %convert_element_type.133), channel_id=1, source_target_pairs={{0,4},{4,0},{1,5},{5,1},{2,6},{6,2},{3,7},{7,3},{8,12},{12,8},{9,1... | collective-permute-start | bytes 393224 | tf_op jit(solution)/shard_map/ppermute | solution.py:295
  90.4 6.3 %collective-permute-done.2 = f16[64,1024]{1,0:T(8,128)(2,1)S(1)} collective-permute-done((f16[64,1024]{1,0:T(8,128)(2,1)S(1)}, f16[64,1024]{1,0:T(8,128)(2,1)S(1)}, u32[]{:S(2)}, u32[]{:S(2)}) %collective-permute-start.2) | collective-permute-done | bytes 131104 | tf_op jit(solution)/shard_map/ppermute | solution.py:295
  96.7 0.0 collective-permute-done.3
  96.7 0.1 shard_map.99
  96.9 0.1 shard_map.100
  97.0 10.6 %all_to_all.25 = bf16[4,64,1024]{2,1,0:T(8,128)(2,1)S(1)} all-to-all(bf16[4,64,1024]{2,1,0:T(8,128)(2,1)S(1)} %shard_map.100), channel_id=1, replica_groups=mesh['yl'=4,'z'=8,'c'=2,'yh'=2,'x'=4] {'x'}, dimensions={0} | all-to-all | bytes 1048576 | tf_op jit(solution)/shard_map/all_to_all | solution.py:306
  107.5 0.6 shard_map.101
  108.2 0.7 convert_bitcast_fusion
  108.9 5.2 %all-to-all-start.4 = ((f16[32,8,384]{2,1,0:T(8,128)(2,1)}), f16[32,8,384]{2,1,0:T(8,128)(2,1)S(1)}, u32[]{:S(2)}, u32[]{:S(2)}) async-start(f16[32,8,384]{2,1,0:T(8,128)(2,1)} %convert_bitcast_fusion), calls=%async_computation.4 | async-start | bytes 393216 | tf_op jit(solution)/shard_map/all_to_all | solution.py:313
  114.1 1.9 %collective-permute-start.4 = (f32[296,512]{1,0:T(8,128)S(1)}, f32[296,512]{1,0:T(8,128)S(1)}, u32[]{:S(2)}, u32[]{:S(2)}) collective-permute-start(f32[296,512]{1,0:T(8,128)S(1)} %get-tuple-element.45), channel_id=1, source_target_pairs={{0,8},{8,0},{1,9},{9,1},{2,10},{10,2},{3,11},{11,3},{4,12},{12,4},... | collective-permute-start | bytes 1818632 | tf_op jit(solution)/shard_map/ppermute | solution.py:312
  116.0 8.8 %all-to-all-done.4 = f16[32,8,384]{2,1,0:T(8,128)(2,1)S(1)} async-done(((f16[32,8,384]{2,1,0:T(8,128)(2,1)}), f16[32,8,384]{2,1,0:T(8,128)(2,1)S(1)}, u32[]{:S(2)}, u32[]{:S(2)}) %all-to-all-start.4) | async-done | bytes 196640 | tf_op jit(solution)/shard_map/all_to_all | solution.py:313
  124.9 0.0 collective-permute-done.4.far
  124.9 1.0 shard_map.102
  (31 shorter events, 0.3 us)
Async XLA Ops:
  2.6 25.7 %collective-permute-start.1 = (bf16[512,2304]{1,0:T(8,128)(2,1)}, bf16[512,2304]{1,0:T(8,128)(2,1)}, u32[]{:S(2)}, u32[]{:S(2)}) collective-permute-start(bf16[512,2304]{1,0:T(8,128)(2,1)} %bitcast.35), channel_id=1, source_target_pairs={{0,8},{8,0},{1,9},{9,1},{2,10},{10,2},{3,11},{11,3},{4,12},{12,4},... | collective-permute-start | bytes 7077896 | tf_op jit(solution)/shard_map/ppermute | solution.py:206
  4.6 51.8 %all-to-all-start = ((bf16[32,8,2688]{2,1,0:T(8,128)(2,1)}), bf16[32,8,2688]{2,1,0:T(8,128)(2,1)S(1)}, u32[]{:S(2)}, u32[]{:S(2)}) async-start(bf16[32,8,2688]{2,1,0:T(8,128)(2,1)} %shard_map.94), calls=%async_computation | async-start | bytes 2752512 | tf_op jit(solution)/shard_map/all_to_all | solution.py:198
  18.3 2.3 %copy-start.2 = (f32[512]{0:T(512)S(1)}, f32[512]{0:T(512)}, u32[]{:S(2)}) copy-start(f32[512]{0:T(512)} %param.9) | copy-start | bytes 6148
  18.4 3.4 %copy-start.1 = (bf16[288,512]{1,0:T(8,128)(2,1)S(1)}, bf16[288,512]{1,0:T(8,128)(2,1)}, u32[]{:S(2)}) copy-start(bf16[288,512]{1,0:T(8,128)(2,1)} %param.8) | copy-start | bytes 884740
  18.4 5.9 %copy-start.3 = (s32[8]{0:T(128)S(1)}, s32[8]{0:T(128)}, u32[]{:S(2)}) copy-start(s32[8]{0:T(128)} %param.13) | copy-start | bytes 100
  22.1 3.7 %collective-permute-start = (bf16[464,512]{1,0:T(8,128)(2,1)S(1)}, bf16[464,512]{1,0:T(8,128)(2,1)S(1)}, u32[]{:S(2)}, u32[]{:S(2)}) collective-permute-start(bf16[464,512]{1,0:T(8,128)(2,1)S(1)} %concatenate.37), channel_id=1, source_target_pairs={{0,8},{8,0},{1,9},{9,1},{2,10},{10,2},{3,11},{11,3},{4,12},{12,4},... | collective-permute-start | bytes 1425416 | tf_op jit(solution)/shard_map/ppermute | solution.py:218
  57.7 12.8 %all-to-all-start.2 = ((f16[4,72,1024]{2,1,0:T(8,128)(2,1)}), f16[4,72,1024]{2,1,0:T(8,128)(2,1)S(1)}, u32[]{:S(2)}, u32[]{:S(2)}) async-start(f16[4,72,1024]{2,1,0:T(8,128)(2,1)} %convert_element_type.131), calls=%async_computation.2 | async-start | bytes 1179648 | tf_op jit(solution)/shard_map/all_to_all | solution.py:265
  62.5 1.7 %copy-start = (bf16[1,512,2304]{2,1,0:T(8,128)(2,1)S(1)}, bf16[1,512,2304]{2,1,0:T(8,128)(2,1)}, u32[]{:S(2)}) copy-start(bf16[1,512,2304]{2,1,0:T(8,128)(2,1)} %param.11) | copy-start | bytes 7077892
  70.5 12.3 %all-to-all-start.1 = ((f16[4,64,1024]{2,1,0:T(8,128)(2,1)}), f16[4,64,1024]{2,1,0:T(8,128)(2,1)}, u32[]{:S(2)}, u32[]{:S(2)}) async-start(f16[4,64,1024]{2,1,0:T(8,128)(2,1)} %convert_element_type.129), calls=%async_computation.1 | async-start | bytes 1048576 | tf_op jit(solution)/shard_map/all_to_all | solution.py:286
  76.3 20.4 %collective-permute-start.3 = (f16[72,1024]{1,0:T(8,128)(2,1)S(1)}, f16[72,1024]{1,0:T(8,128)(2,1)S(1)}, u32[]{:S(2)}, u32[]{:S(2)}) collective-permute-start(f16[72,1024]{1,0:T(8,128)(2,1)S(1)} %convert_element_type.136), channel_id=1, source_target_pairs={{0,4},{4,0},{1,5},{5,1},{2,6},{6,2},{3,7},{7,3},{8,12},{12,8},{9,1... | collective-permute-start | bytes 442376 | tf_op jit(solution)/shard_map/ppermute | solution.py:292
  84.1 12.6 %collective-permute-start.2 = (f16[64,1024]{1,0:T(8,128)(2,1)S(1)}, f16[64,1024]{1,0:T(8,128)(2,1)S(1)}, u32[]{:S(2)}, u32[]{:S(2)}) collective-permute-start(f16[64,1024]{1,0:T(8,128)(2,1)S(1)} %convert_element_type.133), channel_id=1, source_target_pairs={{0,4},{4,0},{1,5},{5,1},{2,6},{6,2},{3,7},{7,3},{8,12},{12,8},{9,1... | collective-permute-start | bytes 393224 | tf_op jit(solution)/shard_map/ppermute | solution.py:295
  108.9 16.0 %all-to-all-start.4 = ((f16[32,8,384]{2,1,0:T(8,128)(2,1)}), f16[32,8,384]{2,1,0:T(8,128)(2,1)S(1)}, u32[]{:S(2)}, u32[]{:S(2)}) async-start(f16[32,8,384]{2,1,0:T(8,128)(2,1)} %convert_bitcast_fusion), calls=%async_computation.4 | async-start | bytes 393216 | tf_op jit(solution)/shard_map/all_to_all | solution.py:313
  114.1 10.8 %collective-permute-start.4 = (f32[296,512]{1,0:T(8,128)S(1)}, f32[296,512]{1,0:T(8,128)S(1)}, u32[]{:S(2)}, u32[]{:S(2)}) collective-permute-start(f32[296,512]{1,0:T(8,128)S(1)} %get-tuple-element.45), channel_id=1, source_target_pairs={{0,8},{8,0},{1,9},{9,1},{2,10},{10,2},{3,11},{11,3},{4,12},{12,4},... | collective-permute-start | bytes 1818632 | tf_op jit(solution)/shard_map/ppermute | solution.py:312

commit v8 on v7

--- a/solution.py
+++ b/solution.py
@@ -203,7 +203,6 @@
     gates_send = lax.dynamic_index_in_dim(gates5, 1 - core, 1, keepdims=False).reshape(chunk, lats)
     w_own = w_dec[0]
     square = jnp.einsum("cd,cd->c", w_own, w_own, preferred_element_type=f32)
-    w_other = lax.ppermute(w_own, "c", SWAP)
     pack = jnp.concatenate(
         [
             w_enc,
@@ -216,6 +215,8 @@
         axis=0,
     )
     pack_other = lax.ppermute(pack, "c", SWAP)
+    w_late, pack_other = lax.optimization_barrier((w_own, pack_other))
+    w_other = lax.ppermute(w_late, "c", SWAP)
     enc_both = jnp.concatenate([pack[:LANES], pack_other[:LANES]], axis=1)
     gates_other = pack_other[LANES : LANES + chunk].astype(f32)
     gates = jnp.concatenate([gates_own.astype(f32), gates_other], axis=1)
@@ -240,8 +241,8 @@
         axis=0,
     )
     base = jnp.stack([jnp.sqrt(depth * 1.01 * top_sq), flag])[None]
-    lines, base, enc_both, gates, b_both, w_other, got = lax.optimization_barrier(
-        (lines, base, enc_both, gates, b_both, w_other, got)
+    lines, base, enc_both, gates, b_both, got = lax.optimization_barrier(
+        (lines, base, enc_both, gates, b_both, got)
     )
 
     whole = lambda shape: pl.BlockSpec(shape, lambda i: (0,) * len(shape))

time: 127 us -> 123 us (0.969)
  waiting for transfers between devices: 46.6 us -> 41.1 us
  blocking collectives: 10.6 us -> 12.3 us
    all_to_all x1, waiting for transfers between devices: 28 us -> 21.4 us  [local(): lax.all_to_all(held, PLANE, 0, 0, tiled=True).reshape(wide, depth + LANES)]
    all_to_all x1, blocking collectives: 10.6 us -> 12.3 us  [local(): grad = lax.all_to_all(grad, 'x', 0, 0, tiled=True).reshape(wide, both_lats)]
    ppermute x1, waiting for transfers between devices: 0.2 us -> 1.81 us  [local(): pack_other = lax.ppermute(pack, 'c', SWAP)]
  transfers between devices with their start and end apart: 9 -> 9, of which waited for: 6 -> 6; matrix products, arithmetic and copies ran while one was open for 6% -> 8% of each run, Pallas kernels for 2% -> 3%
where the time goes in v8:
time: 123 us; the launch traced here: 122 us
  starting transfers between devices  47.4 us (39%)
  waiting for transfers between devices  41.1 us (33%)
  blocking collectives  12.3 us (10%)
  other arithmetic  9.49 us (8%)
  Pallas kernels  6.88 us (6%)
  between operations  3.14 us (3%)
  local copies, waits for them, and re-layouts  2.22 us (2%)
    all_to_all x1, waiting for transfers between devices, local(): lax.all_to_all(held, PLANE, 0, 0, tiled=True).reshape(wide, depth + LANES)  21.4 us
    all_to_all x1, starting transfers between devices, local(): lax.all_to_all(held, PLANE, 0, 0, tiled=True).reshape(wide, depth + LANES)  13.8 us
    all_to_all x1, blocking collectives, local(): grad = lax.all_to_all(grad, 'x', 0, 0, tiled=True).reshape(wide, both_lats)  12.3 us
    all_to_all x1, waiting for transfers between devices, local(): lax.all_to_all(sent.astype(f16).reshape(PEERS, rows, LANES), PLANE, 0, 0,...  8.83 us
    all_to_all x1, starting transfers between devices, local(): lax.all_to_all(sent.astype(f16).reshape(PEERS, rows, LANES), PLANE, 0, 0,...  6.43 us
    ppermute x1, waiting for transfers between devices, local(): term_partner = lax.ppermute(term_half, 'yh', SWAP)  6.07 us
    all_to_all x1, starting transfers between devices, local(): lax.all_to_all(term.astype(f16), 'x', 0, 0, tiled=True).astype(f32)  5.56 us
    ppermute x1, starting transfers between devices, local(): partner = lax.ppermute(half, 'yh', SWAP)  5.45 us
  transfers between devices with their start and end apart: 9, of which 6 were waited for; matrix products, arithmetic and copies ran while one was open for 8% of the time, Pallas kernels for 3%

profile of v8, /device:TPU:2, one launch (start us, length us, event | category | flops | bytes accessed | tf_op | source)
XLA Modules:
  0.0 122.4 jit_solution(6257129225652673338)
XLA Ops:
  0.6 2.0 %shard_map.94 = bf16[32,8,2688]{2,1,0:T(8,128)(2,1)} custom-call(bf16[8,2304]{1,0:T(8,128)(2,1)} %bitcast.40, bf16[8,2,288]{2,1,0:T(2,128)(2,1)} %inputs_far.1), custom_call_target="tpu_custom_call" | custom-call | tf_op jit(solution)/shard_map/pallas_call | solution.py:186
  2.6 0.0 copy-start.3
  2.7 13.8 %all-to-all-start = ((bf16[32,8,2688]{2,1,0:T(8,128)(2,1)}), bf16[32,8,2688]{2,1,0:T(8,128)(2,1)S(1)}, u32[]{:S(2)}, u32[]{:S(2)}) async-start(bf16[32,8,2688]{2,1,0:T(8,128)(2,1)} %shard_map.94), calls=%async_computation | async-start | bytes 2752512 | tf_op jit(solution)/shard_map/all_to_all | solution.py:198
  16.4 0.0 copy-start.1
  16.5 0.0 copy-start.4
  16.5 2.2 %fusion = f32[512]{0:T(512)S(1)} fusion(bf16[1,512,2304]{2,1,0:T(8,128)(2,1)} %param.11), kind=kLoop, calls=%fused_computation.1 | loop fusion | flops 3538432 | bytes 2361344 | tf_op jit(solution)/shard_map/cd,cd->c/dot_general | solution.py:205
  18.8 1.0 fusion.3
  19.8 0.3 concatenate.37
  20.1 1.9 %collective-permute-start = (bf16[464,512]{1,0:T(8,128)(2,1)S(1)}, bf16[464,512]{1,0:T(8,128)(2,1)S(1)}, u32[]{:S(2)}, u32[]{:S(2)}) collective-permute-start(bf16[464,512]{1,0:T(8,128)(2,1)S(1)} %concatenate.37), channel_id=1, source_target_pairs={{0,8},{8,0},{1,9},{9,1},{2,10},{10,2},{3,11},{11,3},{4,12},{12,4},... | collective-permute-start | bytes 1425416 | tf_op jit(solution)/shard_map/ppermute | solution.py:217
  22.1 1.8 %collective-permute-done = bf16[464,512]{1,0:T(8,128)(2,1)S(1)} collective-permute-done((bf16[464,512]{1,0:T(8,128)(2,1)S(1)}, bf16[464,512]{1,0:T(8,128)(2,1)S(1)}, u32[]{:S(2)}, u32[]{:S(2)}) %collective-permute-start) | collective-permute-done | bytes 475168 | tf_op jit(solution)/shard_map/ppermute | solution.py:217
  23.9 2.0 %collective-permute-start.1 = (bf16[512,2304]{1,0:T(8,128)(2,1)}, bf16[512,2304]{1,0:T(8,128)(2,1)}, u32[]{:S(2)}, u32[]{:S(2)}) collective-permute-start(bf16[512,2304]{1,0:T(8,128)(2,1)} %bitcast.35), channel_id=1, source_target_pairs={{0,8},{8,0},{1,9},{9,1},{2,10},{10,2},{3,11},{11,3},{4,12},{12,4},... | collective-permute-start | bytes 7077896 | tf_op jit(solution)/shard_map/ppermute | solution.py:219
  26.0 0.6 fusion.10
  27.2 0.1 pad.12.clone
  27.4 0.6 fusion.6
  29.4 0.1 pad.11.clone
  29.5 0.1 maximum_bitcast_fusion.base
  29.6 0.9 slice_convert_fusion
  30.5 0.1 fusion.2.enc_both
  30.6 0.1 maximum_maximum_fusion.lines
  30.7 21.4 %all-to-all-done = bf16[32,8,2688]{2,1,0:T(8,128)(2,1)S(1)} async-done(((bf16[32,8,2688]{2,1,0:T(8,128)(2,1)}), bf16[32,8,2688]{2,1,0:T(8,128)(2,1)S(1)}, u32[]{:S(2)}, u32[]{:S(2)}) %all-to-all-start) | async-done | bytes 1376288 | tf_op jit(solution)/shard_map/all_to_all | solution.py:198
  52.0 0.5 shard_map.95
  52.5 0.9 convert_element_type.131
  53.4 4.8 %all-to-all-start.2 = ((f16[4,72,1024]{2,1,0:T(8,128)(2,1)}), f16[4,72,1024]{2,1,0:T(8,128)(2,1)S(1)}, u32[]{:S(2)}, u32[]{:S(2)}) async-start(f16[4,72,1024]{2,1,0:T(8,128)(2,1)} %convert_element_type.131), calls=%async_computation.2 | async-start | bytes 1179648 | tf_op jit(solution)/shard_map/all_to_all | solution.py:266
  58.2 0.0 collective-permute-done.1.w_far
  58.2 1.7 %copy-done = bf16[1,512,2304]{2,1,0:T(8,128)(2,1)S(1)} copy-done((bf16[1,512,2304]{2,1,0:T(8,128)(2,1)S(1)}, bf16[1,512,2304]{2,1,0:T(8,128)(2,1)}, u32[]{:S(2)}) %copy-start) | copy-done | bytes 2359320
  59.9 2.5 %shard_map.96 = f32[4,64,1024]{2,1,0:T(8,128)S(1)} custom-call(bf16[256,2688]{1,0:T(8,128)(2,1)S(1)} %bitcast.34, bf16[512,2304]{1,0:T(8,128)(2,1)S(1)} %bitcast.36, bf16[512,2304]{1,0:T(8,128)(2,1)} %collective-permute-done.1.w_far, f32[8,128]{1,0:T(8,128)S(1)} %get-tuple-element.36.tops, f32[1,2]{1,0:T(1,128)S(1)} %maximum_bitcast_fusion.base), custom_call_target="tpu_custom_call" | custom-call | flops 1207959552 | bytes 6946816 | tf_op jit(solution)/shard_map/pallas_call | solution.py:267
  62.4 0.9 convert_element_type.129
  63.3 1.9 %all-to-all-done.2 = f16[4,72,1024]{2,1,0:T(8,128)(2,1)S(1)} async-done(((f16[4,72,1024]{2,1,0:T(8,128)(2,1)}), f16[4,72,1024]{2,1,0:T(8,128)(2,1)S(1)}, u32[]{:S(2)}, u32[]{:S(2)}) %all-to-all-start.2) | async-done | bytes 589856 | tf_op jit(solution)/shard_map/all_to_all | solution.py:266
  65.2 5.6 %all-to-all-start.1 = ((f16[4,64,1024]{2,1,0:T(8,128)(2,1)}), f16[4,64,1024]{2,1,0:T(8,128)(2,1)}, u32[]{:S(2)}, u32[]{:S(2)}) async-start(f16[4,64,1024]{2,1,0:T(8,128)(2,1)} %convert_element_type.129), calls=%async_computation.1 | async-start | bytes 1048576 | tf_op jit(solution)/shard_map/all_to_all | solution.py:287
  70.8 0.1 convert_element_type.132.back
  70.9 0.1 shard_map.97
  71.0 5.5 %collective-permute-start.3 = (f16[72,1024]{1,0:T(8,128)(2,1)S(1)}, f16[72,1024]{1,0:T(8,128)(2,1)S(1)}, u32[]{:S(2)}, u32[]{:S(2)}) collective-permute-start(f16[72,1024]{1,0:T(8,128)(2,1)S(1)} %convert_element_type.136), channel_id=1, source_target_pairs={{0,4},{4,0},{1,5},{5,1},{2,6},{6,2},{3,7},{7,3},{8,12},{12,8},{9,1... | collective-permute-start | bytes 442376 | tf_op jit(solution)/shard_map/ppermute | solution.py:293
  76.5 1.1 all-to-all-done.1
  77.5 1.1 convert_element_type.130.back
  78.6 0.1 shard_map.98
  78.7 5.5 %collective-permute-start.2 = (f16[64,1024]{1,0:T(8,128)(2,1)S(1)}, f16[64,1024]{1,0:T(8,128)(2,1)S(1)}, u32[]{:S(2)}, u32[]{:S(2)}) collective-permute-start(f16[64,1024]{1,0:T(8,128)(2,1)S(1)} %convert_element_type.133), channel_id=1, source_target_pairs={{0,4},{4,0},{1,5},{5,1},{2,6},{6,2},{3,7},{7,3},{8,12},{12,8},{9,1... | collective-permute-start | bytes 393224 | tf_op jit(solution)/shard_map/ppermute | solution.py:296
  84.3 0.0 collective-permute-done.3
  84.3 0.1 shard_map.99
  84.4 6.1 %collective-permute-done.2 = f16[64,1024]{1,0:T(8,128)(2,1)S(1)} collective-permute-done((f16[64,1024]{1,0:T(8,128)(2,1)S(1)}, f16[64,1024]{1,0:T(8,128)(2,1)S(1)}, u32[]{:S(2)}, u32[]{:S(2)}) %collective-permute-start.2) | collective-permute-done | bytes 131104 | tf_op jit(solution)/shard_map/ppermute | solution.py:296
  90.5 0.1 shard_map.100
  90.6 12.3 %all_to_all.25 = bf16[4,64,1024]{2,1,0:T(8,128)(2,1)S(1)} all-to-all(bf16[4,64,1024]{2,1,0:T(8,128)(2,1)S(1)} %shard_map.100), channel_id=1, replica_groups=mesh['yl'=4,'z'=8,'c'=2,'yh'=2,'x'=4] {'x'}, dimensions={0} | all-to-all | bytes 1048576 | tf_op jit(solution)/shard_map/all_to_all | solution.py:307
  102.9 0.7 shard_map.101
  103.5 0.7 convert_bitcast_fusion
  104.2 6.4 %all-to-all-start.4 = ((f16[32,8,384]{2,1,0:T(8,128)(2,1)}), f16[32,8,384]{2,1,0:T(8,128)(2,1)S(1)}, u32[]{:S(2)}, u32[]{:S(2)}) async-start(f16[32,8,384]{2,1,0:T(8,128)(2,1)} %convert_bitcast_fusion), calls=%async_computation.4 | async-start | bytes 393216 | tf_op jit(solution)/shard_map/all_to_all | solution.py:314
  110.7 1.9 %collective-permute-start.4 = (f32[296,512]{1,0:T(8,128)S(1)}, f32[296,512]{1,0:T(8,128)S(1)}, u32[]{:S(2)}, u32[]{:S(2)}) collective-permute-start(f32[296,512]{1,0:T(8,128)S(1)} %get-tuple-element.47), channel_id=1, source_target_pairs={{0,8},{8,0},{1,9},{9,1},{2,10},{10,2},{3,11},{11,3},{4,12},{12,4},... | collective-permute-start | bytes 1818632 | tf_op jit(solution)/shard_map/ppermute | solution.py:313
  112.6 8.8 %all-to-all-done.4 = f16[32,8,384]{2,1,0:T(8,128)(2,1)S(1)} async-done(((f16[32,8,384]{2,1,0:T(8,128)(2,1)}), f16[32,8,384]{2,1,0:T(8,128)(2,1)S(1)}, u32[]{:S(2)}, u32[]{:S(2)}) %all-to-all-start.4) | async-done | bytes 196640 | tf_op jit(solution)/shard_map/all_to_all | solution.py:314
  121.4 0.0 collective-permute-done.4.far
  121.5 1.0 shard_map.102
  (33 shorter events, 0.3 us)
Async XLA Ops:
  2.6 13.8 %copy-start.3 = (f32[512]{0:T(512)S(1)}, f32[512]{0:T(512)}, u32[]{:S(2)}) copy-start(f32[512]{0:T(512)} %param.9) | copy-start | bytes 6148
  2.7 49.4 %all-to-all-start = ((bf16[32,8,2688]{2,1,0:T(8,128)(2,1)}), bf16[32,8,2688]{2,1,0:T(8,128)(2,1)S(1)}, u32[]{:S(2)}, u32[]{:S(2)}) async-start(bf16[32,8,2688]{2,1,0:T(8,128)(2,1)} %shard_map.94), calls=%async_computation | async-start | bytes 2752512 | tf_op jit(solution)/shard_map/all_to_all | solution.py:198
  16.4 3.4 %copy-start.1 = (bf16[288,512]{1,0:T(8,128)(2,1)S(1)}, bf16[288,512]{1,0:T(8,128)(2,1)}, u32[]{:S(2)}) copy-start(bf16[288,512]{1,0:T(8,128)(2,1)} %param.8) | copy-start | bytes 884740
  16.5 9.5 %copy-start.4 = (s32[8]{0:T(128)S(1)}, s32[8]{0:T(128)}, u32[]{:S(2)}) copy-start(s32[8]{0:T(128)} %param.13) | copy-start | bytes 100
  20.1 3.7 %collective-permute-start = (bf16[464,512]{1,0:T(8,128)(2,1)S(1)}, bf16[464,512]{1,0:T(8,128)(2,1)S(1)}, u32[]{:S(2)}, u32[]{:S(2)}) collective-permute-start(bf16[464,512]{1,0:T(8,128)(2,1)S(1)} %concatenate.37), channel_id=1, source_target_pairs={{0,8},{8,0},{1,9},{9,1},{2,10},{10,2},{3,11},{11,3},{4,12},{12,4},... | collective-permute-start | bytes 1425416 | tf_op jit(solution)/shard_map/ppermute | solution.py:217
  23.9 5.7 %copy-start.2 = (bf16[464,512]{1,0:T(8,128)(2,1)}, bf16[464,512]{1,0:T(8,128)(2,1)S(1)}, u32[]{:S(2)}) copy-start(bf16[464,512]{1,0:T(8,128)(2,1)S(1)} %collective-permute-done) | copy-start | bytes 1425412
  23.9 34.4 %collective-permute-start.1 = (bf16[512,2304]{1,0:T(8,128)(2,1)}, bf16[512,2304]{1,0:T(8,128)(2,1)}, u32[]{:S(2)}, u32[]{:S(2)}) collective-permute-start(bf16[512,2304]{1,0:T(8,128)(2,1)} %bitcast.35), channel_id=1, source_target_pairs={{0,8},{8,0},{1,9},{9,1},{2,10},{10,2},{3,11},{11,3},{4,12},{12,4},... | collective-permute-start | bytes 7077896 | tf_op jit(solution)/shard_map/ppermute | solution.py:219
  53.4 11.8 %all-to-all-start.2 = ((f16[4,72,1024]{2,1,0:T(8,128)(2,1)}), f16[4,72,1024]{2,1,0:T(8,128)(2,1)S(1)}, u32[]{:S(2)}, u32[]{:S(2)}) async-start(f16[4,72,1024]{2,1,0:T(8,128)(2,1)} %convert_element_type.131), calls=%async_computation.2 | async-start | bytes 1179648 | tf_op jit(solution)/shard_map/all_to_all | solution.py:266
  58.2 1.7 %copy-start = (bf16[1,512,2304]{2,1,0:T(8,128)(2,1)S(1)}, bf16[1,512,2304]{2,1,0:T(8,128)(2,1)}, u32[]{:S(2)}) copy-start(bf16[1,512,2304]{2,1,0:T(8,128)(2,1)} %param.11) | copy-start | bytes 7077892
  65.2 12.3 %all-to-all-start.1 = ((f16[4,64,1024]{2,1,0:T(8,128)(2,1)}), f16[4,64,1024]{2,1,0:T(8,128)(2,1)}, u32[]{:S(2)}, u32[]{:S(2)}) async-start(f16[4,64,1024]{2,1,0:T(8,128)(2,1)} %convert_element_type.129), calls=%async_computation.1 | async-start | bytes 1048576 | tf_op jit(solution)/shard_map/all_to_all | solution.py:287
  71.0 13.3 %collective-permute-start.3 = (f16[72,1024]{1,0:T(8,128)(2,1)S(1)}, f16[72,1024]{1,0:T(8,128)(2,1)S(1)}, u32[]{:S(2)}, u32[]{:S(2)}) collective-permute-start(f16[72,1024]{1,0:T(8,128)(2,1)S(1)} %convert_element_type.136), channel_id=1, source_target_pairs={{0,4},{4,0},{1,5},{5,1},{2,6},{6,2},{3,7},{7,3},{8,12},{12,8},{9,1... | collective-permute-start | bytes 442376 | tf_op jit(solution)/shard_map/ppermute | solution.py:293
  78.7 11.7 %collective-permute-start.2 = (f16[64,1024]{1,0:T(8,128)(2,1)S(1)}, f16[64,1024]{1,0:T(8,128)(2,1)S(1)}, u32[]{:S(2)}, u32[]{:S(2)}) collective-permute-start(f16[64,1024]{1,0:T(8,128)(2,1)S(1)} %convert_element_type.133), channel_id=1, source_target_pairs={{0,4},{4,0},{1,5},{5,1},{2,6},{6,2},{3,7},{7,3},{8,12},{12,8},{9,1... | collective-permute-start | bytes 393224 | tf_op jit(solution)/shard_map/ppermute | solution.py:296
  104.2 17.2 %all-to-all-start.4 = ((f16[32,8,384]{2,1,0:T(8,128)(2,1)}), f16[32,8,384]{2,1,0:T(8,128)(2,1)S(1)}, u32[]{:S(2)}, u32[]{:S(2)}) async-start(f16[32,8,384]{2,1,0:T(8,128)(2,1)} %convert_bitcast_fusion), calls=%async_computation.4 | async-start | bytes 393216 | tf_op jit(solution)/shard_map/all_to_all | solution.py:314
  110.7 10.8 %collective-permute-start.4 = (f32[296,512]{1,0:T(8,128)S(1)}, f32[296,512]{1,0:T(8,128)S(1)}, u32[]{:S(2)}, u32[]{:S(2)}) collective-permute-start(f32[296,512]{1,0:T(8,128)S(1)} %get-tuple-element.47), channel_id=1, source_target_pairs={{0,8},{8,0},{1,9},{9,1},{2,10},{10,2},{3,11},{11,3},{4,12},{12,4},... | collective-permute-start | bytes 1818632 | tf_op jit(solution)/shard_map/ppermute | solution.py:313

commit v9 on v8

--- a/solution.py
+++ b/solution.py
@@ -34,11 +34,10 @@
 
 
 def split_bf16(v):
-    hi = v.astype(bf16)
-    rest = v - hi.astype(f32)
-    mid = rest.astype(bf16)
-    low = (rest - mid.astype(f32)).astype(bf16)
-    return jnp.stack([hi, mid, low])
+    hi = lax.reduce_precision(v, 8, 7)
+    mid = lax.reduce_precision(v - hi, 8, 7)
+    low = lax.reduce_precision(v - hi - mid, 8, 7)
+    return jnp.stack([hi, mid, low]).astype(bf16)
 
 
 def call(body, outs, *args):
@@ -230,7 +229,7 @@
     top_sq = jnp.max(squares)
     e_sq = exponent(top_sq)
     scaled = squares * jnp.exp2(TOP - e_sq)
-    hi = scaled.astype(f16).astype(f32)
+    hi = lax.reduce_precision(scaled, 5, 10)
     lines = jnp.concatenate(
         [
             hi[None],

time: 123 us -> 123 us (level)
  no operation moved by 1% of the time
where the time goes in v9:
time: 123 us; the launch traced here: 122 us
  starting transfers between devices  47.4 us (39%)
  waiting for transfers between devices  41 us (33%)
  blocking collectives  12.3 us (10%)
  other arithmetic  9.52 us (8%)
  Pallas kernels  6.88 us (6%)
  between operations  3.13 us (3%)
  local copies, waits for them, and re-layouts  2.22 us (2%)
    all_to_all x1, waiting for transfers between devices, local(): lax.all_to_all(held, PLANE, 0, 0, tiled=True).reshape(wide, depth + LANES)  21.3 us
    all_to_all x1, starting transfers between devices, local(): lax.all_to_all(held, PLANE, 0, 0, tiled=True).reshape(wide, depth + LANES)  13.8 us
    all_to_all x1, blocking collectives, local(): grad = lax.all_to_all(grad, 'x', 0, 0, tiled=True).reshape(wide, both_lats)  12.3 us
    all_to_all x1, waiting for transfers between devices, local(): lax.all_to_all(sent.astype(f16).reshape(PEERS, rows, LANES), PLANE, 0, 0,...  8.83 us
    all_to_all x1, starting transfers between devices, local(): lax.all_to_all(sent.astype(f16).reshape(PEERS, rows, LANES), PLANE, 0, 0,...  6.43 us
    ppermute x1, waiting for transfers between devices, local(): term_partner = lax.ppermute(term_half, 'yh', SWAP)  6.07 us
    all_to_all x1, starting transfers between devices, local(): lax.all_to_all(term.astype(f16), 'x', 0, 0, tiled=True).astype(f32)  5.56 us
    ppermute x1, starting transfers between devices, local(): partner = lax.ppermute(half, 'yh', SWAP)  5.45 us
  transfers between devices with their start and end apart: 9, of which 6 were waited for; matrix products, arithmetic and copies ran while one was open for 8% of the time, Pallas kernels for 3%

profile of v9, /device:TPU:2, one launch (start us, length us, event | category | flops | bytes accessed | tf_op | source)
XLA Modules:
  0.0 122.4 jit_solution(11520637581756725767)
XLA Ops:
  0.6 2.0 %shard_map.94 = bf16[32,8,2688]{2,1,0:T(8,128)(2,1)} custom-call(bf16[8,2304]{1,0:T(8,128)(2,1)} %bitcast.40, bf16[8,2,288]{2,1,0:T(2,128)(2,1)} %inputs_far.1), custom_call_target="tpu_custom_call" | custom-call | tf_op jit(solution)/shard_map/pallas_call | solution.py:185
  2.6 0.0 copy-start.3
  2.7 13.8 %all-to-all-start = ((bf16[32,8,2688]{2,1,0:T(8,128)(2,1)}), bf16[32,8,2688]{2,1,0:T(8,128)(2,1)S(1)}, u32[]{:S(2)}, u32[]{:S(2)}) async-start(bf16[32,8,2688]{2,1,0:T(8,128)(2,1)} %shard_map.94), calls=%async_computation | async-start | bytes 2752512 | tf_op jit(solution)/shard_map/all_to_all | solution.py:197
  16.4 0.0 copy-start.1
  16.5 0.0 copy-start.4
  16.5 2.2 %fusion = f32[512]{0:T(512)S(1)} fusion(bf16[1,512,2304]{2,1,0:T(8,128)(2,1)} %param.11), kind=kLoop, calls=%fused_computation.1 | loop fusion | flops 3538432 | bytes 2361344 | tf_op jit(solution)/shard_map/cd,cd->c/dot_general | solution.py:204
  18.8 1.0 fusion.3
  19.8 0.3 concatenate.38
  20.1 1.9 %collective-permute-start = (bf16[464,512]{1,0:T(8,128)(2,1)S(1)}, bf16[464,512]{1,0:T(8,128)(2,1)S(1)}, u32[]{:S(2)}, u32[]{:S(2)}) collective-permute-start(bf16[464,512]{1,0:T(8,128)(2,1)S(1)} %concatenate.38), channel_id=1, source_target_pairs={{0,8},{8,0},{1,9},{9,1},{2,10},{10,2},{3,11},{11,3},{4,12},{12,4},... | collective-permute-start | bytes 1425416 | tf_op jit(solution)/shard_map/ppermute | solution.py:216
  22.1 1.8 %collective-permute-done = bf16[464,512]{1,0:T(8,128)(2,1)S(1)} collective-permute-done((bf16[464,512]{1,0:T(8,128)(2,1)S(1)}, bf16[464,512]{1,0:T(8,128)(2,1)S(1)}, u32[]{:S(2)}, u32[]{:S(2)}) %collective-permute-start) | collective-permute-done | bytes 475168 | tf_op jit(solution)/shard_map/ppermute | solution.py:216
  23.9 2.0 %collective-permute-start.1 = (bf16[512,2304]{1,0:T(8,128)(2,1)}, bf16[512,2304]{1,0:T(8,128)(2,1)}, u32[]{:S(2)}, u32[]{:S(2)}) collective-permute-start(bf16[512,2304]{1,0:T(8,128)(2,1)} %bitcast.35), channel_id=1, source_target_pairs={{0,8},{8,0},{1,9},{9,1},{2,10},{10,2},{3,11},{11,3},{4,12},{12,4},... | collective-permute-start | bytes 7077896 | tf_op jit(solution)/shard_map/ppermute | solution.py:218
  26.0 0.6 fusion.11
  27.3 0.1 pad.12.clone
  27.4 0.6 fusion.6
  29.5 0.1 pad.11.clone
  29.5 0.1 maximum_bitcast_fusion.base
  29.6 0.9 slice_convert_fusion
  30.5 0.1 fusion.2.enc_both
  30.7 0.1 maximum_maximum_fusion.lines
  30.7 21.3 %all-to-all-done = bf16[32,8,2688]{2,1,0:T(8,128)(2,1)S(1)} async-done(((bf16[32,8,2688]{2,1,0:T(8,128)(2,1)}), bf16[32,8,2688]{2,1,0:T(8,128)(2,1)S(1)}, u32[]{:S(2)}, u32[]{:S(2)}) %all-to-all-start) | async-done | bytes 1376288 | tf_op jit(solution)/shard_map/all_to_all | solution.py:197
  52.0 0.5 shard_map.95
  52.5 0.9 convert_element_type.63
  53.4 4.8 %all-to-all-start.2 = ((f16[4,72,1024]{2,1,0:T(8,128)(2,1)}), f16[4,72,1024]{2,1,0:T(8,128)(2,1)S(1)}, u32[]{:S(2)}, u32[]{:S(2)}) async-start(f16[4,72,1024]{2,1,0:T(8,128)(2,1)} %convert_element_type.63), calls=%async_computation.2 | async-start | bytes 1179648 | tf_op jit(solution)/shard_map/all_to_all | solution.py:265
  58.2 0.0 collective-permute-done.1.w_far
  58.2 1.7 %copy-done = bf16[1,512,2304]{2,1,0:T(8,128)(2,1)S(1)} copy-done((bf16[1,512,2304]{2,1,0:T(8,128)(2,1)S(1)}, bf16[1,512,2304]{2,1,0:T(8,128)(2,1)}, u32[]{:S(2)}) %copy-start) | copy-done | bytes 2359320
  59.9 2.5 %shard_map.96 = f32[4,64,1024]{2,1,0:T(8,128)S(1)} custom-call(bf16[256,2688]{1,0:T(8,128)(2,1)S(1)} %bitcast.34, bf16[512,2304]{1,0:T(8,128)(2,1)S(1)} %bitcast.36, bf16[512,2304]{1,0:T(8,128)(2,1)} %collective-permute-done.1.w_far, f32[8,128]{1,0:T(8,128)S(1)} %get-tuple-element.36.tops, f32[1,2]{1,0:T(1,128)S(1)} %maximum_bitcast_fusion.base), custom_call_target="tpu_custom_call" | custom-call | flops 1207959552 | bytes 6946816 | tf_op jit(solution)/shard_map/pallas_call | solution.py:266
  62.4 0.9 convert_element_type.61
  63.3 1.9 %all-to-all-done.2 = f16[4,72,1024]{2,1,0:T(8,128)(2,1)S(1)} async-done(((f16[4,72,1024]{2,1,0:T(8,128)(2,1)}), f16[4,72,1024]{2,1,0:T(8,128)(2,1)S(1)}, u32[]{:S(2)}, u32[]{:S(2)}) %all-to-all-start.2) | async-done | bytes 589856 | tf_op jit(solution)/shard_map/all_to_all | solution.py:265
  65.2 5.6 %all-to-all-start.1 = ((f16[4,64,1024]{2,1,0:T(8,128)(2,1)}), f16[4,64,1024]{2,1,0:T(8,128)(2,1)}, u32[]{:S(2)}, u32[]{:S(2)}) async-start(f16[4,64,1024]{2,1,0:T(8,128)(2,1)} %convert_element_type.61), calls=%async_computation.1 | async-start | bytes 1048576 | tf_op jit(solution)/shard_map/all_to_all | solution.py:286
  70.8 0.1 convert_element_type.64.back
  70.9 0.1 shard_map.97
  71.0 5.5 %collective-permute-start.3 = (f16[72,1024]{1,0:T(8,128)(2,1)S(1)}, f16[72,1024]{1,0:T(8,128)(2,1)S(1)}, u32[]{:S(2)}, u32[]{:S(2)}) collective-permute-start(f16[72,1024]{1,0:T(8,128)(2,1)S(1)} %convert_element_type.68), channel_id=1, source_target_pairs={{0,4},{4,0},{1,5},{5,1},{2,6},{6,2},{3,7},{7,3},{8,12},{12,8},{9,1... | collective-permute-start | bytes 442376 | tf_op jit(solution)/shard_map/ppermute | solution.py:292
  76.5 1.1 all-to-all-done.1
  77.5 1.1 convert_element_type.62.back
  78.6 0.1 shard_map.98
  78.7 5.5 %collective-permute-start.2 = (f16[64,1024]{1,0:T(8,128)(2,1)S(1)}, f16[64,1024]{1,0:T(8,128)(2,1)S(1)}, u32[]{:S(2)}, u32[]{:S(2)}) collective-permute-start(f16[64,1024]{1,0:T(8,128)(2,1)S(1)} %convert_element_type.65), channel_id=1, source_target_pairs={{0,4},{4,0},{1,5},{5,1},{2,6},{6,2},{3,7},{7,3},{8,12},{12,8},{9,1... | collective-permute-start | bytes 393224 | tf_op jit(solution)/shard_map/ppermute | solution.py:295
  84.3 0.0 collective-permute-done.3
  84.3 0.1 shard_map.99
  84.4 6.1 %collective-permute-done.2 = f16[64,1024]{1,0:T(8,128)(2,1)S(1)} collective-permute-done((f16[64,1024]{1,0:T(8,128)(2,1)S(1)}, f16[64,1024]{1,0:T(8,128)(2,1)S(1)}, u32[]{:S(2)}, u32[]{:S(2)}) %collective-permute-start.2) | collective-permute-done | bytes 131104 | tf_op jit(solution)/shard_map/ppermute | solution.py:295
  90.5 0.1 shard_map.100
  90.6 12.3 %all_to_all.25 = bf16[4,64,1024]{2,1,0:T(8,128)(2,1)S(1)} all-to-all(bf16[4,64,1024]{2,1,0:T(8,128)(2,1)S(1)} %shard_map.100), channel_id=1, replica_groups=mesh['yl'=4,'z'=8,'c'=2,'yh'=2,'x'=4] {'x'}, dimensions={0} | all-to-all | bytes 1048576 | tf_op jit(solution)/shard_map/all_to_all | solution.py:306
  102.9 0.7 shard_map.101
  103.5 0.7 convert_bitcast_fusion
  104.2 6.4 %all-to-all-start.4 = ((f16[32,8,384]{2,1,0:T(8,128)(2,1)}), f16[32,8,384]{2,1,0:T(8,128)(2,1)S(1)}, u32[]{:S(2)}, u32[]{:S(2)}) async-start(f16[32,8,384]{2,1,0:T(8,128)(2,1)} %convert_bitcast_fusion), calls=%async_computation.4 | async-start | bytes 393216 | tf_op jit(solution)/shard_map/all_to_all | solution.py:313
  110.7 1.9 %collective-permute-start.4 = (f32[296,512]{1,0:T(8,128)S(1)}, f32[296,512]{1,0:T(8,128)S(1)}, u32[]{:S(2)}, u32[]{:S(2)}) collective-permute-start(f32[296,512]{1,0:T(8,128)S(1)} %get-tuple-element.47), channel_id=1, source_target_pairs={{0,8},{8,0},{1,9},{9,1},{2,10},{10,2},{3,11},{11,3},{4,12},{12,4},... | collective-permute-start | bytes 1818632 | tf_op jit(solution)/shard_map/ppermute | solution.py:312
  112.6 8.8 %all-to-all-done.4 = f16[32,8,384]{2,1,0:T(8,128)(2,1)S(1)} async-done(((f16[32,8,384]{2,1,0:T(8,128)(2,1)}), f16[32,8,384]{2,1,0:T(8,128)(2,1)S(1)}, u32[]{:S(2)}, u32[]{:S(2)}) %all-to-all-start.4) | async-done | bytes 196640 | tf_op jit(solution)/shard_map/all_to_all | solution.py:313
  121.4 0.0 collective-permute-done.4.far
  121.5 1.0 shard_map.102
  (33 shorter events, 0.4 us)
Async XLA Ops:
  2.6 13.8 %copy-start.3 = (f32[512]{0:T(512)S(1)}, f32[512]{0:T(512)}, u32[]{:S(2)}) copy-start(f32[512]{0:T(512)} %param.9) | copy-start | bytes 6148
  2.7 49.4 %all-to-all-start = ((bf16[32,8,2688]{2,1,0:T(8,128)(2,1)}), bf16[32,8,2688]{2,1,0:T(8,128)(2,1)S(1)}, u32[]{:S(2)}, u32[]{:S(2)}) async-start(bf16[32,8,2688]{2,1,0:T(8,128)(2,1)} %shard_map.94), calls=%async_computation | async-start | bytes 2752512 | tf_op jit(solution)/shard_map/all_to_all | solution.py:197
  16.4 3.4 %copy-start.1 = (bf16[288,512]{1,0:T(8,128)(2,1)S(1)}, bf16[288,512]{1,0:T(8,128)(2,1)}, u32[]{:S(2)}) copy-start(bf16[288,512]{1,0:T(8,128)(2,1)} %param.8) | copy-start | bytes 884740
  16.5 9.5 %copy-start.4 = (s32[8]{0:T(128)S(1)}, s32[8]{0:T(128)}, u32[]{:S(2)}) copy-start(s32[8]{0:T(128)} %param.13) | copy-start | bytes 100
  20.1 3.7 %collective-permute-start = (bf16[464,512]{1,0:T(8,128)(2,1)S(1)}, bf16[464,512]{1,0:T(8,128)(2,1)S(1)}, u32[]{:S(2)}, u32[]{:S(2)}) collective-permute-start(bf16[464,512]{1,0:T(8,128)(2,1)S(1)} %concatenate.38), channel_id=1, source_target_pairs={{0,8},{8,0},{1,9},{9,1},{2,10},{10,2},{3,11},{11,3},{4,12},{12,4},... | collective-permute-start | bytes 1425416 | tf_op jit(solution)/shard_map/ppermute | solution.py:216
  23.9 5.7 %copy-start.2 = (bf16[464,512]{1,0:T(8,128)(2,1)}, bf16[464,512]{1,0:T(8,128)(2,1)S(1)}, u32[]{:S(2)}) copy-start(bf16[464,512]{1,0:T(8,128)(2,1)S(1)} %collective-permute-done) | copy-start | bytes 1425412
  23.9 34.4 %collective-permute-start.1 = (bf16[512,2304]{1,0:T(8,128)(2,1)}, bf16[512,2304]{1,0:T(8,128)(2,1)}, u32[]{:S(2)}, u32[]{:S(2)}) collective-permute-start(bf16[512,2304]{1,0:T(8,128)(2,1)} %bitcast.35), channel_id=1, source_target_pairs={{0,8},{8,0},{1,9},{9,1},{2,10},{10,2},{3,11},{11,3},{4,12},{12,4},... | collective-permute-start | bytes 7077896 | tf_op jit(solution)/shard_map/ppermute | solution.py:218
  53.4 11.8 %all-to-all-start.2 = ((f16[4,72,1024]{2,1,0:T(8,128)(2,1)}), f16[4,72,1024]{2,1,0:T(8,128)(2,1)S(1)}, u32[]{:S(2)}, u32[]{:S(2)}) async-start(f16[4,72,1024]{2,1,0:T(8,128)(2,1)} %convert_element_type.63), calls=%async_computation.2 | async-start | bytes 1179648 | tf_op jit(solution)/shard_map/all_to_all | solution.py:265
  58.2 1.7 %copy-start = (bf16[1,512,2304]{2,1,0:T(8,128)(2,1)S(1)}, bf16[1,512,2304]{2,1,0:T(8,128)(2,1)}, u32[]{:S(2)}) copy-start(bf16[1,512,2304]{2,1,0:T(8,128)(2,1)} %param.11) | copy-start | bytes 7077892
  65.2 12.3 %all-to-all-start.1 = ((f16[4,64,1024]{2,1,0:T(8,128)(2,1)}), f16[4,64,1024]{2,1,0:T(8,128)(2,1)}, u32[]{:S(2)}, u32[]{:S(2)}) async-start(f16[4,64,1024]{2,1,0:T(8,128)(2,1)} %convert_element_type.61), calls=%async_computation.1 | async-start | bytes 1048576 | tf_op jit(solution)/shard_map/all_to_all | solution.py:286
  71.0 13.3 %collective-permute-start.3 = (f16[72,1024]{1,0:T(8,128)(2,1)S(1)}, f16[72,1024]{1,0:T(8,128)(2,1)S(1)}, u32[]{:S(2)}, u32[]{:S(2)}) collective-permute-start(f16[72,1024]{1,0:T(8,128)(2,1)S(1)} %convert_element_type.68), channel_id=1, source_target_pairs={{0,4},{4,0},{1,5},{5,1},{2,6},{6,2},{3,7},{7,3},{8,12},{12,8},{9,1... | collective-permute-start | bytes 442376 | tf_op jit(solution)/shard_map/ppermute | solution.py:292
  78.7 11.7 %collective-permute-start.2 = (f16[64,1024]{1,0:T(8,128)(2,1)S(1)}, f16[64,1024]{1,0:T(8,128)(2,1)S(1)}, u32[]{:S(2)}, u32[]{:S(2)}) collective-permute-start(f16[64,1024]{1,0:T(8,128)(2,1)S(1)} %convert_element_type.65), channel_id=1, source_target_pairs={{0,4},{4,0},{1,5},{5,1},{2,6},{6,2},{3,7},{7,3},{8,12},{12,8},{9,1... | collective-permute-start | bytes 393224 | tf_op jit(solution)/shard_map/ppermute | solution.py:295
  104.2 17.2 %all-to-all-start.4 = ((f16[32,8,384]{2,1,0:T(8,128)(2,1)}), f16[32,8,384]{2,1,0:T(8,128)(2,1)S(1)}, u32[]{:S(2)}, u32[]{:S(2)}) async-start(f16[32,8,384]{2,1,0:T(8,128)(2,1)} %convert_bitcast_fusion), calls=%async_computation.4 | async-start | bytes 393216 | tf_op jit(solution)/shard_map/all_to_all | solution.py:313
  110.7 10.8 %collective-permute-start.4 = (f32[296,512]{1,0:T(8,128)S(1)}, f32[296,512]{1,0:T(8,128)S(1)}, u32[]{:S(2)}, u32[]{:S(2)}) collective-permute-start(f32[296,512]{1,0:T(8,128)S(1)} %get-tuple-element.47), channel_id=1, source_target_pairs={{0,8},{8,0},{1,9},{9,1},{2,10},{10,2},{3,11},{11,3},{4,12},{12,4},... | collective-permute-start | bytes 1818632 | tf_op jit(solution)/shard_map/ppermute | solution.py:312

commit v10 on v9

--- a/solution.py
+++ b/solution.py
@@ -118,13 +118,6 @@
     out[at + 4 :, :] = jnp.zeros((EXTRA - 4, out.shape[1]), f32)
 
 
-def terms_along_x(back, weights, out):
-    total = 0.0
-    for i in range(X):
-        total += back[i] * weights[i : i + 1, :]
-    out[...] = total
-
-
 def penalties(one, two, gates, bias, out, weights):
     at = gates.shape[0]
     pre, sumsq = 0.0, 0.0
@@ -283,14 +276,14 @@
             transcendentals=0,
         ),
     )(got, w_own, w_other, tops, base)
-    terms_in = lax.all_to_all(term.astype(f16), "x", 0, 0, tiled=True).astype(f32)
+    terms_in = lax.all_to_all(term.astype(f16), "x", 0, 0, tiled=True)
 
     half, weights = call(
         pre_along_x, [((chunk + EXTRA, both_lats), f32), ((EXTRA, both_lats), f32)], pre_in
     )
     half = lax.optimization_barrier(half.astype(f16))
     partner = lax.ppermute(half, "yh", SWAP)
-    (term_half,) = call(terms_along_x, [((chunk, both_lats), f32)], terms_in, weights)
+    term_half = jnp.sum(terms_in.astype(f32) * weights[:X, None, :], axis=0)
     term_half = lax.optimization_barrier(term_half.astype(f16))
     term_partner = lax.ppermute(term_half, "yh", SWAP)
     pull, weights = call(

time: 123 us -> 122 us (level)
  waiting for transfers between devices: 41 us -> 43 us
    ppermute x1, waiting for transfers between devices: 6.07 us -> 7.78 us  [local(): term_partner = lax.ppermute(term_half, 'yh', SWAP)]
  transfers between devices with their start and end apart: 9 -> 9, of which waited for: 6 -> 7; matrix products, arithmetic and copies ran while one was open for 8% -> 7% of each run, Pallas kernels for 3% -> 3%
where the time goes in v10:
time: 122 us
  starting transfers between devices  46.6 us (38%)
  waiting for transfers between devices  43 us (35%)
  blocking collectives  11.2 us (9%)
  other arithmetic  8.53 us (7%)
  Pallas kernels  6.83 us (6%)
  between operations  3.12 us (3%)
  local copies, waits for them, and re-layouts  2.23 us (2%)
    all_to_all x1, waiting for transfers between devices, local(): lax.all_to_all(held, PLANE, 0, 0, tiled=True).reshape(wide, depth + LANES)  21.3 us
    all_to_all x1, starting transfers between devices, local(): lax.all_to_all(held, PLANE, 0, 0, tiled=True).reshape(wide, depth + LANES)  13.8 us
    all_to_all x1, blocking collectives, local(): grad = lax.all_to_all(grad, 'x', 0, 0, tiled=True).reshape(wide, both_lats)  11.2 us
    all_to_all x1, waiting for transfers between devices, local(): lax.all_to_all(sent.astype(f16).reshape(PEERS, rows, LANES), PLANE, 0, 0,...  8.83 us
    ppermute x1, waiting for transfers between devices, local(): term_partner = lax.ppermute(term_half, 'yh', SWAP)  7.78 us
    all_to_all x1, starting transfers between devices, local(): lax.all_to_all(sent.astype(f16).reshape(PEERS, rows, LANES), PLANE, 0, 0,...  6.36 us
    ppermute x1, starting transfers between devices, local(): partner = lax.ppermute(half, 'yh', SWAP)  5.46 us
    ppermute x1, starting transfers between devices, local(): term_partner = lax.ppermute(term_half, 'yh', SWAP)  5.46 us
  transfers between devices with their start and end apart: 9, of which 7 were waited for; matrix products, arithmetic and copies ran while one was open for 7% of the time, Pallas kernels for 3%

profile of v10, /device:TPU:2, one launch (start us, length us, event | category | flops | bytes accessed | tf_op | source)
XLA Modules:
  0.0 121.5 jit_solution(2722942403135315146)
XLA Ops:
  0.6 2.0 %shard_map.94 = bf16[32,8,2688]{2,1,0:T(8,128)(2,1)} custom-call(bf16[8,2304]{1,0:T(8,128)(2,1)} %bitcast.40, bf16[8,2,288]{2,1,0:T(2,128)(2,1)} %inputs_far.1), custom_call_target="tpu_custom_call" | custom-call | tf_op jit(solution)/shard_map/pallas_call | solution.py:178
  2.7 0.0 copy-start.3
  2.7 13.8 %all-to-all-start = ((bf16[32,8,2688]{2,1,0:T(8,128)(2,1)}), bf16[32,8,2688]{2,1,0:T(8,128)(2,1)S(1)}, u32[]{:S(2)}, u32[]{:S(2)}) async-start(bf16[32,8,2688]{2,1,0:T(8,128)(2,1)} %shard_map.94), calls=%async_computation | async-start | bytes 2752512 | tf_op jit(solution)/shard_map/all_to_all | solution.py:190
  16.4 0.0 copy-done.3
  16.4 0.0 copy-start.1
  16.5 0.0 copy-start.4
  16.5 2.2 %fusion = f32[512]{0:T(512)S(1)} fusion(bf16[1,512,2304]{2,1,0:T(8,128)(2,1)} %param.11), kind=kLoop, calls=%fused_computation.1 | loop fusion | flops 3538432 | bytes 2361344 | tf_op jit(solution)/shard_map/cd,cd->c/dot_general | solution.py:197
  18.8 1.0 fusion.3
  19.9 0.3 concatenate.38
  20.2 1.9 %collective-permute-start = (bf16[464,512]{1,0:T(8,128)(2,1)S(1)}, bf16[464,512]{1,0:T(8,128)(2,1)S(1)}, u32[]{:S(2)}, u32[]{:S(2)}) collective-permute-start(bf16[464,512]{1,0:T(8,128)(2,1)S(1)} %concatenate.38), channel_id=1, source_target_pairs={{0,8},{8,0},{1,9},{9,1},{2,10},{10,2},{3,11},{11,3},{4,12},{12,4},... | collective-permute-start | bytes 1425416 | tf_op jit(solution)/shard_map/ppermute | solution.py:209
  22.1 1.8 %collective-permute-done = bf16[464,512]{1,0:T(8,128)(2,1)S(1)} collective-permute-done((bf16[464,512]{1,0:T(8,128)(2,1)S(1)}, bf16[464,512]{1,0:T(8,128)(2,1)S(1)}, u32[]{:S(2)}, u32[]{:S(2)}) %collective-permute-start) | collective-permute-done | bytes 475168 | tf_op jit(solution)/shard_map/ppermute | solution.py:209
  23.9 2.0 %collective-permute-start.1 = (bf16[512,2304]{1,0:T(8,128)(2,1)}, bf16[512,2304]{1,0:T(8,128)(2,1)}, u32[]{:S(2)}, u32[]{:S(2)}) collective-permute-start(bf16[512,2304]{1,0:T(8,128)(2,1)} %bitcast.35), channel_id=1, source_target_pairs={{0,8},{8,0},{1,9},{9,1},{2,10},{10,2},{3,11},{11,3},{4,12},{12,4},... | collective-permute-start | bytes 7077896 | tf_op jit(solution)/shard_map/ppermute | solution.py:211
  26.0 0.6 fusion.11
  27.3 0.1 pad.12.clone
  27.4 0.6 fusion.6
  29.5 0.1 pad.11.clone
  29.5 0.1 maximum_bitcast_fusion.base
  29.7 0.9 slice_convert_fusion
  30.5 0.1 fusion.2.enc_both
  30.7 0.1 maximum_maximum_fusion.lines
  30.7 21.3 %all-to-all-done = bf16[32,8,2688]{2,1,0:T(8,128)(2,1)S(1)} async-done(((bf16[32,8,2688]{2,1,0:T(8,128)(2,1)}), bf16[32,8,2688]{2,1,0:T(8,128)(2,1)S(1)}, u32[]{:S(2)}, u32[]{:S(2)}) %all-to-all-start) | async-done | bytes 1376288 | tf_op jit(solution)/shard_map/all_to_all | solution.py:190
  52.1 0.5 shard_map.95
  52.5 0.9 convert_element_type.63
  53.4 4.8 %all-to-all-start.2 = ((f16[4,72,1024]{2,1,0:T(8,128)(2,1)}), f16[4,72,1024]{2,1,0:T(8,128)(2,1)S(1)}, u32[]{:S(2)}, u32[]{:S(2)}) async-start(f16[4,72,1024]{2,1,0:T(8,128)(2,1)} %convert_element_type.63), calls=%async_computation.2 | async-start | bytes 1179648 | tf_op jit(solution)/shard_map/all_to_all | solution.py:258
  58.3 0.0 collective-permute-done.1.w_far
  58.3 1.7 %copy-done = bf16[1,512,2304]{2,1,0:T(8,128)(2,1)S(1)} copy-done((bf16[1,512,2304]{2,1,0:T(8,128)(2,1)S(1)}, bf16[1,512,2304]{2,1,0:T(8,128)(2,1)}, u32[]{:S(2)}) %copy-start) | copy-done | bytes 2359320
  59.9 2.5 %shard_map.96 = f32[4,64,1024]{2,1,0:T(8,128)S(1)} custom-call(bf16[256,2688]{1,0:T(8,128)(2,1)S(1)} %bitcast.34, bf16[512,2304]{1,0:T(8,128)(2,1)S(1)} %bitcast.36, bf16[512,2304]{1,0:T(8,128)(2,1)} %collective-permute-done.1.w_far, f32[8,128]{1,0:T(8,128)S(1)} %get-tuple-element.36.tops, f32[1,2]{1,0:T(1,128)S(1)} %maximum_bitcast_fusion.base), custom_call_target="tpu_custom_call" | custom-call | flops 1207959552 | bytes 6946816 | tf_op jit(solution)/shard_map/pallas_call | solution.py:259
  62.4 0.9 convert_element_type.61
  63.3 1.9 %all-to-all-done.2 = f16[4,72,1024]{2,1,0:T(8,128)(2,1)S(1)} async-done(((f16[4,72,1024]{2,1,0:T(8,128)(2,1)}), f16[4,72,1024]{2,1,0:T(8,128)(2,1)S(1)}, u32[]{:S(2)}, u32[]{:S(2)}) %all-to-all-start.2) | async-done | bytes 589856 | tf_op jit(solution)/shard_map/all_to_all | solution.py:258
  65.2 4.9 %all-to-all-start.1 = ((f16[4,64,1024]{2,1,0:T(8,128)(2,1)}), f16[4,64,1024]{2,1,0:T(8,128)(2,1)S(1)}, u32[]{:S(2)}, u32[]{:S(2)}) async-start(f16[4,64,1024]{2,1,0:T(8,128)(2,1)} %convert_element_type.61), calls=%async_computation.1 | async-start | bytes 1048576 | tf_op jit(solution)/shard_map/all_to_all | solution.py:279
  70.1 0.1 convert_element_type.64.back
  70.2 0.1 shard_map.97
  70.4 5.5 %collective-permute-start.3 = (f16[72,1024]{1,0:T(8,128)(2,1)S(1)}, f16[72,1024]{1,0:T(8,128)(2,1)S(1)}, u32[]{:S(2)}, u32[]{:S(2)}) collective-permute-start(f16[72,1024]{1,0:T(8,128)(2,1)S(1)} %convert_element_type.68), channel_id=1, source_target_pairs={{0,4},{4,0},{1,5},{5,1},{2,6},{6,2},{3,7},{7,3},{8,12},{12,8},{9,1... | collective-permute-start | bytes 442376 | tf_op jit(solution)/shard_map/ppermute | solution.py:285
  75.8 0.9 all-to-all-done.1
  76.8 0.1 multiply_reduce_fusion
  76.9 5.5 %collective-permute-start.2 = (f16[64,1024]{1,0:T(8,128)(2,1)S(1)}, f16[64,1024]{1,0:T(8,128)(2,1)S(1)}, u32[]{:S(2)}, u32[]{:S(2)}) collective-permute-start(f16[64,1024]{1,0:T(8,128)(2,1)S(1)} %convert_element_type.65), channel_id=1, source_target_pairs={{0,4},{4,0},{1,5},{5,1},{2,6},{6,2},{3,7},{7,3},{8,12},{12,8},{9,1... | collective-permute-start | bytes 393224 | tf_op jit(solution)/shard_map/ppermute | solution.py:288
  82.4 0.4 collective-permute-done.3
  82.8 0.1 shard_map.98
  82.9 7.8 %collective-permute-done.2 = f16[64,1024]{1,0:T(8,128)(2,1)S(1)} collective-permute-done((f16[64,1024]{1,0:T(8,128)(2,1)S(1)}, f16[64,1024]{1,0:T(8,128)(2,1)S(1)}, u32[]{:S(2)}, u32[]{:S(2)}) %collective-permute-start.2) | collective-permute-done | bytes 131104 | tf_op jit(solution)/shard_map/ppermute | solution.py:288
  90.8 0.1 shard_map.99
  90.8 11.2 %all_to_all.25 = bf16[4,64,1024]{2,1,0:T(8,128)(2,1)S(1)} all-to-all(bf16[4,64,1024]{2,1,0:T(8,128)(2,1)S(1)} %shard_map.99), channel_id=1, replica_groups=mesh['yl'=4,'z'=8,'c'=2,'yh'=2,'x'=4] {'x'}, dimensions={0} | all-to-all | bytes 1048576 | tf_op jit(solution)/shard_map/all_to_all | solution.py:299
  102.0 0.7 shard_map.100
  102.7 0.7 convert_bitcast_fusion
  103.4 6.4 %all-to-all-start.4 = ((f16[32,8,384]{2,1,0:T(8,128)(2,1)}), f16[32,8,384]{2,1,0:T(8,128)(2,1)S(1)}, u32[]{:S(2)}, u32[]{:S(2)}) async-start(f16[32,8,384]{2,1,0:T(8,128)(2,1)} %convert_bitcast_fusion), calls=%async_computation.4 | async-start | bytes 393216 | tf_op jit(solution)/shard_map/all_to_all | solution.py:306
  109.8 1.9 %collective-permute-start.4 = (f32[296,512]{1,0:T(8,128)S(1)}, f32[296,512]{1,0:T(8,128)S(1)}, u32[]{:S(2)}, u32[]{:S(2)}) collective-permute-start(f32[296,512]{1,0:T(8,128)S(1)} %get-tuple-element.47), channel_id=1, source_target_pairs={{0,8},{8,0},{1,9},{9,1},{2,10},{10,2},{3,11},{11,3},{4,12},{12,4},... | collective-permute-start | bytes 1818632 | tf_op jit(solution)/shard_map/ppermute | solution.py:305
  111.7 8.8 %all-to-all-done.4 = f16[32,8,384]{2,1,0:T(8,128)(2,1)S(1)} async-done(((f16[32,8,384]{2,1,0:T(8,128)(2,1)}), f16[32,8,384]{2,1,0:T(8,128)(2,1)S(1)}, u32[]{:S(2)}, u32[]{:S(2)}) %all-to-all-start.4) | async-done | bytes 196640 | tf_op jit(solution)/shard_map/all_to_all | solution.py:306
  120.5 0.0 collective-permute-done.4.far
  120.6 1.0 shard_map.101
  (33 shorter events, 0.4 us)
Async XLA Ops:
  2.7 13.8 %copy-start.3 = (f32[512]{0:T(512)S(1)}, f32[512]{0:T(512)}, u32[]{:S(2)}) copy-start(f32[512]{0:T(512)} %param.9) | copy-start | bytes 6148
  2.7 49.4 %all-to-all-start = ((bf16[32,8,2688]{2,1,0:T(8,128)(2,1)}), bf16[32,8,2688]{2,1,0:T(8,128)(2,1)S(1)}, u32[]{:S(2)}, u32[]{:S(2)}) async-start(bf16[32,8,2688]{2,1,0:T(8,128)(2,1)} %shard_map.94), calls=%async_computation | async-start | bytes 2752512 | tf_op jit(solution)/shard_map/all_to_all | solution.py:190
  16.4 3.4 %copy-start.1 = (bf16[288,512]{1,0:T(8,128)(2,1)S(1)}, bf16[288,512]{1,0:T(8,128)(2,1)}, u32[]{:S(2)}) copy-start(bf16[288,512]{1,0:T(8,128)(2,1)} %param.8) | copy-start | bytes 884740
  16.5 9.5 %copy-start.4 = (s32[8]{0:T(128)S(1)}, s32[8]{0:T(128)}, u32[]{:S(2)}) copy-start(s32[8]{0:T(128)} %param.13) | copy-start | bytes 100
  20.2 3.7 %collective-permute-start = (bf16[464,512]{1,0:T(8,128)(2,1)S(1)}, bf16[464,512]{1,0:T(8,128)(2,1)S(1)}, u32[]{:S(2)}, u32[]{:S(2)}) collective-permute-start(bf16[464,512]{1,0:T(8,128)(2,1)S(1)} %concatenate.38), channel_id=1, source_target_pairs={{0,8},{8,0},{1,9},{9,1},{2,10},{10,2},{3,11},{11,3},{4,12},{12,4},... | collective-permute-start | bytes 1425416 | tf_op jit(solution)/shard_map/ppermute | solution.py:209
  23.9 5.7 %copy-start.2 = (bf16[464,512]{1,0:T(8,128)(2,1)}, bf16[464,512]{1,0:T(8,128)(2,1)S(1)}, u32[]{:S(2)}) copy-start(bf16[464,512]{1,0:T(8,128)(2,1)S(1)} %collective-permute-done) | copy-start | bytes 1425412
  23.9 34.4 %collective-permute-start.1 = (bf16[512,2304]{1,0:T(8,128)(2,1)}, bf16[512,2304]{1,0:T(8,128)(2,1)}, u32[]{:S(2)}, u32[]{:S(2)}) collective-permute-start(bf16[512,2304]{1,0:T(8,128)(2,1)} %bitcast.35), channel_id=1, source_target_pairs={{0,8},{8,0},{1,9},{9,1},{2,10},{10,2},{3,11},{11,3},{4,12},{12,4},... | collective-permute-start | bytes 7077896 | tf_op jit(solution)/shard_map/ppermute | solution.py:211
  53.4 11.8 %all-to-all-start.2 = ((f16[4,72,1024]{2,1,0:T(8,128)(2,1)}), f16[4,72,1024]{2,1,0:T(8,128)(2,1)S(1)}, u32[]{:S(2)}, u32[]{:S(2)}) async-start(f16[4,72,1024]{2,1,0:T(8,128)(2,1)} %convert_element_type.63), calls=%async_computation.2 | async-start | bytes 1179648 | tf_op jit(solution)/shard_map/all_to_all | solution.py:258
  58.3 1.7 %copy-start = (bf16[1,512,2304]{2,1,0:T(8,128)(2,1)S(1)}, bf16[1,512,2304]{2,1,0:T(8,128)(2,1)}, u32[]{:S(2)}) copy-start(bf16[1,512,2304]{2,1,0:T(8,128)(2,1)} %param.11) | copy-start | bytes 7077892
  65.2 11.5 %all-to-all-start.1 = ((f16[4,64,1024]{2,1,0:T(8,128)(2,1)}), f16[4,64,1024]{2,1,0:T(8,128)(2,1)S(1)}, u32[]{:S(2)}, u32[]{:S(2)}) async-start(f16[4,64,1024]{2,1,0:T(8,128)(2,1)} %convert_element_type.61), calls=%async_computation.1 | async-start | bytes 1048576 | tf_op jit(solution)/shard_map/all_to_all | solution.py:279
  70.4 12.5 %collective-permute-start.3 = (f16[72,1024]{1,0:T(8,128)(2,1)S(1)}, f16[72,1024]{1,0:T(8,128)(2,1)S(1)}, u32[]{:S(2)}, u32[]{:S(2)}) collective-permute-start(f16[72,1024]{1,0:T(8,128)(2,1)S(1)} %convert_element_type.68), channel_id=1, source_target_pairs={{0,4},{4,0},{1,5},{5,1},{2,6},{6,2},{3,7},{7,3},{8,12},{12,8},{9,1... | collective-permute-start | bytes 442376 | tf_op jit(solution)/shard_map/ppermute | solution.py:285
  76.9 13.8 %collective-permute-start.2 = (f16[64,1024]{1,0:T(8,128)(2,1)S(1)}, f16[64,1024]{1,0:T(8,128)(2,1)S(1)}, u32[]{:S(2)}, u32[]{:S(2)}) collective-permute-start(f16[64,1024]{1,0:T(8,128)(2,1)S(1)} %convert_element_type.65), channel_id=1, source_target_pairs={{0,4},{4,0},{1,5},{5,1},{2,6},{6,2},{3,7},{7,3},{8,12},{12,8},{9,1... | collective-permute-start | bytes 393224 | tf_op jit(solution)/shard_map/ppermute | solution.py:288
  103.4 17.1 %all-to-all-start.4 = ((f16[32,8,384]{2,1,0:T(8,128)(2,1)}), f16[32,8,384]{2,1,0:T(8,128)(2,1)S(1)}, u32[]{:S(2)}, u32[]{:S(2)}) async-start(f16[32,8,384]{2,1,0:T(8,128)(2,1)} %convert_bitcast_fusion), calls=%async_computation.4 | async-start | bytes 393216 | tf_op jit(solution)/shard_map/all_to_all | solution.py:306
  109.8 10.8 %collective-permute-start.4 = (f32[296,512]{1,0:T(8,128)S(1)}, f32[296,512]{1,0:T(8,128)S(1)}, u32[]{:S(2)}, u32[]{:S(2)}) collective-permute-start(f32[296,512]{1,0:T(8,128)S(1)} %get-tuple-element.47), channel_id=1, source_target_pairs={{0,8},{8,0},{1,9},{9,1},{2,10},{10,2},{3,11},{11,3},{4,12},{12,4},... | collective-permute-start | bytes 1818632 | tf_op jit(solution)/shard_map/ppermute | solution.py:305

commit v11 on v10

--- a/solution.py
+++ b/solution.py
@@ -108,7 +108,6 @@
         pre += back[i, :at, :]
         squares += (line(i, 0) + line(i, 1)) * jnp.exp2(line(i, 2) - e_sq)
         weights[i : i + 1, :] = jnp.exp2(line(i, 3) - e_term)
-    weights[X:, :] = jnp.zeros((EXTRA - X, out.shape[1]), f32)
     out[:at, :] = pre
     hi = squares.astype(bf16).astype(f32)
     out[at : at + 1, :] = hi
@@ -279,11 +278,11 @@
     terms_in = lax.all_to_all(term.astype(f16), "x", 0, 0, tiled=True)
 
     half, weights = call(
-        pre_along_x, [((chunk + EXTRA, both_lats), f32), ((EXTRA, both_lats), f32)], pre_in
+        pre_along_x, [((chunk + EXTRA, both_lats), f32), ((X, both_lats), f32)], pre_in
     )
     half = lax.optimization_barrier(half.astype(f16))
     partner = lax.ppermute(half, "yh", SWAP)
-    term_half = jnp.sum(terms_in.astype(f32) * weights[:X, None, :], axis=0)
+    term_half = jnp.sum(terms_in.astype(f32) * weights[:, None, :], axis=0)
     term_half = lax.optimization_barrier(term_half.astype(f16))
     term_partner = lax.ppermute(term_half, "yh", SWAP)
     pull, weights = call(

time: 122 us -> 122 us (level)
  no operation moved by 1% of the time
where the time goes in v11:
time: 122 us
  starting transfers between devices  46.6 us (38%)
  waiting for transfers between devices  43 us (35%)
  blocking collectives  11.2 us (9%)
  other arithmetic  8.53 us (7%)
  Pallas kernels  6.82 us (6%)
  between operations  3.11 us (3%)
  local copies, waits for them, and re-layouts  2.22 us (2%)
    all_to_all x1, waiting for transfers between devices, local(): lax.all_to_all(held, PLANE, 0, 0, tiled=True).reshape(wide, depth + LANES)  21.3 us
    all_to_all x1, starting transfers between devices, local(): lax.all_to_all(held, PLANE, 0, 0, tiled=True).reshape(wide, depth + LANES)  13.8 us
    all_to_all x1, blocking collectives, local(): grad = lax.all_to_all(grad, 'x', 0, 0, tiled=True).reshape(wide, both_lats)  11.2 us
    all_to_all x1, waiting for transfers between devices, local(): lax.all_to_all(sent.astype(f16).reshape(PEERS, rows, LANES), PLANE, 0, 0,...  8.83 us
    ppermute x1, waiting for transfers between devices, local(): term_partner = lax.ppermute(term_half, 'yh', SWAP)  7.79 us
    all_to_all x1, starting transfers between devices, local(): lax.all_to_all(sent.astype(f16).reshape(PEERS, rows, LANES), PLANE, 0, 0,...  6.37 us
    ppermute x1, starting transfers between devices, local(): partner = lax.ppermute(half, 'yh', SWAP)  5.46 us
    ppermute x1, starting transfers between devices, local(): term_partner = lax.ppermute(term_half, 'yh', SWAP)  5.46 us
  transfers between devices with their start and end apart: 9, of which 7 were waited for; matrix products, arithmetic and copies ran while one was open for 7% of the time, Pallas kernels for 3%

profile of v11, /device:TPU:2, one launch (start us, length us, event | category | flops | bytes accessed | tf_op | source)
XLA Modules:
  0.0 121.5 jit_solution(7736141131410264897)
XLA Ops:
  0.6 2.0 %shard_map.94 = bf16[32,8,2688]{2,1,0:T(8,128)(2,1)} custom-call(bf16[8,2304]{1,0:T(8,128)(2,1)} %bitcast.40, bf16[8,2,288]{2,1,0:T(2,128)(2,1)} %inputs_far.1), custom_call_target="tpu_custom_call" | custom-call | tf_op jit(solution)/shard_map/pallas_call | solution.py:177
  2.7 0.0 copy-start.3
  2.7 13.8 %all-to-all-start = ((bf16[32,8,2688]{2,1,0:T(8,128)(2,1)}), bf16[32,8,2688]{2,1,0:T(8,128)(2,1)S(1)}, u32[]{:S(2)}, u32[]{:S(2)}) async-start(bf16[32,8,2688]{2,1,0:T(8,128)(2,1)} %shard_map.94), calls=%async_computation | async-start | bytes 2752512 | tf_op jit(solution)/shard_map/all_to_all | solution.py:189
  16.4 0.0 copy-done.3
  16.4 0.0 copy-start.1
  16.5 0.0 copy-start.4
  16.5 2.2 %fusion = f32[512]{0:T(512)S(1)} fusion(bf16[1,512,2304]{2,1,0:T(8,128)(2,1)} %param.11), kind=kLoop, calls=%fused_computation.1 | loop fusion | flops 3538432 | bytes 2361344 | tf_op jit(solution)/shard_map/cd,cd->c/dot_general | solution.py:196
  18.8 1.0 fusion.3
  19.9 0.3 concatenate.38
  20.2 1.9 %collective-permute-start = (bf16[464,512]{1,0:T(8,128)(2,1)S(1)}, bf16[464,512]{1,0:T(8,128)(2,1)S(1)}, u32[]{:S(2)}, u32[]{:S(2)}) collective-permute-start(bf16[464,512]{1,0:T(8,128)(2,1)S(1)} %concatenate.38), channel_id=1, source_target_pairs={{0,8},{8,0},{1,9},{9,1},{2,10},{10,2},{3,11},{11,3},{4,12},{12,4},... | collective-permute-start | bytes 1425416 | tf_op jit(solution)/shard_map/ppermute | solution.py:208
  22.1 1.8 %collective-permute-done = bf16[464,512]{1,0:T(8,128)(2,1)S(1)} collective-permute-done((bf16[464,512]{1,0:T(8,128)(2,1)S(1)}, bf16[464,512]{1,0:T(8,128)(2,1)S(1)}, u32[]{:S(2)}, u32[]{:S(2)}) %collective-permute-start) | collective-permute-done | bytes 475168 | tf_op jit(solution)/shard_map/ppermute | solution.py:208
  23.9 2.0 %collective-permute-start.1 = (bf16[512,2304]{1,0:T(8,128)(2,1)}, bf16[512,2304]{1,0:T(8,128)(2,1)}, u32[]{:S(2)}, u32[]{:S(2)}) collective-permute-start(bf16[512,2304]{1,0:T(8,128)(2,1)} %bitcast.35), channel_id=1, source_target_pairs={{0,8},{8,0},{1,9},{9,1},{2,10},{10,2},{3,11},{11,3},{4,12},{12,4},... | collective-permute-start | bytes 7077896 | tf_op jit(solution)/shard_map/ppermute | solution.py:210
  26.0 0.6 fusion.11
  27.3 0.1 pad.12.clone
  27.4 0.6 fusion.6
  29.5 0.1 pad.11.clone
  29.5 0.1 maximum_bitcast_fusion.base
  29.7 0.9 slice_convert_fusion
  30.5 0.1 fusion.2.enc_both
  30.7 0.1 maximum_maximum_fusion.lines
  30.7 21.3 %all-to-all-done = bf16[32,8,2688]{2,1,0:T(8,128)(2,1)S(1)} async-done(((bf16[32,8,2688]{2,1,0:T(8,128)(2,1)}), bf16[32,8,2688]{2,1,0:T(8,128)(2,1)S(1)}, u32[]{:S(2)}, u32[]{:S(2)}) %all-to-all-start) | async-done | bytes 1376288 | tf_op jit(solution)/shard_map/all_to_all | solution.py:189
  52.1 0.5 shard_map.95
  52.5 0.9 convert_element_type.63
  53.4 4.8 %all-to-all-start.2 = ((f16[4,72,1024]{2,1,0:T(8,128)(2,1)}), f16[4,72,1024]{2,1,0:T(8,128)(2,1)S(1)}, u32[]{:S(2)}, u32[]{:S(2)}) async-start(f16[4,72,1024]{2,1,0:T(8,128)(2,1)} %convert_element_type.63), calls=%async_computation.2 | async-start | bytes 1179648 | tf_op jit(solution)/shard_map/all_to_all | solution.py:257
  58.3 0.0 collective-permute-done.1.w_far
  58.3 1.7 %copy-done = bf16[1,512,2304]{2,1,0:T(8,128)(2,1)S(1)} copy-done((bf16[1,512,2304]{2,1,0:T(8,128)(2,1)S(1)}, bf16[1,512,2304]{2,1,0:T(8,128)(2,1)}, u32[]{:S(2)}) %copy-start) | copy-done | bytes 2359320
  59.9 2.5 %shard_map.96 = f32[4,64,1024]{2,1,0:T(8,128)S(1)} custom-call(bf16[256,2688]{1,0:T(8,128)(2,1)S(1)} %bitcast.34, bf16[512,2304]{1,0:T(8,128)(2,1)S(1)} %bitcast.36, bf16[512,2304]{1,0:T(8,128)(2,1)} %collective-permute-done.1.w_far, f32[8,128]{1,0:T(8,128)S(1)} %get-tuple-element.36.tops, f32[1,2]{1,0:T(1,128)S(1)} %maximum_bitcast_fusion.base), custom_call_target="tpu_custom_call" | custom-call | flops 1207959552 | bytes 6946816 | tf_op jit(solution)/shard_map/pallas_call | solution.py:258
  62.4 0.9 convert_element_type.61
  63.3 1.9 %all-to-all-done.2 = f16[4,72,1024]{2,1,0:T(8,128)(2,1)S(1)} async-done(((f16[4,72,1024]{2,1,0:T(8,128)(2,1)}), f16[4,72,1024]{2,1,0:T(8,128)(2,1)S(1)}, u32[]{:S(2)}, u32[]{:S(2)}) %all-to-all-start.2) | async-done | bytes 589856 | tf_op jit(solution)/shard_map/all_to_all | solution.py:257
  65.2 4.9 %all-to-all-start.1 = ((f16[4,64,1024]{2,1,0:T(8,128)(2,1)}), f16[4,64,1024]{2,1,0:T(8,128)(2,1)S(1)}, u32[]{:S(2)}, u32[]{:S(2)}) async-start(f16[4,64,1024]{2,1,0:T(8,128)(2,1)} %convert_element_type.61), calls=%async_computation.1 | async-start | bytes 1048576 | tf_op jit(solution)/shard_map/all_to_all | solution.py:278
  70.1 0.1 convert_element_type.64.back
  70.2 0.1 shard_map.97
  70.3 5.5 %collective-permute-start.3 = (f16[72,1024]{1,0:T(8,128)(2,1)S(1)}, f16[72,1024]{1,0:T(8,128)(2,1)S(1)}, u32[]{:S(2)}, u32[]{:S(2)}) collective-permute-start(f16[72,1024]{1,0:T(8,128)(2,1)S(1)} %convert_element_type.68), channel_id=1, source_target_pairs={{0,4},{4,0},{1,5},{5,1},{2,6},{6,2},{3,7},{7,3},{8,12},{12,8},{9,1... | collective-permute-start | bytes 442376 | tf_op jit(solution)/shard_map/ppermute | solution.py:284
  75.8 1.0 all-to-all-done.1
  76.8 0.1 multiply_reduce_fusion
  76.9 5.5 %collective-permute-start.2 = (f16[64,1024]{1,0:T(8,128)(2,1)S(1)}, f16[64,1024]{1,0:T(8,128)(2,1)S(1)}, u32[]{:S(2)}, u32[]{:S(2)}) collective-permute-start(f16[64,1024]{1,0:T(8,128)(2,1)S(1)} %convert_element_type.65), channel_id=1, source_target_pairs={{0,4},{4,0},{1,5},{5,1},{2,6},{6,2},{3,7},{7,3},{8,12},{12,8},{9,1... | collective-permute-start | bytes 393224 | tf_op jit(solution)/shard_map/ppermute | solution.py:287
  82.4 0.4 collective-permute-done.3
  82.8 0.1 shard_map.98
  82.9 7.8 %collective-permute-done.2 = f16[64,1024]{1,0:T(8,128)(2,1)S(1)} collective-permute-done((f16[64,1024]{1,0:T(8,128)(2,1)S(1)}, f16[64,1024]{1,0:T(8,128)(2,1)S(1)}, u32[]{:S(2)}, u32[]{:S(2)}) %collective-permute-start.2) | collective-permute-done | bytes 131104 | tf_op jit(solution)/shard_map/ppermute | solution.py:287
  90.8 0.1 shard_map.99
  90.8 11.2 %all_to_all.25 = bf16[4,64,1024]{2,1,0:T(8,128)(2,1)S(1)} all-to-all(bf16[4,64,1024]{2,1,0:T(8,128)(2,1)S(1)} %shard_map.99), channel_id=1, replica_groups=mesh['yl'=4,'z'=8,'c'=2,'yh'=2,'x'=4] {'x'}, dimensions={0} | all-to-all | bytes 1048576 | tf_op jit(solution)/shard_map/all_to_all | solution.py:298
  102.0 0.6 shard_map.100
  102.7 0.7 convert_bitcast_fusion
  103.4 6.4 %all-to-all-start.4 = ((f16[32,8,384]{2,1,0:T(8,128)(2,1)}), f16[32,8,384]{2,1,0:T(8,128)(2,1)S(1)}, u32[]{:S(2)}, u32[]{:S(2)}) async-start(f16[32,8,384]{2,1,0:T(8,128)(2,1)} %convert_bitcast_fusion), calls=%async_computation.4 | async-start | bytes 393216 | tf_op jit(solution)/shard_map/all_to_all | solution.py:305
  109.7 1.9 %collective-permute-start.4 = (f32[296,512]{1,0:T(8,128)S(1)}, f32[296,512]{1,0:T(8,128)S(1)}, u32[]{:S(2)}, u32[]{:S(2)}) collective-permute-start(f32[296,512]{1,0:T(8,128)S(1)} %get-tuple-element.47), channel_id=1, source_target_pairs={{0,8},{8,0},{1,9},{9,1},{2,10},{10,2},{3,11},{11,3},{4,12},{12,4},... | collective-permute-start | bytes 1818632 | tf_op jit(solution)/shard_map/ppermute | solution.py:304
  111.7 8.8 %all-to-all-done.4 = f16[32,8,384]{2,1,0:T(8,128)(2,1)S(1)} async-done(((f16[32,8,384]{2,1,0:T(8,128)(2,1)}), f16[32,8,384]{2,1,0:T(8,128)(2,1)S(1)}, u32[]{:S(2)}, u32[]{:S(2)}) %all-to-all-start.4) | async-done | bytes 196640 | tf_op jit(solution)/shard_map/all_to_all | solution.py:305
  120.5 0.0 collective-permute-done.4.far
  120.5 1.0 shard_map.101
  (32 shorter events, 0.4 us)
Async XLA Ops:
  2.7 13.8 %copy-start.3 = (f32[512]{0:T(512)S(1)}, f32[512]{0:T(512)}, u32[]{:S(2)}) copy-start(f32[512]{0:T(512)} %param.9) | copy-start | bytes 6148
  2.7 49.4 %all-to-all-start = ((bf16[32,8,2688]{2,1,0:T(8,128)(2,1)}), bf16[32,8,2688]{2,1,0:T(8,128)(2,1)S(1)}, u32[]{:S(2)}, u32[]{:S(2)}) async-start(bf16[32,8,2688]{2,1,0:T(8,128)(2,1)} %shard_map.94), calls=%async_computation | async-start | bytes 2752512 | tf_op jit(solution)/shard_map/all_to_all | solution.py:189
  16.4 3.4 %copy-start.1 = (bf16[288,512]{1,0:T(8,128)(2,1)S(1)}, bf16[288,512]{1,0:T(8,128)(2,1)}, u32[]{:S(2)}) copy-start(bf16[288,512]{1,0:T(8,128)(2,1)} %param.8) | copy-start | bytes 884740
  16.5 9.5 %copy-start.4 = (s32[8]{0:T(128)S(1)}, s32[8]{0:T(128)}, u32[]{:S(2)}) copy-start(s32[8]{0:T(128)} %param.13) | copy-start | bytes 100
  20.2 3.7 %collective-permute-start = (bf16[464,512]{1,0:T(8,128)(2,1)S(1)}, bf16[464,512]{1,0:T(8,128)(2,1)S(1)}, u32[]{:S(2)}, u32[]{:S(2)}) collective-permute-start(bf16[464,512]{1,0:T(8,128)(2,1)S(1)} %concatenate.38), channel_id=1, source_target_pairs={{0,8},{8,0},{1,9},{9,1},{2,10},{10,2},{3,11},{11,3},{4,12},{12,4},... | collective-permute-start | bytes 1425416 | tf_op jit(solution)/shard_map/ppermute | solution.py:208
  23.9 5.7 %copy-start.2 = (bf16[464,512]{1,0:T(8,128)(2,1)}, bf16[464,512]{1,0:T(8,128)(2,1)S(1)}, u32[]{:S(2)}) copy-start(bf16[464,512]{1,0:T(8,128)(2,1)S(1)} %collective-permute-done) | copy-start | bytes 1425412
  23.9 34.4 %collective-permute-start.1 = (bf16[512,2304]{1,0:T(8,128)(2,1)}, bf16[512,2304]{1,0:T(8,128)(2,1)}, u32[]{:S(2)}, u32[]{:S(2)}) collective-permute-start(bf16[512,2304]{1,0:T(8,128)(2,1)} %bitcast.35), channel_id=1, source_target_pairs={{0,8},{8,0},{1,9},{9,1},{2,10},{10,2},{3,11},{11,3},{4,12},{12,4},... | collective-permute-start | bytes 7077896 | tf_op jit(solution)/shard_map/ppermute | solution.py:210
  53.4 11.8 %all-to-all-start.2 = ((f16[4,72,1024]{2,1,0:T(8,128)(2,1)}), f16[4,72,1024]{2,1,0:T(8,128)(2,1)S(1)}, u32[]{:S(2)}, u32[]{:S(2)}) async-start(f16[4,72,1024]{2,1,0:T(8,128)(2,1)} %convert_element_type.63), calls=%async_computation.2 | async-start | bytes 1179648 | tf_op jit(solution)/shard_map/all_to_all | solution.py:257
  58.3 1.7 %copy-start = (bf16[1,512,2304]{2,1,0:T(8,128)(2,1)S(1)}, bf16[1,512,2304]{2,1,0:T(8,128)(2,1)}, u32[]{:S(2)}) copy-start(bf16[1,512,2304]{2,1,0:T(8,128)(2,1)} %param.11) | copy-start | bytes 7077892
  65.2 11.5 %all-to-all-start.1 = ((f16[4,64,1024]{2,1,0:T(8,128)(2,1)}), f16[4,64,1024]{2,1,0:T(8,128)(2,1)S(1)}, u32[]{:S(2)}, u32[]{:S(2)}) async-start(f16[4,64,1024]{2,1,0:T(8,128)(2,1)} %convert_element_type.61), calls=%async_computation.1 | async-start | bytes 1048576 | tf_op jit(solution)/shard_map/all_to_all | solution.py:278
  70.3 12.5 %collective-permute-start.3 = (f16[72,1024]{1,0:T(8,128)(2,1)S(1)}, f16[72,1024]{1,0:T(8,128)(2,1)S(1)}, u32[]{:S(2)}, u32[]{:S(2)}) collective-permute-start(f16[72,1024]{1,0:T(8,128)(2,1)S(1)} %convert_element_type.68), channel_id=1, source_target_pairs={{0,4},{4,0},{1,5},{5,1},{2,6},{6,2},{3,7},{7,3},{8,12},{12,8},{9,1... | collective-permute-start | bytes 442376 | tf_op jit(solution)/shard_map/ppermute | solution.py:284
  76.9 13.8 %collective-permute-start.2 = (f16[64,1024]{1,0:T(8,128)(2,1)S(1)}, f16[64,1024]{1,0:T(8,128)(2,1)S(1)}, u32[]{:S(2)}, u32[]{:S(2)}) collective-permute-start(f16[64,1024]{1,0:T(8,128)(2,1)S(1)} %convert_element_type.65), channel_id=1, source_target_pairs={{0,4},{4,0},{1,5},{5,1},{2,6},{6,2},{3,7},{7,3},{8,12},{12,8},{9,1... | collective-permute-start | bytes 393224 | tf_op jit(solution)/shard_map/ppermute | solution.py:287
  103.4 17.1 %all-to-all-start.4 = ((f16[32,8,384]{2,1,0:T(8,128)(2,1)}), f16[32,8,384]{2,1,0:T(8,128)(2,1)S(1)}, u32[]{:S(2)}, u32[]{:S(2)}) async-start(f16[32,8,384]{2,1,0:T(8,128)(2,1)} %convert_bitcast_fusion), calls=%async_computation.4 | async-start | bytes 393216 | tf_op jit(solution)/shard_map/all_to_all | solution.py:305
  109.7 10.8 %collective-permute-start.4 = (f32[296,512]{1,0:T(8,128)S(1)}, f32[296,512]{1,0:T(8,128)S(1)}, u32[]{:S(2)}, u32[]{:S(2)}) collective-permute-start(f32[296,512]{1,0:T(8,128)S(1)} %get-tuple-element.47), channel_id=1, source_target_pairs={{0,8},{8,0},{1,9},{9,1},{2,10},{10,2},{3,11},{11,3},{4,12},{12,4},... | collective-permute-start | bytes 1818632 | tf_op jit(solution)/shard_map/ppermute | solution.py:304
